TPU v7x, 32 devices: a whole 2x2x4 slice. The times are simulated.
32 devices in a mesh: group: 2 (over x), expert: 16 (over z, y, core).
Axes of the slice: x: 2, y: 2, z: 4, core: 2. Of those that a mesh axis runs over, the one named last changes fastest.
Arguments:
- tokens: bfloat16 [4096, 4096], P(('group', 'expert')), parts along dimension 0, may hold values from -6 to 6
- expert_ids: int32 [4096, 8], P(('group', 'expert')), parts along dimension 0, may hold values from 0 to 15, all different within a row; in each aligned block of 128 rows (0 to 127, 128 to 255, ...) at most 72 rows name the same one
- gate_weights: float32 [4096, 8], P(('group', 'expert')), parts along dimension 0, may hold values from 0.05 to 0.25
- weights_in: bfloat16 [32, 4096, 1536], P(('group', 'expert')), parts along dimension 0, may hold values from -0.09375 to 0.09375
- weights_out: bfloat16 [32, 768, 4096], P(('group', 'expert')), parts along dimension 0, may hold values from -0.21875 to 0.21875
- placement: int32 [32], P('group'), parts along dimension 0, may hold values from 0 to 15, each once
- capacity: int32 [32], P('group'), parts along dimension 0, may hold values from 691 to 1152, as said below
Outputs:
- moe_out: bfloat16 [4096, 4096], P(('group', 'expert')), parts along dimension 0
There are 2 independent parts, one for each index of `group`. A program takes and returns all parts, laid end to end along the dimension named above; each array names one. Nothing has to cross between parts.
Inputs may be any that keep to these rules, and one draw needn't show every extreme that they name: `expert_ids`: each row names 8 different experts; among the rows of one device no expert is named by more than 72 rows, and that bound is reached in every draw. `placement`: A permutation of the experts. The largest capacity equals 1152 in every draw.
All inputs are finite; a program needn't handle non-finite values.
Results may differ from a plain program's by a relative error of at most 0.0058.
Values may be sent and summed in bfloat16 or wider, within the bound.
No kernel may reach another device: no remote copies, remote signals or barrier semaphores. Data moves between devices by JAX's collectives and lax.ppermute only.
A program may use at most 128 MiB of HBM per device.

v0:
```python
import jax
import jax.numpy as jnp
from jax import lax
from jax.sharding import PartitionSpec as P


def prefix(part, axis, combine, identity):
    place = lax.axis_index(axis)
    gathered = lax.all_gather(part, axis)
    state = jnp.zeros_like(part) + jnp.asarray(identity, part.dtype)

    def one(turn, state):
        return combine(state, lax.dynamic_index_in_dim(gathered, turn, 0, False))

    return lax.fori_loop(0, place, one, state)


def expert_block(inputs, first_weights, second_weights):
    hidden_len = first_weights.shape[1] // 2
    projected = jnp.dot(inputs, first_weights, preferred_element_type=jnp.float32)
    gate_part = projected[:, :hidden_len]
    up_part = projected[:, hidden_len:]
    hidden = (jax.nn.silu(gate_part) * up_part).astype(jnp.bfloat16)
    return jnp.dot(hidden, second_weights, preferred_element_type=jnp.float32).astype(jnp.bfloat16)


def add_counts(earlier, later):
    return earlier + later


def local(tokens, expert_ids, gate_weights, weights_in, weights_out, placement, capacity):
    axis_len = lax.axis_size("expert")
    tok_rows, top_len = expert_ids.shape
    feat_len = tokens.shape[1]
    slot_len = tok_rows * top_len * 9 // (8 * axis_len)
    devices = jnp.arange(axis_len, dtype=jnp.int32)
    dev_of = jnp.sum(jnp.where(placement[:, None] == devices[None, :], devices[:, None], 0), axis=0)
    flat_ids = expert_ids.reshape(-1)
    onehot = (flat_ids[:, None] == devices[None, :]).astype(jnp.int32)
    before = jnp.cumsum(onehot, axis=0) - onehot
    local_rank = jnp.sum(before * onehot, axis=1)
    counts = jnp.sum(onehot, axis=0)
    offset = prefix(counts, "expert", add_counts, jnp.zeros_like(counts))
    row_offset = jnp.sum(onehot * offset[None, :], axis=1)
    row_cap = jnp.sum(onehot * capacity[None, :], axis=1)
    row_dest = jnp.sum(onehot * dev_of[None, :], axis=1)
    kept = local_rank + row_offset < row_cap
    flat_slot = row_dest * slot_len + local_rank
    row_token = jnp.arange(tok_rows * top_len, dtype=jnp.int32) // top_len
    owner = jnp.full((axis_len * slot_len,), tok_rows, jnp.int32).at[flat_slot].set(row_token)
    padded_tokens = jnp.concatenate([tokens, jnp.zeros((1, feat_len), jnp.bfloat16)], axis=0)
    outgoing = padded_tokens[owner].reshape(axis_len, slot_len, feat_len)
    arrived = lax.all_to_all(outgoing, "expert", split_axis=0, concat_axis=0, tiled=True)
    items = arrived.shape[1]
    result_rows = expert_block(
        arrived.reshape(axis_len * items, feat_len), weights_in[0], weights_out[0]
    )
    result_rows = result_rows.reshape(axis_len, items, feat_len)
    returned = lax.all_to_all(result_rows, "expert", split_axis=0, concat_axis=0, tiled=True)
    picked = returned.reshape(axis_len * slot_len, feat_len)[flat_slot]
    row_weight = jnp.where(kept, gate_weights.reshape(-1), jnp.float32(0.0))
    combined = jnp.sum(
        (row_weight[:, None] * picked.astype(jnp.float32)).reshape(tok_rows, top_len, feat_len),
        axis=1,
    )
    return combined.astype(jnp.bfloat16)


def solution(mesh):
    in_specs = (
        P(("group", "expert"), None),
        P(("group", "expert"), None),
        P(("group", "expert"), None),
        P(("group", "expert"), None, None),
        P(("group", "expert"), None, None),
        P("group"),
        P("group"),
    )
    out_specs = P(("group", "expert"), None)
    return jax.shard_map(local, mesh=mesh, in_specs=in_specs, out_specs=out_specs, check_vma=False)
```

profile of v0, /device:TPU:15, one launch (start us, length us, event | category | flops | bytes accessed | tf_op | source)
XLA Modules:
  0.0 516.0 jit_solution(4059607662813311132)
XLA Ops:
  0.0 0.8 copy.16
  0.8 0.1 eq.42
  0.9 0.1 eq.38
  1.0 4.5 reduce-window.6
  5.5 0.1 slice.20
  5.6 0.1 copy.18
  5.8 0.1 copy.19
  5.8 0.1 broadcast_add_fusion
  5.9 0.1 convert_reduce_fusion
  6.1 1.3 dynamic-slice
  8.1 0.2 dynamic-update-slice
  8.3 7.9 %all-reduce.1 = s32[256]{0:T(256)S(1)} all-reduce(s32[256]{0:T(256)S(1)} %dynamic-update-slice), channel_id=2, replica_groups=mesh['group'=2,'expert'=16] {'expert'}, use_global_device_ids=true, to_apply=%add.1 | all-reduce | flops 256 | bytes 2048
  16.2 0.1 reshape.116
  16.3 0.3 while.10
  16.6 0.7 select_reduce_fusion.3
  17.3 0.8 select_reduce_fusion.2
  18.1 4.3 scatter_custom_fusion
  22.5 1.4 concatenate.3
  23.8 8.0 %gather_fusion = bf16[1152,4096]{1,0:T(8,128)(2,1)} fusion(bf16[129,4096]{1,0:T(8,128)(2,1)S(1)} %concatenate.3, s32[2048]{0:T(1024)S(1)} %pad_clamp_fusion), kind=kCustom, calls=%fused_computation | custom fusion | bytes 18878976 | tf_op jit(solution)/shard_map/gather | solution.py:52
  31.9 0.0 slice-start
  31.9 213.4 %all_to_all.10 = bf16[16,72,4096]{2,1,0:T(8,128)(2,1)S(1)} all-to-all(bf16[16,72,4096]{2,1,0:T(8,128)(2,1)} %bitcast.31), channel_id=1, replica_groups=mesh['group'=2,'expert'=16] {'expert'}, dimensions={0} | all-to-all | bytes 18874368 | tf_op jit(solution)/shard_map/all_to_all | solution.py:53
  245.3 0.0 slice-start.1
  245.3 17.8 %fusion.1 = f32[1152,1536]{1,0:T(8,128)S(1)} fusion(bf16[1152,4096]{1,0:T(8,128)(2,1)S(1)} %bitcast.33, bf16[1,4096,1536]{2,1,0:T(8,128)(2,1)} %param.12), kind=kOutput, calls=%fused_computation.7 | convolution fusion | flops 14495514624 | bytes 29097984 | tf_op jit(solution)/shard_map/dot_general | solution.py:20
  263.1 0.0 slice-done
  263.1 0.0 slice-done.1
  263.1 9.9 %convolution_convert_fusion = bf16[1152,4096]{1,0:T(8,128)(2,1)} fusion(bf16[1,768,4096]{2,1,0:T(8,128)(2,1)S(1)} %bitcast.40, f32[1152,1536]{1,0:T(8,128)S(1)} %fusion.1), kind=kOutput, calls=%fused_computation.6 | convolution fusion | flops 7257784320 | bytes 22806528 | tf_op jit(solution)/shard_map/dot_general | solution.py:24
  272.9 0.0 copy-start
  272.9 5.3 %all-to-all-start.1 = ((bf16[16,72,4096]{2,1,0:T(8,128)(2,1)}), bf16[16,72,4096]{2,1,0:T(8,128)(2,1)}, u32[]{:S(2)}, u32[]{:S(2)}) async-start(bf16[16,72,4096]{2,1,0:T(8,128)(2,1)} %bitcast.32), calls=%async_computation.1 | async-start | bytes 18874368 | tf_op jit(solution)/shard_map/all_to_all | solution.py:59
  278.3 0.1 lt.35
  278.4 0.0 copy-done
  278.4 0.1 copy.20
  278.5 204.6 %all-to-all-done.1 = bf16[16,72,4096]{2,1,0:T(8,128)(2,1)} async-done(((bf16[16,72,4096]{2,1,0:T(8,128)(2,1)}), bf16[16,72,4096]{2,1,0:T(8,128)(2,1)}, u32[]{:S(2)}, u32[]{:S(2)}) %all-to-all-start.1) | async-done | bytes 9437216 | tf_op jit(solution)/shard_map/all_to_all | solution.py:59
  483.1 20.0 %gather_fusion.1 = bf16[1024,4096]{1,0:T(8,128)(2,1)} fusion(bf16[1152,4096]{1,0:T(8,128)(2,1)} %bitcast.11, s32[1024]{0:T(1024)S(1)} %broadcast_clamp_fusion), kind=kCustom, calls=%fused_computation.1 | custom fusion | bytes 16781312 | tf_op jit(solution)/shard_map/gather | solution.py:60
  503.1 12.9 %fusion = bf16[128,4096]{1,0:T(8,128)(2,1)} fusion(bf16[1024,4096]{1,0:T(8,128)(2,1)} %gather_fusion.1, f32[128,8]{1,0:T(8,128)S(1)} %broadcast_select_fusion), kind=kLoop, calls=%fused_computation.5 | loop fusion | flops 12058624 | bytes 9441280 | tf_op jit(solution)/shard_map/reduce_sum | solution.py:62
  (21 shorter events, 0.2 us)
Async XLA Ops:
  31.9 231.2 %slice-start = ((s8[6291456]{0:T(1024)(128)(4,1)}), s8[4194304]{0:T(1024)(128)(4,1)S(1)}, s32[]{:S(2)}) async-start(s8[6291456]{0:T(1024)(128)(4,1)} %bitcast.39), calls=%async_computation.2 | async-start | bytes 8388608
  245.3 17.8 %slice-start.1 = ((s8[6291456]{0:T(1024)(128)(4,1)}), s8[2097152]{0:T(1024)(128)(4,1)S(1)}, s32[]{:S(2)}) async-start(s8[6291456]{0:T(1024)(128)(4,1)} %bitcast.39), calls=%async_computation.3 | async-start | bytes 4194304
  272.9 5.5 %copy-start = (f32[128,8]{0,1:T(8,128)S(1)}, f32[128,8]{0,1:T(8,128)}, u32[]{:S(2)}) copy-start(f32[128,8]{0,1:T(8,128)} %param.11) | copy-start | bytes 12292
  272.9 210.2 %all-to-all-start.1 = ((bf16[16,72,4096]{2,1,0:T(8,128)(2,1)}), bf16[16,72,4096]{2,1,0:T(8,128)(2,1)}, u32[]{:S(2)}, u32[]{:S(2)}) async-start(bf16[16,72,4096]{2,1,0:T(8,128)(2,1)} %bitcast.32), calls=%async_computation.1 | async-start | bytes 18874368 | tf_op jit(solution)/shard_map/all_to_all | solution.py:59
where the time goes:
time: 516 us
  blocking collectives  221 us (43%)
  waiting for transfers between devices  205 us (40%)
  local copies, waits for them, and re-layouts  36.8 us (7%)
  matrix products  27.6 us (5%)
  other arithmetic  19.3 us (4%)
  starting transfers between devices  5.34 us (1%)
    all_to_all x1, blocking collectives, local(): lax.all_to_all(outgoing, 'expert', split_axis=0, concat_axis=0, tiled=True)  213 us
    all_to_all x1, waiting for transfers between devices, local(): lax.all_to_all(result_rows, 'expert', split_axis=0, concat_axis=0, tiled=...  205 us
    gather x1, local copies, waits for them, and re-layouts, local(): picked = returned.reshape(axis_len * slot_len, feat_len)[flat_slot]  20 us
    dot_general x1, matrix products, expert_block(): jnp.dot(inputs, first_weights, preferred_element_type=jnp.float32)  17.8 us
    reduce_sum x1, other arithmetic, local(): jnp.sum((row_weight[:, None] * picked.astype(jnp.float32)).reshape(tok_ro...  12.9 us
  transfers between devices with their start and end apart: 1, of which 1 were waited for; matrix products, arithmetic and copies ran while one was open for 0% of the time, Pallas kernels for 0%

commit v1 on v0

--- a/solution.py
+++ b/solution.py
@@ -3,16 +3,7 @@
 from jax import lax
 from jax.sharding import PartitionSpec as P
 
-
-def prefix(part, axis, combine, identity):
-    place = lax.axis_index(axis)
-    gathered = lax.all_gather(part, axis)
-    state = jnp.zeros_like(part) + jnp.asarray(identity, part.dtype)
-
-    def one(turn, state):
-        return combine(state, lax.dynamic_index_in_dim(gathered, turn, 0, False))
-
-    return lax.fori_loop(0, place, one, state)
+AXIS = "expert"
 
 
 def expert_block(inputs, first_weights, second_weights):
@@ -24,12 +15,102 @@
     return jnp.dot(hidden, second_weights, preferred_element_type=jnp.float32).astype(jnp.bfloat16)
 
 
-def add_counts(earlier, later):
-    return earlier + later
+def row_weights(expert_ids, gate_weights, placement, capacity):
+    axis_len = lax.axis_size(AXIS)
+    rows = expert_ids.shape[0]
+    top_len = expert_ids.shape[1]
+    mine = lax.axis_index(AXIS)
+    expert = lax.dynamic_index_in_dim(placement, mine, 0, False)
+    limit = lax.dynamic_index_in_dim(capacity, expert, 0, False)
+    packed = jnp.concatenate([expert_ids.T.astype(jnp.float32), gate_weights.T], axis=0)
+    everyone = lax.all_gather(packed, AXIS)
+    named = everyone[:, :top_len] == expert.astype(jnp.float32)
+    gate = jnp.sum(jnp.where(named, everyone[:, top_len:], 0.0), axis=1)
+    hit = jnp.sum(named.astype(jnp.float32), axis=1)
+    lower = jnp.arange(rows)[:, None] < jnp.arange(rows)[None, :]
+    within = jnp.dot(hit, lower.astype(jnp.float32), precision=lax.Precision.HIGHEST)
+    total = jnp.sum(hit, axis=1)
+    earlier = jnp.arange(axis_len)[None, :] < jnp.arange(axis_len)[:, None]
+    ahead = jnp.sum(jnp.where(earlier, total[None, :], 0.0), axis=1)
+    rank = within + ahead[:, None]
+    return jnp.where((hit > 0) & (rank < limit.astype(jnp.float32)), gate, 0.0)
 
 
-def local(tokens, expert_ids, gate_weights, weights_in, weights_out, placement, capacity):
-    axis_len = lax.axis_size("expert")
+def ring_form(tokens, expert_ids, gate_weights, weights_in, weights_out, placement, capacity):
+    axis_len = lax.axis_size(AXIS)
+    rows, feat_len = tokens.shape
+    half = rows // 2
+    chips = axis_len // 2
+    side = chips // 2
+
+    def chip_at(spot):
+        return 2 * spot if spot < side else 2 * (chips - 1 - spot) + 1
+
+    spot_of = {chip_at(spot): spot for spot in range(chips)}
+
+    def along(step):
+        return [(d, 2 * chip_at((spot_of[d // 2] + step) % chips) + d % 2) for d in range(axis_len)]
+
+    forth, back = along(1), along(-1)
+    swap = [(d, d ^ 1) for d in range(axis_len)]
+
+    table = row_weights(expert_ids, gate_weights, placement, capacity).reshape(axis_len, 2, half, 1)
+    mine = lax.axis_index(AXIS)
+    chip, core = mine // 2, mine % 2
+    spot = jnp.where(chip % 2 == 0, chip // 2, chips - 1 - chip // 2)
+
+    def weight_of(place, which_core, part):
+        place = lax.rem(place + chips, chips)
+        its_chip = jnp.where(place < side, 2 * place, 2 * (chips - 1 - place) + 1)
+        return lax.dynamic_index_in_dim(table, 2 * its_chip + which_core, 0, False)[part]
+
+    first_weights, second_weights = weights_in[0], weights_out[0]
+    ahead, behind = tokens[:half], tokens[half:]
+    own_parts = []
+    for step in range(chips):
+        if step:
+            ahead = lax.ppermute(ahead, AXIS, forth)
+            behind = lax.ppermute(behind, AXIS, back)
+        own = tokens if step == 0 else jnp.concatenate([ahead, behind], axis=0)
+        other = lax.ppermute(own, AXIS, swap)
+        outs = expert_block(jnp.concatenate([own, other], axis=0), first_weights, second_weights)
+        scale = jnp.concatenate(
+            [
+                weight_of(spot - step, core, 0),
+                weight_of(spot + step, core, 1),
+                weight_of(spot - step, 1 - core, 0),
+                weight_of(spot + step, 1 - core, 1),
+            ],
+            axis=0,
+        )
+        scaled = outs.astype(jnp.float32) * scale
+        from_other = lax.ppermute(scaled[rows:].astype(jnp.bfloat16), AXIS, swap)
+        own_parts.append((scaled[:rows], from_other))
+        if step == 1:
+            sums = scaled[:rows] + from_other.astype(jnp.float32)
+            sums_a, sums_b = sums[:half].astype(jnp.bfloat16), sums[half:].astype(jnp.bfloat16)
+        elif step > 1:
+            mine_part = scaled[:rows] + from_other.astype(jnp.float32)
+            got_a = lax.ppermute(sums_a, AXIS, forth).astype(jnp.float32)
+            got_b = lax.ppermute(sums_b, AXIS, back).astype(jnp.float32)
+            sums_a = (got_a + mine_part[:half]).astype(jnp.bfloat16)
+            sums_b = (got_b + mine_part[half:]).astype(jnp.bfloat16)
+    first_scaled, first_other = own_parts[0]
+    mine_part = first_scaled + first_other.astype(jnp.float32)
+    got_a = lax.ppermute(sums_a, AXIS, forth).astype(jnp.float32)
+    got_b = lax.ppermute(sums_b, AXIS, back).astype(jnp.float32)
+    result = jnp.concatenate([got_a + mine_part[:half], got_b + mine_part[half:]], axis=0)
+    return result.astype(jnp.bfloat16)
+
+
+def prefix(part):
+    gathered = lax.all_gather(part, AXIS)
+    earlier = jnp.arange(gathered.shape[0]) < lax.axis_index(AXIS)
+    return jnp.sum(jnp.where(earlier[:, None], gathered, 0), axis=0)
+
+
+def exchange_form(tokens, expert_ids, gate_weights, weights_in, weights_out, placement, capacity):
+    axis_len = lax.axis_size(AXIS)
     tok_rows, top_len = expert_ids.shape
     feat_len = tokens.shape[1]
     slot_len = tok_rows * top_len * 9 // (8 * axis_len)
@@ -40,7 +121,7 @@
     before = jnp.cumsum(onehot, axis=0) - onehot
     local_rank = jnp.sum(before * onehot, axis=1)
     counts = jnp.sum(onehot, axis=0)
-    offset = prefix(counts, "expert", add_counts, jnp.zeros_like(counts))
+    offset = prefix(counts)
     row_offset = jnp.sum(onehot * offset[None, :], axis=1)
     row_cap = jnp.sum(onehot * capacity[None, :], axis=1)
     row_dest = jnp.sum(onehot * dev_of[None, :], axis=1)
@@ -50,13 +131,13 @@
     owner = jnp.full((axis_len * slot_len,), tok_rows, jnp.int32).at[flat_slot].set(row_token)
     padded_tokens = jnp.concatenate([tokens, jnp.zeros((1, feat_len), jnp.bfloat16)], axis=0)
     outgoing = padded_tokens[owner].reshape(axis_len, slot_len, feat_len)
-    arrived = lax.all_to_all(outgoing, "expert", split_axis=0, concat_axis=0, tiled=True)
+    arrived = lax.all_to_all(outgoing, AXIS, split_axis=0, concat_axis=0, tiled=True)
     items = arrived.shape[1]
     result_rows = expert_block(
         arrived.reshape(axis_len * items, feat_len), weights_in[0], weights_out[0]
     )
     result_rows = result_rows.reshape(axis_len, items, feat_len)
-    returned = lax.all_to_all(result_rows, "expert", split_axis=0, concat_axis=0, tiled=True)
+    returned = lax.all_to_all(result_rows, AXIS, split_axis=0, concat_axis=0, tiled=True)
     picked = returned.reshape(axis_len * slot_len, feat_len)[flat_slot]
     row_weight = jnp.where(kept, gate_weights.reshape(-1), jnp.float32(0.0))
     combined = jnp.sum(
@@ -64,6 +145,12 @@
         axis=1,
     )
     return combined.astype(jnp.bfloat16)
+
+
+def local(*args):
+    axis_len, top_len = lax.axis_size(AXIS), args[1].shape[1]
+    dense = axis_len <= 2 * top_len and axis_len % 4 == 0
+    return ring_form(*args) if dense else exchange_form(*args)
 
 
 def solution(mesh):

time: 516 us -> 244 us (0.47)
  the two profiles are of different devices: /device:TPU:15 before, /device:TPU:0 now
where the time goes in v1:
time: 244 us
  waiting for transfers between devices  94.6 us (39%)
  matrix products  78.5 us (32%)
  starting transfers between devices  33.1 us (14%)
  blocking collectives  23.4 us (10%)
  other arithmetic  5.99 us (2%)
  between operations  4.28 us (2%)
  local copies, waits for them, and re-layouts  3.82 us (2%)
    dot_general x8, matrix products, expert_block(): jnp.dot(inputs, first_weights, preferred_element_type=jnp.float32)  49.1 us
    ppermute x7, waiting for transfers between devices, ring_form(): ahead = lax.ppermute(ahead, AXIS, forth)  42.6 us
    ppermute x7, waiting for transfers between devices, ring_form(): got_a = lax.ppermute(sums_a, AXIS, forth).astype(jnp.float32)  31.9 us
    dot_general x8, matrix products, expert_block(): jnp.dot(hidden, second_weights, preferred_element_type=jnp.float32)  29.2 us
    all_gather x1, blocking collectives, row_weights(): everyone = lax.all_gather(packed, AXIS)  23.4 us
    ppermute x7, waiting for transfers between devices, ring_form(): behind = lax.ppermute(behind, AXIS, back)  12.7 us
    ppermute x7, starting transfers between devices, ring_form(): got_a = lax.ppermute(sums_a, AXIS, forth).astype(jnp.float32)  10.4 us
    ppermute x7, starting transfers between devices, ring_form(): behind = lax.ppermute(behind, AXIS, back)  7.71 us
  transfers between devices with their start and end apart: 44, of which 20 were waited for; matrix products, arithmetic and copies ran while one was open for 36% of the time, Pallas kernels for 0%

profile of v1, /device:TPU:0, one launch (start us, length us, event | category | flops | bytes accessed | tf_op | source)
XLA Modules:
  0.0 243.7 jit_solution(2702179826791676137)
XLA Ops:
  0.0 0.5 collective-permute-start.35
  0.5 1.3 fusion.234
  1.8 2.6 %collective-permute-start = (bf16[64,4096]{1,0:T(8,128)(2,1)S(1)}, bf16[64,4096]{1,0:T(8,128)(2,1)S(1)}, u32[]{:S(2)}, u32[]{:S(2)}) collective-permute-start(bf16[64,4096]{1,0:T(8,128)(2,1)S(1)} %get-tuple-element.24), channel_id=1, source_target_pairs={{0,4},{1,5},{2,0},{3,1},{4,8},{5,9},{6,2},{7,3},{8,12},{9,13},{10,... | collective-permute-start | bytes 1572872 | tf_op jit(solution)/shard_map/ppermute | solution.py:72
  4.5 0.6 dynamic_slice.100
  7.8 0.6 dynamic_slice.101
  9.1 23.4 %all-gather = f32[256,128]{1,0:T(8,128)S(1)} all-gather(f32[16,128]{1,0:T(8,128)S(1)} %pad_maximum_fusion.8), channel_id=2, replica_groups=mesh['group'=2,'expert'=16] {'expert'}, dimensions={0}, use_global_device_ids=true | all-gather | bytes 139264 | tf_op jit(solution)/shard_map/all_gather | solution.py:26
  33.9 2.0 collective-permute-start.6
  36.2 11.9 %collective-permute-done.5 = bf16[64,4096]{1,0:T(8,128)(2,1)S(1)} collective-permute-done((bf16[64,4096]{1,0:T(8,128)(2,1)S(1)}, bf16[64,4096]{1,0:T(8,128)(2,1)S(1)}, u32[]{:S(2)}, u32[]{:S(2)}) %collective-permute-start.5) | collective-permute-done | bytes 524320 | tf_op jit(solution)/shard_map/ppermute | solution.py:72
  48.4 6.6 %fusion = f32[256,1536]{1,0:T(8,128)S(1)} fusion(bf16[1,4096,1536]{2,1,0:T(8,128)(2,1)} %param.10, bf16[128,4096]{1,0:T(8,128)(2,1)S(1)} %collective-permute-done.35, bf16[128,4096]{1,0:T(8,128)(2,1)S(1)} %copy-done), kind=kOutput, calls=%fused_computation | convolution fusion | flops 3225419776 | bytes 16252928 | tf_op jit(solution)/shard_map/dot_general | solution.py:11
  55.0 4.8 %fusion.101 = f32[256,4096]{1,0:T(8,128)S(1)} fusion(bf16[1,768,4096]{2,1,0:T(8,128)(2,1)} %param.11, f32[256]{0:T(256)S(1)} %bitcast.202, f32[256,1536]{1,0:T(8,128)S(1)} %fusion), kind=kOutput, calls=%fused_computation.55 | convolution fusion | flops 1614938112 | bytes 12059648 | tf_op jit(solution)/shard_map/dot_general | solution.py:15
  59.9 0.5 collective-permute-start.36
  60.7 1.8 collective-permute-start.11
  62.5 3.4 %fusion.14 = f32[256,1536]{1,0:T(8,128)S(1)} fusion(bf16[1,4096,1536]{2,1,0:T(8,128)(2,1)S(1)} %bitcast.204, bf16[128,4096]{1,0:T(8,128)(2,1)S(1)} %collective-permute-done.2, bf16[64,4096]{1,0:T(8,128)(2,1)S(1)} %collective-permute-done.1, bf16[64,4096]{1,0:T(8,128)(2,1)S(1)} %collective-permute-done), kind=kOutput, calls=%fused_computation.14 | convolution fusion | flops 3227516928 | bytes 16252928 | tf_op jit(solution)/shard_map/dot_general | solution.py:11
  66.0 4.7 %fusion.38 = f32[256,4096]{1,0:T(8,128)S(1)} fusion(bf16[1,768,4096]{2,1,0:T(8,128)(2,1)} %param.11, f32[256]{0:T(256)S(1)} %bitcast.201, f32[256,1536]{1,0:T(8,128)S(1)} %fusion.14), kind=kOutput, calls=%fused_computation.34 | convolution fusion | flops 1614938112 | bytes 12059648 | tf_op jit(solution)/shard_map/dot_general | solution.py:15
  70.9 3.5 %collective-permute-done.10 = bf16[64,4096]{1,0:T(8,128)(2,1)S(1)} collective-permute-done((bf16[64,4096]{1,0:T(8,128)(2,1)S(1)}, bf16[64,4096]{1,0:T(8,128)(2,1)S(1)}, u32[]{:S(2)}, u32[]{:S(2)}) %collective-permute-start.10) | collective-permute-done | bytes 524320 | tf_op jit(solution)/shard_map/ppermute | solution.py:72
  74.9 1.8 collective-permute-start.16
  76.7 6.7 %fusion.12 = f32[256,1536]{1,0:T(8,128)S(1)} fusion(bf16[1,4096,1536]{2,1,0:T(8,128)(2,1)} %param.10, bf16[128,4096]{1,0:T(8,128)(2,1)} %collective-permute-done.7, bf16[64,4096]{1,0:T(8,128)(2,1)S(1)} %collective-permute-done.6, bf16[64,4096]{1,0:T(8,128)(2,1)S(1)} %collective-permute-done.5), kind=kOutput, calls=%fused_computation.12 | convolution fusion | flops 3227516928 | bytes 16252928 | tf_op jit(solution)/shard_map/dot_general | solution.py:11
  83.4 1.9 fusion.47
  85.5 3.4 %collective-permute-done.15 = bf16[64,4096]{1,0:T(8,128)(2,1)S(1)} collective-permute-done((bf16[64,4096]{1,0:T(8,128)(2,1)S(1)}, bf16[64,4096]{1,0:T(8,128)(2,1)S(1)}, u32[]{:S(2)}, u32[]{:S(2)}) %collective-permute-start.15) | collective-permute-done | bytes 524320 | tf_op jit(solution)/shard_map/ppermute | solution.py:72
  89.0 0.6 collective-permute-start.17
  89.6 0.6 collective-permute-start.20
  90.2 6.4 %fusion.10 = f32[256,1536]{1,0:T(8,128)S(1)} fusion(bf16[1,4096,1536]{2,1,0:T(8,128)(2,1)} %param.10, bf16[128,4096]{1,0:T(8,128)(2,1)S(1)} %collective-permute-done.12, bf16[64,4096]{1,0:T(8,128)(2,1)S(1)} %collective-permute-done.11, bf16[64,4096]{1,0:T(8,128)(2,1)S(1)} %collective-permute-done.10), kind=kOutput, calls=%fused_computation.10 | convolution fusion | flops 3227516928 | bytes 16252928 | tf_op jit(solution)/shard_map/dot_general | solution.py:11
  96.6 4.7 %fusion.56 = f32[256,4096]{1,0:T(8,128)S(1)} fusion(bf16[1,768,4096]{2,1,0:T(8,128)(2,1)} %param.11, f32[256]{0:T(256)S(1)} %bitcast.199, f32[256,1536]{1,0:T(8,128)S(1)} %fusion.10), kind=kOutput, calls=%fused_computation.40 | convolution fusion | flops 1614938112 | bytes 12059648 | tf_op jit(solution)/shard_map/dot_general | solution.py:15
  101.4 1.5 collective-permute-start.21
  103.5 1.7 collective-permute-start.37
  105.2 11.1 %collective-permute-done.21 = bf16[64,4096]{1,0:T(8,128)(2,1)S(1)} collective-permute-done((bf16[64,4096]{1,0:T(8,128)(2,1)S(1)}, bf16[64,4096]{1,0:T(8,128)(2,1)S(1)}, u32[]{:S(2)}, u32[]{:S(2)}) %collective-permute-start.21) | collective-permute-done | bytes 524320 | tf_op jit(solution)/shard_map/ppermute | solution.py:73
  116.2 0.9 collective-permute-start.4
  117.4 6.4 %fusion.8 = f32[256,1536]{1,0:T(8,128)S(1)} fusion(bf16[1,4096,1536]{2,1,0:T(8,128)(2,1)} %param.10, bf16[128,4096]{1,0:T(8,128)(2,1)S(1)} %collective-permute-done.17, bf16[64,4096]{1,0:T(8,128)(2,1)S(1)} %collective-permute-done.16, bf16[64,4096]{1,0:T(8,128)(2,1)S(1)} %collective-permute-done.15), kind=kOutput, calls=%fused_computation.8 | convolution fusion | flops 3227516928 | bytes 16252928 | tf_op jit(solution)/shard_map/dot_general | solution.py:11
  123.8 4.7 %fusion.65 = f32[256,4096]{1,0:T(8,128)S(1)} fusion(bf16[1,768,4096]{2,1,0:T(8,128)(2,1)} %param.11, f32[256]{0:T(256)S(1)} %bitcast.198, f32[256,1536]{1,0:T(8,128)S(1)} %fusion.8), kind=kOutput, calls=%fused_computation.43 | convolution fusion | flops 1614938112 | bytes 12059648 | tf_op jit(solution)/shard_map/dot_general | solution.py:15
  128.6 0.5 collective-permute-start.22
  129.4 1.8 collective-permute-start.25
  131.2 0.3 collective-permute-start.26
  131.8 11.6 %collective-permute-done.25 = bf16[64,4096]{1,0:T(8,128)(2,1)S(1)} collective-permute-done((bf16[64,4096]{1,0:T(8,128)(2,1)S(1)}, bf16[64,4096]{1,0:T(8,128)(2,1)S(1)}, u32[]{:S(2)}, u32[]{:S(2)}) %collective-permute-start.25) | collective-permute-done | bytes 524320 | tf_op jit(solution)/shard_map/ppermute | solution.py:72
  143.3 1.4 collective-permute-done.26
  144.8 0.3 collective-permute-start.38
  145.2 2.0 collective-permute-start.9
  147.2 6.5 %fusion.6 = f32[256,1536]{1,0:T(8,128)S(1)} fusion(bf16[1,4096,1536]{2,1,0:T(8,128)(2,1)} %param.10, bf16[128,4096]{1,0:T(8,128)(2,1)S(1)} %collective-permute-done.22, bf16[64,4096]{1,0:T(8,128)(2,1)S(1)} %collective-permute-done.21, bf16[64,4096]{1,0:T(8,128)(2,1)S(1)} %collective-permute-done.20), kind=kOutput, calls=%fused_computation.6 | convolution fusion | flops 3227516928 | bytes 16252928 | tf_op jit(solution)/shard_map/dot_general | solution.py:11
  153.7 4.7 %fusion.74 = f32[256,4096]{1,0:T(8,128)S(1)} fusion(bf16[1,768,4096]{2,1,0:T(8,128)(2,1)} %param.11, f32[256]{0:T(256)S(1)} %bitcast.197, f32[256,1536]{1,0:T(8,128)S(1)} %fusion.6), kind=kOutput, calls=%fused_computation.46 | convolution fusion | flops 1614938112 | bytes 12059648 | tf_op jit(solution)/shard_map/dot_general | solution.py:15
  158.8 1.8 collective-permute-start.30
  161.1 12.0 %collective-permute-done.30 = bf16[64,4096]{1,0:T(8,128)(2,1)S(1)} collective-permute-done((bf16[64,4096]{1,0:T(8,128)(2,1)S(1)}, bf16[64,4096]{1,0:T(8,128)(2,1)S(1)}, u32[]{:S(2)}, u32[]{:S(2)}) %collective-permute-start.30) | collective-permute-done | bytes 524320 | tf_op jit(solution)/shard_map/ppermute | solution.py:72
  173.2 1.8 collective-permute-start.14
  175.6 11.1 %collective-permute-done.14 = bf16[64,4096]{1,0:T(8,128)(2,1)S(1)} collective-permute-done((bf16[64,4096]{1,0:T(8,128)(2,1)S(1)}, bf16[64,4096]{1,0:T(8,128)(2,1)S(1)}, u32[]{:S(2)}, u32[]{:S(2)}) %collective-permute-start.14) | collective-permute-done | bytes 524320 | tf_op jit(solution)/shard_map/ppermute | solution.py:94
  186.7 1.5 collective-permute-done.39
  188.5 1.8 collective-permute-start.19
  190.3 0.3 collective-permute-start.40
  190.5 6.6 %fusion.4 = f32[256,1536]{1,0:T(8,128)S(1)} fusion(bf16[1,4096,1536]{2,1,0:T(8,128)(2,1)} %param.10, bf16[128,4096]{1,0:T(8,128)(2,1)S(1)} %collective-permute-done.27, bf16[64,4096]{1,0:T(8,128)(2,1)S(1)} %collective-permute-done.26, bf16[64,4096]{1,0:T(8,128)(2,1)S(1)} %collective-permute-done.25), kind=kOutput, calls=%fused_computation.4 | convolution fusion | flops 3227516928 | bytes 16252928 | tf_op jit(solution)/shard_map/dot_general | solution.py:11
  197.2 1.9 fusion.83
  199.5 1.8 collective-permute-done.19
  201.4 1.5 collective-permute-done.40
  203.1 1.8 collective-permute-start.24
  204.9 0.3 collective-permute-start.41
  205.2 6.5 %fusion.2 = f32[256,1536]{1,0:T(8,128)S(1)} fusion(bf16[1,4096,1536]{2,1,0:T(8,128)(2,1)} %param.10, bf16[128,4096]{1,0:T(8,128)(2,1)S(1)} %collective-permute-done.32, bf16[64,4096]{1,0:T(8,128)(2,1)S(1)} %collective-permute-done.31, bf16[64,4096]{1,0:T(8,128)(2,1)S(1)} %collective-permute-done.30), kind=kOutput, calls=%fused_computation.2 | convolution fusion | flops 3227516928 | bytes 16252928 | tf_op jit(solution)/shard_map/dot_general | solution.py:11
  211.7 1.9 fusion.92
  214.1 1.1 collective-permute-done.24
  215.2 2.2 collective-permute-done.41
  217.5 1.3 collective-permute-start.29
  218.8 0.8 collective-permute-start.42
  219.8 9.3 %collective-permute-done.29 = bf16[64,4096]{1,0:T(8,128)(2,1)S(1)} collective-permute-done((bf16[64,4096]{1,0:T(8,128)(2,1)S(1)}, bf16[64,4096]{1,0:T(8,128)(2,1)S(1)}, u32[]{:S(2)}, u32[]{:S(2)}) %collective-permute-start.29) | collective-permute-done | bytes 524320 | tf_op jit(solution)/shard_map/ppermute | solution.py:94
  229.1 1.5 collective-permute-done.42
  230.8 0.9 collective-permute-start.34
  231.7 1.2 collective-permute-start.43
  233.1 8.6 %collective-permute-done.34 = bf16[64,4096]{1,0:T(8,128)(2,1)S(1)} collective-permute-done((bf16[64,4096]{1,0:T(8,128)(2,1)S(1)}, bf16[64,4096]{1,0:T(8,128)(2,1)S(1)}, u32[]{:S(2)}, u32[]{:S(2)}) %collective-permute-start.34) | collective-permute-done | bytes 524320 | tf_op jit(solution)/shard_map/ppermute | solution.py:100
  241.7 0.8 collective-permute-done.43
  242.7 1.0 pad_maximum_fusion.7
  (119 shorter events, 8.5 us)
Async XLA Ops:
  0.0 4.5 %copy-start.3 = (s32[16]{0:T(128)S(1)}, s32[16]{0:T(128)}, u32[]{:S(2)}) copy-start(s32[16]{0:T(128)} %param.12) | copy-start | bytes 196
  0.0 7.8 %copy-start.4 = (s32[16]{0:T(128)S(1)}, s32[16]{0:T(128)}, u32[]{:S(2)}) copy-start(s32[16]{0:T(128)} %param.13) | copy-start | bytes 196
  0.0 9.1 %copy-start.1 = (s32[128,8]{0,1:T(8,128)S(1)}, s32[128,8]{0,1:T(8,128)}, u32[]{:S(2)}) copy-start(s32[128,8]{0,1:T(8,128)} %param.8) | copy-start | bytes 12292
  0.0 9.1 %copy-start.2 = (f32[128,8]{0,1:T(8,128)S(1)}, f32[128,8]{0,1:T(8,128)}, u32[]{:S(2)}) copy-start(f32[128,8]{0,1:T(8,128)} %param.9) | copy-start | bytes 12292
  0.0 48.3 %collective-permute-start.35 = (bf16[128,4096]{1,0:T(8,128)(2,1)}, bf16[128,4096]{1,0:T(8,128)(2,1)S(1)}, u32[]{:S(2)}, u32[]{:S(2)}) collective-permute-start(bf16[128,4096]{1,0:T(8,128)(2,1)} %param.7), channel_id=1, source_target_pairs={{0,1},{1,0},{2,3},{3,2},{4,5},{5,4},{6,7},{7,6},{8,9},{9,8},{10,11... | collective-permute-start | bytes 3145736 | tf_op jit(solution)/shard_map/ppermute | solution.py:75
  1.8 32.1 %collective-permute-start = (bf16[64,4096]{1,0:T(8,128)(2,1)S(1)}, bf16[64,4096]{1,0:T(8,128)(2,1)S(1)}, u32[]{:S(2)}, u32[]{:S(2)}) collective-permute-start(bf16[64,4096]{1,0:T(8,128)(2,1)S(1)} %get-tuple-element.24), channel_id=1, source_target_pairs={{0,4},{1,5},{2,0},{3,1},{4,8},{5,9},{6,2},{7,3},{8,12},{9,13},{10,... | collective-permute-start | bytes 1572872 | tf_op jit(solution)/shard_map/ppermute | solution.py:72
  4.4 29.5 %collective-permute-start.1 = (bf16[64,4096]{1,0:T(8,128)(2,1)S(1)}, bf16[64,4096]{1,0:T(8,128)(2,1)S(1)}, u32[]{:S(2)}, u32[]{:S(2)}) collective-permute-start(bf16[64,4096]{1,0:T(8,128)(2,1)S(1)} %get-tuple-element.25), channel_id=1, source_target_pairs={{0,2},{1,3},{2,6},{3,7},{4,0},{5,1},{6,10},{7,11},{8,4},{9,5},{10,... | collective-permute-start | bytes 1572872 | tf_op jit(solution)/shard_map/ppermute | solution.py:73
  33.9 14.2 %collective-permute-start.5 = (bf16[64,4096]{1,0:T(8,128)(2,1)S(1)}, bf16[64,4096]{1,0:T(8,128)(2,1)S(1)}, u32[]{:S(2)}, u32[]{:S(2)}) collective-permute-start(bf16[64,4096]{1,0:T(8,128)(2,1)S(1)} %collective-permute-done), channel_id=1, source_target_pairs={{0,4},{1,5},{2,0},{3,1},{4,8},{5,9},{6,2},{7,3},{8,12},{9,13},{10,... | collective-permute-start | bytes 1572872 | tf_op jit(solution)/shard_map/ppermute | solution.py:72
  33.9 14.2 %collective-permute-start.6 = (bf16[64,4096]{1,0:T(8,128)(2,1)S(1)}, bf16[64,4096]{1,0:T(8,128)(2,1)S(1)}, u32[]{:S(2)}, u32[]{:S(2)}) collective-permute-start(bf16[64,4096]{1,0:T(8,128)(2,1)S(1)} %collective-permute-done.1), channel_id=1, source_target_pairs={{0,2},{1,3},{2,6},{3,7},{4,0},{5,1},{6,10},{7,11},{8,4},{9,5},{10,... | collective-permute-start | bytes 1572872 | tf_op jit(solution)/shard_map/ppermute | solution.py:73
  36.0 12.3 %copy-start = (bf16[128,4096]{1,0:T(8,128)(2,1)S(1)}, bf16[128,4096]{1,0:T(8,128)(2,1)}, u32[]{:S(2)}) copy-start(bf16[128,4096]{1,0:T(8,128)(2,1)} %param.7) | copy-start | bytes 3145732
  36.1 26.4 %collective-permute-start.2 = (bf16[128,4096]{1,0:T(8,128)(2,1)S(1)}, bf16[128,4096]{1,0:T(8,128)(2,1)S(1)}, u32[]{:S(2)}, u32[]{:S(2)}) collective-permute-start(bf16[128,4096]{1,0:T(8,128)(2,1)S(1)} %pad_maximum_fusion), channel_id=1, source_target_pairs={{0,1},{1,0},{2,3},{3,2},{4,5},{5,4},{6,7},{7,6},{8,9},{9,8},{10,11... | collective-permute-start | bytes 3145736 | tf_op jit(solution)/shard_map/ppermute | solution.py:75
  48.3 26.6 %collective-permute-start.7 = (bf16[128,4096]{1,0:T(8,128)(2,1)S(1)}, bf16[128,4096]{1,0:T(8,128)(2,1)}, u32[]{:S(2)}, u32[]{:S(2)}) collective-permute-start(bf16[128,4096]{1,0:T(8,128)(2,1)S(1)} %pad_maximum_fusion.1), channel_id=1, source_target_pairs={{0,1},{1,0},{2,3},{3,2},{4,5},{5,4},{6,7},{7,6},{8,9},{9,8},{10,11... | collective-permute-start | bytes 3145736 | tf_op jit(solution)/shard_map/ppermute | solution.py:75
  48.4 14.1 %slice-start = ((s8[12582912]{0:T(1024)(128)(4,1)}), s8[4194304]{0:T(1024)(128)(4,1)S(1)}, s32[]{:S(2)}) async-start(s8[12582912]{0:T(1024)(128)(4,1)} %bitcast.203), calls=%async_computation | async-start | bytes 8388608
  48.4 14.1 %slice-start.1 = ((s8[12582912]{0:T(1024)(128)(4,1)}), s8[4194304]{0:T(1024)(128)(4,1)S(1)}, s32[]{:S(2)}) async-start(s8[12582912]{0:T(1024)(128)(4,1)} %bitcast.203), calls=%async_computation.1 | async-start | bytes 8388608
  55.0 7.5 %slice-start.2 = ((s8[12582912]{0:T(1024)(128)(4,1)}), s8[4194304]{0:T(1024)(128)(4,1)S(1)}, s32[]{:S(2)}) async-start(s8[12582912]{0:T(1024)(128)(4,1)} %bitcast.203), calls=%async_computation.2 | async-start | bytes 8388608
  59.9 172.9 %collective-permute-start.36 = (bf16[128,4096]{1,0:T(8,128)(2,1)S(1)}, bf16[128,4096]{1,0:T(8,128)(2,1)S(1)}, u32[]{:S(2)}, u32[]{:S(2)}) collective-permute-start(bf16[128,4096]{1,0:T(8,128)(2,1)S(1)} %slice.540), channel_id=1, source_target_pairs={{0,1},{1,0},{2,3},{3,2},{4,5},{5,4},{6,7},{7,6},{8,9},{9,8},{10,11... | collective-permute-start | bytes 3145736 | tf_op jit(solution)/shard_map/ppermute | solution.py:87
  60.5 13.9 %collective-permute-start.10 = (bf16[64,4096]{1,0:T(8,128)(2,1)S(1)}, bf16[64,4096]{1,0:T(8,128)(2,1)S(1)}, u32[]{:S(2)}, u32[]{:S(2)}) collective-permute-start(bf16[64,4096]{1,0:T(8,128)(2,1)S(1)} %collective-permute-done.5), channel_id=1, source_target_pairs={{0,4},{1,5},{2,0},{3,1},{4,8},{5,9},{6,2},{7,3},{8,12},{9,13},{10,... | collective-permute-start | bytes 1572872 | tf_op jit(solution)/shard_map/ppermute | solution.py:72
  60.7 13.7 %collective-permute-start.11 = (bf16[64,4096]{1,0:T(8,128)(2,1)S(1)}, bf16[64,4096]{1,0:T(8,128)(2,1)S(1)}, u32[]{:S(2)}, u32[]{:S(2)}) collective-permute-start(bf16[64,4096]{1,0:T(8,128)(2,1)S(1)} %collective-permute-done.6), channel_id=1, source_target_pairs={{0,2},{1,3},{2,6},{3,7},{4,0},{5,1},{6,10},{7,11},{8,4},{9,5},{10,... | collective-permute-start | bytes 1572872 | tf_op jit(solution)/shard_map/ppermute | solution.py:73
  70.8 30.6 %collective-permute-start.3 = (bf16[128,4096]{1,0:T(8,128)(2,1)S(1)}, bf16[128,4096]{1,0:T(8,128)(2,1)S(1)}, u32[]{:S(2)}, u32[]{:S(2)}) collective-permute-start(bf16[128,4096]{1,0:T(8,128)(2,1)S(1)} %slice.547), channel_id=1, source_target_pairs={{0,1},{1,0},{2,3},{3,2},{4,5},{5,4},{6,7},{7,6},{8,9},{9,8},{10,11... | collective-permute-start | bytes 3145736 | tf_op jit(solution)/shard_map/ppermute | solution.py:87
  74.4 9.0 %slice-start.3 = ((s8[6291456]{0:T(1024)(128)(4,1)}), s8[4194304]{0:T(1024)(128)(4,1)S(1)}, s32[]{:S(2)}) async-start(s8[6291456]{0:T(1024)(128)(4,1)} %bitcast.205), calls=%async_computation.3 | async-start | bytes 8388608
  74.5 8.9 %slice-start.4 = ((s8[6291456]{0:T(1024)(128)(4,1)}), s8[2097152]{0:T(1024)(128)(4,1)S(1)}, s32[]{:S(2)}) async-start(s8[6291456]{0:T(1024)(128)(4,1)} %bitcast.205), calls=%async_computation.4 | async-start | bytes 4194304
  74.5 15.1 %collective-permute-start.12 = (bf16[128,4096]{1,0:T(8,128)(2,1)S(1)}, bf16[128,4096]{1,0:T(8,128)(2,1)S(1)}, u32[]{:S(2)}, u32[]{:S(2)}) collective-permute-start(bf16[128,4096]{1,0:T(8,128)(2,1)S(1)} %pad_maximum_fusion.2), channel_id=1, source_target_pairs={{0,1},{1,0},{2,3},{3,2},{4,5},{5,4},{6,7},{7,6},{8,9},{9,8},{10,11... | collective-permute-start | bytes 3145736 | tf_op jit(solution)/shard_map/ppermute | solution.py:75
  74.6 14.3 %collective-permute-start.15 = (bf16[64,4096]{1,0:T(8,128)(2,1)S(1)}, bf16[64,4096]{1,0:T(8,128)(2,1)S(1)}, u32[]{:S(2)}, u32[]{:S(2)}) collective-permute-start(bf16[64,4096]{1,0:T(8,128)(2,1)S(1)} %collective-permute-done.10), channel_id=1, source_target_pairs={{0,4},{1,5},{2,0},{3,1},{4,8},{5,9},{6,2},{7,3},{8,12},{9,13},{10,... | collective-permute-start | bytes 1572872 | tf_op jit(solution)/shard_map/ppermute | solution.py:72
  74.9 14.1 %collective-permute-start.16 = (bf16[64,4096]{1,0:T(8,128)(2,1)S(1)}, bf16[64,4096]{1,0:T(8,128)(2,1)S(1)}, u32[]{:S(2)}, u32[]{:S(2)}) collective-permute-start(bf16[64,4096]{1,0:T(8,128)(2,1)S(1)} %collective-permute-done.11), channel_id=1, source_target_pairs={{0,2},{1,3},{2,6},{3,7},{4,0},{5,1},{6,10},{7,11},{8,4},{9,5},{10,... | collective-permute-start | bytes 1572872 | tf_op jit(solution)/shard_map/ppermute | solution.py:73
  88.9 39.7 %collective-permute-start.8 = (bf16[128,4096]{1,0:T(8,128)(2,1)S(1)}, bf16[128,4096]{1,0:T(8,128)(2,1)S(1)}, u32[]{:S(2)}, u32[]{:S(2)}) collective-permute-start(bf16[128,4096]{1,0:T(8,128)(2,1)S(1)} %slice.546), channel_id=1, source_target_pairs={{0,1},{1,0},{2,3},{3,2},{4,5},{5,4},{6,7},{7,6},{8,9},{9,8},{10,11... | collective-permute-start | bytes 3145736 | tf_op jit(solution)/shard_map/ppermute | solution.py:87
  89.0 28.3 %collective-permute-start.17 = (bf16[128,4096]{1,0:T(8,128)(2,1)S(1)}, bf16[128,4096]{1,0:T(8,128)(2,1)S(1)}, u32[]{:S(2)}, u32[]{:S(2)}) collective-permute-start(bf16[128,4096]{1,0:T(8,128)(2,1)S(1)} %pad_maximum_fusion.3), channel_id=1, source_target_pairs={{0,1},{1,0},{2,3},{3,2},{4,5},{5,4},{6,7},{7,6},{8,9},{9,8},{10,11... | collective-permute-start | bytes 3145736 | tf_op jit(solution)/shard_map/ppermute | solution.py:75
  89.6 13.9 %collective-permute-start.20 = (bf16[64,4096]{1,0:T(8,128)(2,1)S(1)}, bf16[64,4096]{1,0:T(8,128)(2,1)S(1)}, u32[]{:S(2)}, u32[]{:S(2)}) collective-permute-start(bf16[64,4096]{1,0:T(8,128)(2,1)S(1)} %collective-permute-done.15), channel_id=1, source_target_pairs={{0,4},{1,5},{2,0},{3,1},{4,8},{5,9},{6,2},{7,3},{8,12},{9,13},{10,... | collective-permute-start | bytes 1572872 | tf_op jit(solution)/shard_map/ppermute | solution.py:72
  101.4 14.8 %collective-permute-start.21 = (bf16[64,4096]{1,0:T(8,128)(2,1)S(1)}, bf16[64,4096]{1,0:T(8,128)(2,1)S(1)}, u32[]{:S(2)}, u32[]{:S(2)}) collective-permute-start(bf16[64,4096]{1,0:T(8,128)(2,1)S(1)} %collective-permute-done.16), channel_id=1, source_target_pairs={{0,2},{1,3},{2,6},{3,7},{4,0},{5,1},{6,10},{7,11},{8,4},{9,5},{10,... | collective-permute-start | bytes 1572872 | tf_op jit(solution)/shard_map/ppermute | solution.py:73
  103.5 25.9 %collective-permute-start.37 = (bf16[64,4096]{1,0:T(8,128)(2,1)S(1)}, bf16[64,4096]{1,0:T(8,128)(2,1)S(1)}, u32[]{:S(2)}, u32[]{:S(2)}) collective-permute-start(bf16[64,4096]{1,0:T(8,128)(2,1)S(1)} %get-tuple-element.23), channel_id=1, source_target_pairs={{0,2},{1,3},{2,6},{3,7},{4,0},{5,1},{6,10},{7,11},{8,4},{9,5},{10,... | collective-permute-start | bytes 1572872 | tf_op jit(solution)/shard_map/ppermute | solution.py:95
  116.2 15.0 %collective-permute-start.4 = (bf16[64,4096]{1,0:T(8,128)(2,1)S(1)}, bf16[64,4096]{1,0:T(8,128)(2,1)S(1)}, u32[]{:S(2)}, u32[]{:S(2)}) collective-permute-start(bf16[64,4096]{1,0:T(8,128)(2,1)S(1)} %get-tuple-element.22), channel_id=1, source_target_pairs={{0,4},{1,5},{2,0},{3,1},{4,8},{5,9},{6,2},{7,3},{8,12},{9,13},{10,... | collective-permute-start | bytes 1572872 | tf_op jit(solution)/shard_map/ppermute | solution.py:94
  117.3 41.2 %collective-permute-start.13 = (bf16[128,4096]{1,0:T(8,128)(2,1)S(1)}, bf16[128,4096]{1,0:T(8,128)(2,1)S(1)}, u32[]{:S(2)}, u32[]{:S(2)}) collective-permute-start(bf16[128,4096]{1,0:T(8,128)(2,1)S(1)} %slice.545), channel_id=1, source_target_pairs={{0,1},{1,0},{2,3},{3,2},{4,5},{5,4},{6,7},{7,6},{8,9},{9,8},{10,11... | collective-permute-start | bytes 3145736 | tf_op jit(solution)/shard_map/ppermute | solution.py:87
  128.6 16.5 %collective-permute-start.22 = (bf16[128,4096]{1,0:T(8,128)(2,1)S(1)}, bf16[128,4096]{1,0:T(8,128)(2,1)S(1)}, u32[]{:S(2)}, u32[]{:S(2)}) collective-permute-start(bf16[128,4096]{1,0:T(8,128)(2,1)S(1)} %pad_maximum_fusion.4), channel_id=1, source_target_pairs={{0,1},{1,0},{2,3},{3,2},{4,5},{5,4},{6,7},{7,6},{8,9},{9,8},{10,11... | collective-permute-start | bytes 3145736 | tf_op jit(solution)/shard_map/ppermute | solution.py:75
  129.4 13.9 %collective-permute-start.25 = (bf16[64,4096]{1,0:T(8,128)(2,1)S(1)}, bf16[64,4096]{1,0:T(8,128)(2,1)S(1)}, u32[]{:S(2)}, u32[]{:S(2)}) collective-permute-start(bf16[64,4096]{1,0:T(8,128)(2,1)S(1)} %collective-permute-done.20), channel_id=1, source_target_pairs={{0,4},{1,5},{2,0},{3,1},{4,8},{5,9},{6,2},{7,3},{8,12},{9,13},{10,... | collective-permute-start | bytes 1572872 | tf_op jit(solution)/shard_map/ppermute | solution.py:72
  131.2 13.6 %collective-permute-start.26 = (bf16[64,4096]{1,0:T(8,128)(2,1)S(1)}, bf16[64,4096]{1,0:T(8,128)(2,1)S(1)}, u32[]{:S(2)}, u32[]{:S(2)}) collective-permute-start(bf16[64,4096]{1,0:T(8,128)(2,1)S(1)} %collective-permute-done.21), channel_id=1, source_target_pairs={{0,2},{1,3},{2,6},{3,7},{4,0},{5,1},{6,10},{7,11},{8,4},{9,5},{10,... | collective-permute-start | bytes 1572872 | tf_op jit(solution)/shard_map/ppermute | solution.py:73
  143.3 32.0 %collective-permute-start.18 = (bf16[128,4096]{1,0:T(8,128)(2,1)S(1)}, bf16[128,4096]{1,0:T(8,128)(2,1)S(1)}, u32[]{:S(2)}, u32[]{:S(2)}) collective-permute-start(bf16[128,4096]{1,0:T(8,128)(2,1)S(1)} %slice.544), channel_id=1, source_target_pairs={{0,1},{1,0},{2,3},{3,2},{4,5},{5,4},{6,7},{7,6},{8,9},{9,8},{10,11... | collective-permute-start | bytes 3145736 | tf_op jit(solution)/shard_map/ppermute | solution.py:87
  144.8 14.0 %collective-permute-start.38 = (bf16[64,4096]{1,0:T(8,128)(2,1)S(1)}, bf16[64,4096]{1,0:T(8,128)(2,1)S(1)}, u32[]{:S(2)}, u32[]{:S(2)}) collective-permute-start(bf16[64,4096]{1,0:T(8,128)(2,1)S(1)} %get-tuple-element.21), channel_id=1, source_target_pairs={{0,2},{1,3},{2,6},{3,7},{4,0},{5,1},{6,10},{7,11},{8,4},{9,5},{10,... | collective-permute-start | bytes 1572872 | tf_op jit(solution)/shard_map/ppermute | solution.py:95
  145.2 15.4 %collective-permute-start.9 = (bf16[64,4096]{1,0:T(8,128)(2,1)S(1)}, bf16[64,4096]{1,0:T(8,128)(2,1)S(1)}, u32[]{:S(2)}, u32[]{:S(2)}) collective-permute-start(bf16[64,4096]{1,0:T(8,128)(2,1)S(1)} %get-tuple-element.20), channel_id=1, source_target_pairs={{0,4},{1,5},{2,0},{3,1},{4,8},{5,9},{6,2},{7,3},{8,12},{9,13},{10,... | collective-permute-start | bytes 1572872 | tf_op jit(solution)/shard_map/ppermute | solution.py:94
  158.5 31.8 %collective-permute-start.27 = (bf16[128,4096]{1,0:T(8,128)(2,1)S(1)}, bf16[128,4096]{1,0:T(8,128)(2,1)S(1)}, u32[]{:S(2)}, u32[]{:S(2)}) collective-permute-start(bf16[128,4096]{1,0:T(8,128)(2,1)S(1)} %pad_maximum_fusion.5), channel_id=1, source_target_pairs={{0,1},{1,0},{2,3},{3,2},{4,5},{5,4},{6,7},{7,6},{8,9},{9,8},{10,11... | collective-permute-start | bytes 3145736 | tf_op jit(solution)/shard_map/ppermute | solution.py:75
  158.8 14.4 %collective-permute-start.30 = (bf16[64,4096]{1,0:T(8,128)(2,1)S(1)}, bf16[64,4096]{1,0:T(8,128)(2,1)S(1)}, u32[]{:S(2)}, u32[]{:S(2)}) collective-permute-start(bf16[64,4096]{1,0:T(8,128)(2,1)S(1)} %collective-permute-done.25), channel_id=1, source_target_pairs={{0,4},{1,5},{2,0},{3,1},{4,8},{5,9},{6,2},{7,3},{8,12},{9,13},{10,... | collective-permute-start | bytes 1572872 | tf_op jit(solution)/shard_map/ppermute | solution.py:72
  160.6 14.3 %collective-permute-start.31 = (bf16[64,4096]{1,0:T(8,128)(2,1)S(1)}, bf16[64,4096]{1,0:T(8,128)(2,1)S(1)}, u32[]{:S(2)}, u32[]{:S(2)}) collective-permute-start(bf16[64,4096]{1,0:T(8,128)(2,1)S(1)} %collective-permute-done.26), channel_id=1, source_target_pairs={{0,2},{1,3},{2,6},{3,7},{4,0},{5,1},{6,10},{7,11},{8,4},{9,5},{10,... | collective-permute-start | bytes 1572872 | tf_op jit(solution)/shard_map/ppermute | solution.py:73
  173.2 13.5 %collective-permute-start.14 = (bf16[64,4096]{1,0:T(8,128)(2,1)S(1)}, bf16[64,4096]{1,0:T(8,128)(2,1)S(1)}, u32[]{:S(2)}, u32[]{:S(2)}) collective-permute-start(bf16[64,4096]{1,0:T(8,128)(2,1)S(1)} %get-tuple-element.18), channel_id=1, source_target_pairs={{0,4},{1,5},{2,0},{3,1},{4,8},{5,9},{6,2},{7,3},{8,12},{9,13},{10,... | collective-permute-start | bytes 1572872 | tf_op jit(solution)/shard_map/ppermute | solution.py:94
  174.9 13.3 %collective-permute-start.39 = (bf16[64,4096]{1,0:T(8,128)(2,1)S(1)}, bf16[64,4096]{1,0:T(8,128)(2,1)S(1)}, u32[]{:S(2)}, u32[]{:S(2)}) collective-permute-start(bf16[64,4096]{1,0:T(8,128)(2,1)S(1)} %get-tuple-element.19), channel_id=1, source_target_pairs={{0,2},{1,3},{2,6},{3,7},{4,0},{5,1},{6,10},{7,11},{8,4},{9,5},{10,... | collective-permute-start | bytes 1572872 | tf_op jit(solution)/shard_map/ppermute | solution.py:95
  175.3 23.9 %collective-permute-start.23 = (bf16[128,4096]{1,0:T(8,128)(2,1)S(1)}, bf16[128,4096]{1,0:T(8,128)(2,1)S(1)}, u32[]{:S(2)}, u32[]{:S(2)}) collective-permute-start(bf16[128,4096]{1,0:T(8,128)(2,1)S(1)} %slice.543), channel_id=1, source_target_pairs={{0,1},{1,0},{2,3},{3,2},{4,5},{5,4},{6,7},{7,6},{8,9},{9,8},{10,11... | collective-permute-start | bytes 3145736 | tf_op jit(solution)/shard_map/ppermute | solution.py:87
  186.7 18.5 %collective-permute-start.32 = (bf16[128,4096]{1,0:T(8,128)(2,1)S(1)}, bf16[128,4096]{1,0:T(8,128)(2,1)S(1)}, u32[]{:S(2)}, u32[]{:S(2)}) collective-permute-start(bf16[128,4096]{1,0:T(8,128)(2,1)S(1)} %pad_maximum_fusion.6), channel_id=1, source_target_pairs={{0,1},{1,0},{2,3},{3,2},{4,5},{5,4},{6,7},{7,6},{8,9},{9,8},{10,11... | collective-permute-start | bytes 3145736 | tf_op jit(solution)/shard_map/ppermute | solution.py:75
  188.5 12.9 %collective-permute-start.19 = (bf16[64,4096]{1,0:T(8,128)(2,1)S(1)}, bf16[64,4096]{1,0:T(8,128)(2,1)S(1)}, u32[]{:S(2)}, u32[]{:S(2)}) collective-permute-start(bf16[64,4096]{1,0:T(8,128)(2,1)S(1)} %get-tuple-element.16), channel_id=1, source_target_pairs={{0,4},{1,5},{2,0},{3,1},{4,8},{5,9},{6,2},{7,3},{8,12},{9,13},{10,... | collective-permute-start | bytes 1572872 | tf_op jit(solution)/shard_map/ppermute | solution.py:94
  190.3 6.9 %slice-start.5 = ((s8[6291456]{0:T(1024)(128)(4,1)}), s8[4194304]{0:T(1024)(128)(4,1)S(1)}, s32[]{:S(2)}) async-start(s8[6291456]{0:T(1024)(128)(4,1)} %bitcast.207), calls=%async_computation.5 | async-start | bytes 8388608
  190.3 6.9 %slice-start.6 = ((s8[6291456]{0:T(1024)(128)(4,1)}), s8[2097152]{0:T(1024)(128)(4,1)S(1)}, s32[]{:S(2)}) async-start(s8[6291456]{0:T(1024)(128)(4,1)} %bitcast.207), calls=%async_computation.6 | async-start | bytes 4194304
  190.3 12.6 %collective-permute-start.40 = (bf16[64,4096]{1,0:T(8,128)(2,1)S(1)}, bf16[64,4096]{1,0:T(8,128)(2,1)S(1)}, u32[]{:S(2)}, u32[]{:S(2)}) collective-permute-start(bf16[64,4096]{1,0:T(8,128)(2,1)S(1)} %get-tuple-element.17), channel_id=1, source_target_pairs={{0,2},{1,3},{2,6},{3,7},{4,0},{5,1},{6,10},{7,11},{8,4},{9,5},{10,... | collective-permute-start | bytes 1572872 | tf_op jit(solution)/shard_map/ppermute | solution.py:95
  199.2 14.6 %collective-permute-start.28 = (bf16[128,4096]{1,0:T(8,128)(2,1)S(1)}, bf16[128,4096]{1,0:T(8,128)(2,1)S(1)}, u32[]{:S(2)}, u32[]{:S(2)}) collective-permute-start(bf16[128,4096]{1,0:T(8,128)(2,1)S(1)} %slice.542), channel_id=1, source_target_pairs={{0,1},{1,0},{2,3},{3,2},{4,5},{5,4},{6,7},{7,6},{8,9},{9,8},{10,11... | collective-permute-start | bytes 3145736 | tf_op jit(solution)/shard_map/ppermute | solution.py:87
  203.1 12.0 %collective-permute-start.24 = (bf16[64,4096]{1,0:T(8,128)(2,1)S(1)}, bf16[64,4096]{1,0:T(8,128)(2,1)S(1)}, u32[]{:S(2)}, u32[]{:S(2)}) collective-permute-start(bf16[64,4096]{1,0:T(8,128)(2,1)S(1)} %get-tuple-element.14), channel_id=1, source_target_pairs={{0,4},{1,5},{2,0},{3,1},{4,8},{5,9},{6,2},{7,3},{8,12},{9,13},{10,... | collective-permute-start | bytes 1572872 | tf_op jit(solution)/shard_map/ppermute | solution.py:94
  204.9 12.5 %collective-permute-start.41 = (bf16[64,4096]{1,0:T(8,128)(2,1)S(1)}, bf16[64,4096]{1,0:T(8,128)(2,1)S(1)}, u32[]{:S(2)}, u32[]{:S(2)}) collective-permute-start(bf16[64,4096]{1,0:T(8,128)(2,1)S(1)} %get-tuple-element.15), channel_id=1, source_target_pairs={{0,2},{1,3},{2,6},{3,7},{4,0},{5,1},{6,10},{7,11},{8,4},{9,5},{10,... | collective-permute-start | bytes 1572872 | tf_op jit(solution)/shard_map/ppermute | solution.py:95
  213.7 5.9 %collective-permute-start.33 = (bf16[128,4096]{1,0:T(8,128)(2,1)S(1)}, bf16[128,4096]{1,0:T(8,128)(2,1)S(1)}, u32[]{:S(2)}, u32[]{:S(2)}) collective-permute-start(bf16[128,4096]{1,0:T(8,128)(2,1)S(1)} %slice.541), channel_id=1, source_target_pairs={{0,1},{1,0},{2,3},{3,2},{4,5},{5,4},{6,7},{7,6},{8,9},{9,8},{10,11... | collective-permute-start | bytes 3145736 | tf_op jit(solution)/shard_map/ppermute | solution.py:87
  217.5 11.6 %collective-permute-start.29 = (bf16[64,4096]{1,0:T(8,128)(2,1)S(1)}, bf16[64,4096]{1,0:T(8,128)(2,1)S(1)}, u32[]{:S(2)}, u32[]{:S(2)}) collective-permute-start(bf16[64,4096]{1,0:T(8,128)(2,1)S(1)} %get-tuple-element.12), channel_id=1, source_target_pairs={{0,4},{1,5},{2,0},{3,1},{4,8},{5,9},{6,2},{7,3},{8,12},{9,13},{10,... | collective-permute-start | bytes 1572872 | tf_op jit(solution)/shard_map/ppermute | solution.py:94
  218.8 11.8 %collective-permute-start.42 = (bf16[64,4096]{1,0:T(8,128)(2,1)S(1)}, bf16[64,4096]{1,0:T(8,128)(2,1)S(1)}, u32[]{:S(2)}, u32[]{:S(2)}) collective-permute-start(bf16[64,4096]{1,0:T(8,128)(2,1)S(1)} %get-tuple-element.13), channel_id=1, source_target_pairs={{0,2},{1,3},{2,6},{3,7},{4,0},{5,1},{6,10},{7,11},{8,4},{9,5},{10,... | collective-permute-start | bytes 1572872 | tf_op jit(solution)/shard_map/ppermute | solution.py:95
  230.8 10.9 %collective-permute-start.34 = (bf16[64,4096]{1,0:T(8,128)(2,1)S(1)}, bf16[64,4096]{1,0:T(8,128)(2,1)S(1)}, u32[]{:S(2)}, u32[]{:S(2)}) collective-permute-start(bf16[64,4096]{1,0:T(8,128)(2,1)S(1)} %get-tuple-element.10), channel_id=1, source_target_pairs={{0,4},{1,5},{2,0},{3,1},{4,8},{5,9},{6,2},{7,3},{8,12},{9,13},{10,... | collective-permute-start | bytes 1572872 | tf_op jit(solution)/shard_map/ppermute | solution.py:100
  231.7 10.8 %collective-permute-start.43 = (bf16[64,4096]{1,0:T(8,128)(2,1)S(1)}, bf16[64,4096]{1,0:T(8,128)(2,1)S(1)}, u32[]{:S(2)}, u32[]{:S(2)}) collective-permute-start(bf16[64,4096]{1,0:T(8,128)(2,1)S(1)} %get-tuple-element.11), channel_id=1, source_target_pairs={{0,2},{1,3},{2,6},{3,7},{4,0},{5,1},{6,10},{7,11},{8,4},{9,5},{10,... | collective-permute-start | bytes 1572872 | tf_op jit(solution)/shard_map/ppermute | solution.py:101

commit v2 on v0

--- a/solution.py
+++ b/solution.py
@@ -1,18 +1,13 @@
 import jax
 import jax.numpy as jnp
+import numpy as np
 from jax import lax
+from jax.experimental import pallas as pl
+from jax.experimental.pallas import tpu as pltpu
 from jax.sharding import PartitionSpec as P
 
-
-def prefix(part, axis, combine, identity):
-    place = lax.axis_index(axis)
-    gathered = lax.all_gather(part, axis)
-    state = jnp.zeros_like(part) + jnp.asarray(identity, part.dtype)
-
-    def one(turn, state):
-        return combine(state, lax.dynamic_index_in_dim(gathered, turn, 0, False))
-
-    return lax.fori_loop(0, place, one, state)
+AXIS = "expert"
+COST = pl.CostEstimate(flops=12_000_000_000, transcendentals=0, bytes_accessed=60_000_000)
 
 
 def expert_block(inputs, first_weights, second_weights):
@@ -24,12 +19,123 @@
     return jnp.dot(hidden, second_weights, preferred_element_type=jnp.float32).astype(jnp.bfloat16)
 
 
-def add_counts(earlier, later):
-    return earlier + later
+def incoming_gates(expert_ids, gate_weights, placement):
+    named = expert_ids.T[None] == placement[:, None, None]
+    outgoing = jnp.sum(jnp.where(named, gate_weights.T[None], 0.0), axis=1)
+    return lax.all_to_all(outgoing[:, None], AXIS, split_axis=0, concat_axis=0, tiled=True)[:, 0]
 
 
-def local(tokens, expert_ids, gate_weights, weights_in, weights_out, placement, capacity):
-    axis_len = lax.axis_size("expert")
+def table_kernel(limit, where, gate_ref, *refs):
+    gate = gate_ref[...]
+    devices, rows = gate.shape
+    hit = jnp.where(gate > 0, 1.0, 0.0).astype(jnp.bfloat16)
+    shape = (rows, rows)
+    lower = lax.broadcasted_iota(jnp.int32, shape, 0) < lax.broadcasted_iota(jnp.int32, shape, 1)
+    lower = jnp.where(lower, 1.0, 0.0).astype(jnp.bfloat16)
+    within = jnp.dot(hit, lower, preferred_element_type=jnp.float32)
+    shape = (devices, devices)
+    earlier = lax.broadcasted_iota(jnp.int32, shape, 1) < lax.broadcasted_iota(jnp.int32, shape, 0)
+    earlier = jnp.where(earlier, 1.0, 0.0).astype(jnp.bfloat16)
+    before = jnp.dot(earlier, hit, preferred_element_type=jnp.float32)
+    rank = within + jnp.sum(before, axis=1, keepdims=True)
+    table = jnp.where(rank < limit[0].astype(jnp.float32), gate, 0.0).T
+    out = refs[-1]
+    steps = out.shape[1]
+    half = rows // 2
+    column = lax.broadcasted_iota(jnp.int32, (half, devices), 1)
+    turn = lax.broadcasted_iota(jnp.int32, (half, steps), 1)
+    for index in range(4):
+        part = index % 2 * half
+        piece = table[part : part + half]
+        made = jnp.zeros((half, steps), jnp.float32)
+        for step in range(steps):
+            picked = jnp.sum(jnp.where(column == where[step, index], piece, 0.0), axis=1, keepdims=True)
+            made = jnp.where(turn == step, picked, made)
+        out[index * half : (index + 1) * half, :] = made
+
+
+def weight_table(gate, where, placement, capacity, gates):
+    expert = lax.dynamic_index_in_dim(placement, lax.axis_index(AXIS), 0, False)
+    limit = lax.dynamic_index_in_dim(capacity, expert, 0, True)
+    smem = pl.BlockSpec(memory_space=pltpu.SMEM)
+    hbm = pl.BlockSpec(memory_space=pl.ANY)
+    vmem = pl.BlockSpec(memory_space=pltpu.VMEM)
+    return pl.pallas_call(
+        table_kernel,
+        out_shape=jax.ShapeDtypeStruct((2 * gate.shape[1], where.shape[0]), jnp.float32),
+        in_specs=[smem, smem, vmem] + [hbm] * len(gates),
+        out_specs=vmem,
+        cost_estimate=COST,
+    )(limit, where, gate, *gates)
+
+
+def ring_form(tokens, expert_ids, gate_weights, weights_in, weights_out, placement, capacity):
+    axis_len = lax.axis_size(AXIS)
+    rows = tokens.shape[0]
+    half = rows // 2
+    chips = axis_len // 2
+    side = chips // 2
+
+    def chip_at(spot):
+        return 2 * spot if spot < side else 2 * (chips - 1 - spot) + 1
+
+    spot_of = {chip_at(spot): spot for spot in range(chips)}
+
+    def along(step):
+        return [(d, 2 * chip_at((spot_of[d // 2] + step) % chips) + d % 2) for d in range(axis_len)]
+
+    forth, back = along(1), along(-1)
+    swap = [(d, d ^ 1) for d in range(axis_len)]
+
+    def send(value, where, name):
+        with jax.named_scope(name):
+            return lax.ppermute(value, AXIS, where)
+
+    owners = np.zeros((axis_len, chips, 4), np.int32)
+    for d in range(axis_len):
+        for step in range(chips):
+            for index, (way, core) in enumerate([(-1, 0), (1, 0), (-1, 1), (1, 1)]):
+                owners[d, step, index] = 2 * chip_at((spot_of[d // 2] + way * step) % chips) + (d + core) % 2
+    where = lax.dynamic_index_in_dim(jnp.asarray(owners), lax.axis_index(AXIS), 0, False)
+    first_weights, second_weights = weights_in[0], weights_out[0]
+
+    aheads, behinds = [tokens[:half]], [tokens[half:]]
+    for step in range(1, chips):
+        aheads.append(send(aheads[-1], forth, f"ag{step}a"))
+        behinds.append(send(behinds[-1], back, f"ag{step}b"))
+    with jax.named_scope("meta"):
+        gate = incoming_gates(expert_ids, gate_weights, placement)
+        scales = weight_table(gate, where, placement, capacity, (aheads[1], behinds[1]))
+    sums_a = sums_b = None
+    for turn in range(1, chips + 1):
+        step = turn % chips
+        pieces = [aheads[step], behinds[step]]
+        pieces += [send(pieces[0], swap, f"xs{step}a"), send(pieces[1], swap, f"xs{step}b")]
+        with jax.named_scope(f"kernel{step}"):
+            outs = expert_block(jnp.concatenate(pieces, axis=0), first_weights, second_weights)
+            outs = outs.astype(jnp.float32) * scales[:, step : step + 1]
+            kept, other = outs[:rows], outs[rows:].astype(jnp.bfloat16)
+        from_other = send(other, swap, f"ps{step}")
+        with jax.named_scope(f"add{step}"):
+            part = kept + from_other.astype(jnp.float32)
+            part_a, part_b = part[:half], part[half:]
+        if turn != 1:
+            sums_a, sums_b = send(sums_a, forth, f"rs{step}a"), send(sums_b, back, f"rs{step}b")
+            with jax.named_scope(f"add{step}"):
+                part_a, part_b = part_a + sums_a.astype(jnp.float32), part_b + sums_b.astype(jnp.float32)
+        with jax.named_scope(f"add{step}"):
+            sums_a, sums_b = part_a.astype(jnp.bfloat16), part_b.astype(jnp.bfloat16)
+    return jnp.concatenate([sums_a, sums_b], axis=0)
+
+
+def prefix(part):
+    gathered = lax.all_gather(part, AXIS)
+    earlier = jnp.arange(gathered.shape[0]) < lax.axis_index(AXIS)
+    return jnp.sum(jnp.where(earlier[:, None], gathered, 0), axis=0)
+
+
+def exchange_form(tokens, expert_ids, gate_weights, weights_in, weights_out, placement, capacity):
+    axis_len = lax.axis_size(AXIS)
     tok_rows, top_len = expert_ids.shape
     feat_len = tokens.shape[1]
     slot_len = tok_rows * top_len * 9 // (8 * axis_len)
@@ -40,7 +146,7 @@
     before = jnp.cumsum(onehot, axis=0) - onehot
     local_rank = jnp.sum(before * onehot, axis=1)
     counts = jnp.sum(onehot, axis=0)
-    offset = prefix(counts, "expert", add_counts, jnp.zeros_like(counts))
+    offset = prefix(counts)
     row_offset = jnp.sum(onehot * offset[None, :], axis=1)
     row_cap = jnp.sum(onehot * capacity[None, :], axis=1)
     row_dest = jnp.sum(onehot * dev_of[None, :], axis=1)
@@ -50,13 +156,13 @@
     owner = jnp.full((axis_len * slot_len,), tok_rows, jnp.int32).at[flat_slot].set(row_token)
     padded_tokens = jnp.concatenate([tokens, jnp.zeros((1, feat_len), jnp.bfloat16)], axis=0)
     outgoing = padded_tokens[owner].reshape(axis_len, slot_len, feat_len)
-    arrived = lax.all_to_all(outgoing, "expert", split_axis=0, concat_axis=0, tiled=True)
+    arrived = lax.all_to_all(outgoing, AXIS, split_axis=0, concat_axis=0, tiled=True)
     items = arrived.shape[1]
     result_rows = expert_block(
         arrived.reshape(axis_len * items, feat_len), weights_in[0], weights_out[0]
     )
     result_rows = result_rows.reshape(axis_len, items, feat_len)
-    returned = lax.all_to_all(result_rows, "expert", split_axis=0, concat_axis=0, tiled=True)
+    returned = lax.all_to_all(result_rows, AXIS, split_axis=0, concat_axis=0, tiled=True)
     picked = returned.reshape(axis_len * slot_len, feat_len)[flat_slot]
     row_weight = jnp.where(kept, gate_weights.reshape(-1), jnp.float32(0.0))
     combined = jnp.sum(
@@ -64,6 +170,12 @@
         axis=1,
     )
     return combined.astype(jnp.bfloat16)
+
+
+def local(*args):
+    axis_len, top_len = lax.axis_size(AXIS), args[1].shape[1]
+    dense = axis_len <= 2 * top_len and axis_len % 4 == 0
+    return ring_form(*args) if dense else exchange_form(*args)
 
 
 def solution(mesh):

time: 516 us -> 208 us (0.40)
  the two profiles are of different devices: /device:TPU:15 before, /device:TPU:0 now
where the time goes in v2:
time: 208 us
  waiting for transfers between devices  83.8 us (40%)
  matrix products  67.9 us (33%)
  starting transfers between devices  36.6 us (18%)
  local copies, waits for them, and re-layouts  8.93 us (4%)
  other arithmetic  5.52 us (3%)
  Pallas kernels  2.65 us (1%)
  between operations  2.52 us (1%)
    ppermute x52, waiting for transfers between devices, send(): return lax.ppermute(value, AXIS, where)  83.8 us
    dot_general x8, matrix products, expert_block(): jnp.dot(inputs, first_weights, preferred_element_type=jnp.float32)  52.7 us
    ppermute x52, starting transfers between devices, send(): return lax.ppermute(value, AXIS, where)  30.3 us
    dot_general x8, matrix products, expert_block(): jnp.dot(hidden, second_weights, preferred_element_type=jnp.float32)  15.2 us
    all_to_all x1, starting transfers between devices, incoming_gates(): lax.all_to_all(outgoing[:, None], AXIS, split_axis=0, concat_axis=0, tile...  6.38 us
  transfers between devices with their start and end apart: 53, of which 25 were waited for; matrix products, arithmetic and copies ran while one was open for 38% of the time, Pallas kernels for 1%

profile of v2, /device:TPU:0, one launch (start us, length us, event | category | flops | bytes accessed | tf_op | source)
XLA Modules:
  0.0 207.9 jit_solution(11995710269561697852)
XLA Ops:
  0.0 1.3 fusion.222
  1.3 3.1 %collective-permute-start.2 = (bf16[64,4096]{1,0:T(8,128)(2,1)S(1)}, bf16[64,4096]{1,0:T(8,128)(2,1)S(1)}, u32[]{:S(2)}, u32[]{:S(2)}) collective-permute-start(bf16[64,4096]{1,0:T(8,128)(2,1)S(1)} %get-tuple-element.30), channel_id=1, source_target_pairs={{0,4},{1,5},{2,0},{3,1},{4,8},{5,9},{6,2},{7,3},{8,12},{9,13},{10,... | collective-permute-start | bytes 1572872 | tf_op jit(solution)/shard_map/ag1a/ppermute | solution.py:92
  4.9 1.4 select_reduce_fusion
  6.3 6.4 %all-to-all-start = ((f32[16,1,128]{2,1,0:T(1,128)}), f32[16,1,128]{2,1,0:T(1,128)S(1)}, u32[]{:S(2)}, u32[]{:S(2)}) async-start(f32[16,1,128]{2,1,0:T(1,128)} %bitcast.7), calls=%async_computation | async-start | bytes 16384 | tf_op jit(solution)/shard_map/meta/all_to_all | solution.py:25
  12.7 0.7 dynamic-slice_bitcast_fusion
  13.3 1.2 dynamic_slice.12
  15.9 0.7 copy.13.where
  17.2 1.2 dynamic_slice.13.limit
  18.4 1.9 collective-permute-start.5
  21.2 2.7 %meta.1 = f32[256,8]{1,0:T(8,128)} custom-call(s32[1]{0:T(128)} %dynamic_slice.13.limit, s32[8,4]{1,0:T(8,128)} %copy.13.where, f32[16,128]{1,0:T(8,128)} %bitcast.91, bf16[64,4096]{1,0:T(8,128)(2,1)} %copy-done.2, bf16[64,4096]{1,0:T(8,128)(2,1)} %collective-permute-done.3.refs_1_), custom_call_target="tpu_custom_call" | custom-call | flops 12000000000 | bytes 60000000 | tf_op jit(solution)/shard_map/meta/pallas_call | solution.py:63
  23.9 2.2 %slice_reduce_fusion = (f32[256]{0:T(256)S(1)}, f32[256]{0:T(256)S(1)}, f32[256]{0:T(256)S(1)}, f32[256]{0:T(256)S(1)}, f32[256]{0:T(256)S(1)}, /*index=5*/f32[256]{0:T(256)S(1)}, f32[256]{0:T(256)S(1)}, f32[256]{0:T(256)S(1)}) fusion(f32[256,8]{1,0:T(8,128)} %meta.1), kind=kLoop, calls=%fused_computation.180 | loop fusion | bytes 16384 | tf_op jit(solution)/shard_map/kernel1/slice | solution.py:116
  26.4 6.9 %fusion.14 = f32[256,1536]{1,0:T(8,128)S(1)} fusion(bf16[1,4096,1536]{2,1,0:T(8,128)(2,1)} %param.11, bf16[64,4096]{1,0:T(8,128)(2,1)} %collective-permute-done.1, bf16[64,4096]{1,0:T(8,128)(2,1)} %collective-permute-done, bf16[128,4096]{1,0:T(8,128)(2,1)S(1)} %copy-done), kind=kOutput, calls=%fused_computation.14 | convolution fusion | flops 3227516928 | bytes 16252928 | tf_op jit(solution)/shard_map/kernel0/dot_general | solution.py:15
  33.3 1.9 broadcast_multiply_fusion.7
  36.2 6.8 %fusion = f32[256,1536]{1,0:T(8,128)S(1)} fusion(bf16[1,4096,1536]{2,1,0:T(8,128)(2,1)} %param.11, bf16[64,4096]{1,0:T(8,128)(2,1)S(1)} %collective-permute-done.36, bf16[64,4096]{1,0:T(8,128)(2,1)} %collective-permute-done.35, bf16[64,4096]{1,0:T(8,128)(2,1)} %collective-permute-done.3.refs_1_, bf16[64,4096]{1,0:T(8,128)(2,1)S(1)} %copy-done.3), kind=kOutput, calls=%fused_computation | convolution fusion | flops 3229614080 | bytes 16252928 | tf_op jit(solution)/shard_map/kernel1/dot_general | solution.py:15
  43.0 1.9 broadcast_multiply_fusion
  45.4 1.7 collective-permute-start.6
  47.4 6.6 %fusion.2 = f32[256,1536]{1,0:T(8,128)S(1)} fusion(bf16[1,4096,1536]{2,1,0:T(8,128)(2,1)} %param.11, bf16[64,4096]{1,0:T(8,128)(2,1)S(1)} %collective-permute-done.33, bf16[64,4096]{1,0:T(8,128)(2,1)S(1)} %collective-permute-done.32, bf16[64,4096]{1,0:T(8,128)(2,1)} %collective-permute-done.11, bf16[64,4096]{1,0:T(8,128)(2,1)S(1)} %collective-permute-done.5), kind=kOutput, calls=%fused_computation.2 | convolution fusion | flops 3229614080 | bytes 16252928 | tf_op jit(solution)/shard_map/kernel2/dot_general | solution.py:15
  54.0 1.9 broadcast_multiply_fusion.1
  56.2 3.3 %collective-permute-done.6 = bf16[64,4096]{1,0:T(8,128)(2,1)S(1)} collective-permute-done((bf16[64,4096]{1,0:T(8,128)(2,1)S(1)}, bf16[64,4096]{1,0:T(8,128)(2,1)S(1)}, u32[]{:S(2)}, u32[]{:S(2)}) %collective-permute-start.6) | collective-permute-done | bytes 524320 | tf_op jit(solution)/shard_map/ag3a/ppermute | solution.py:92
  59.5 1.7 collective-permute-done.12
  61.2 1.5 collective-permute-start.7
  63.6 1.0 collective-permute-done.30
  64.6 1.5 collective-permute-start.38
  66.0 6.5 %fusion.4 = f32[256,1536]{1,0:T(8,128)S(1)} fusion(bf16[1,4096,1536]{2,1,0:T(8,128)(2,1)} %param.11, bf16[64,4096]{1,0:T(8,128)(2,1)S(1)} %collective-permute-done.30, bf16[64,4096]{1,0:T(8,128)(2,1)S(1)} %collective-permute-done.29, bf16[64,4096]{1,0:T(8,128)(2,1)S(1)} %collective-permute-done.12, bf16[64,4096]{1,0:T(8,128)(2,1)S(1)} %collective-permute-done.6), kind=kOutput, calls=%fused_computation.4 | convolution fusion | flops 3229614080 | bytes 16252928 | tf_op jit(solution)/shard_map/kernel3/dot_general | solution.py:15
  72.5 1.9 broadcast_multiply_fusion.2
  74.6 0.6 collective-permute-start.45
  76.0 1.6 collective-permute-done.13
  77.6 7.8 %collective-permute-done.38 = bf16[64,4096]{1,0:T(8,128)(2,1)S(1)} collective-permute-done((bf16[64,4096]{1,0:T(8,128)(2,1)S(1)}, bf16[64,4096]{1,0:T(8,128)(2,1)S(1)}, u32[]{:S(2)}, u32[]{:S(2)}) %collective-permute-start.38) | collective-permute-done | bytes 524320 | tf_op jit(solution)/shard_map/rs2a/ppermute | solution.py:92
  85.4 1.5 collective-permute-start.8
  86.9 1.7 collective-permute-done.45
  89.4 1.1 collective-permute-done.27
  90.5 1.5 collective-permute-start.39
  92.0 6.5 %fusion.6 = f32[256,1536]{1,0:T(8,128)S(1)} fusion(bf16[1,4096,1536]{2,1,0:T(8,128)(2,1)} %param.11, bf16[64,4096]{1,0:T(8,128)(2,1)S(1)} %collective-permute-done.27, bf16[64,4096]{1,0:T(8,128)(2,1)S(1)} %collective-permute-done.26, bf16[64,4096]{1,0:T(8,128)(2,1)S(1)} %collective-permute-done.13, bf16[64,4096]{1,0:T(8,128)(2,1)S(1)} %collective-permute-done.7), kind=kOutput, calls=%fused_computation.6 | convolution fusion | flops 3229614080 | bytes 16252928 | tf_op jit(solution)/shard_map/kernel4/dot_general | solution.py:15
  98.5 1.9 broadcast_multiply_fusion.3
  101.4 1.9 collective-permute-done.14
  103.3 6.3 %collective-permute-done.39 = bf16[64,4096]{1,0:T(8,128)(2,1)S(1)} collective-permute-done((bf16[64,4096]{1,0:T(8,128)(2,1)S(1)}, bf16[64,4096]{1,0:T(8,128)(2,1)S(1)}, u32[]{:S(2)}, u32[]{:S(2)}) %collective-permute-start.39) | collective-permute-done | bytes 524320 | tf_op jit(solution)/shard_map/rs3a/ppermute | solution.py:92
  109.6 0.7 collective-permute-start.9
  110.2 4.2 %collective-permute-done.46 = bf16[64,4096]{1,0:T(8,128)(2,1)S(1)} collective-permute-done((bf16[64,4096]{1,0:T(8,128)(2,1)S(1)}, bf16[64,4096]{1,0:T(8,128)(2,1)S(1)}, u32[]{:S(2)}, u32[]{:S(2)}) %collective-permute-start.46) | collective-permute-done | bytes 524320 | tf_op jit(solution)/shard_map/rs3b/ppermute | solution.py:92
  115.3 1.1 collective-permute-done.24
  116.4 1.5 collective-permute-start.40
  117.8 6.5 %fusion.8 = f32[256,1536]{1,0:T(8,128)S(1)} fusion(bf16[1,4096,1536]{2,1,0:T(8,128)(2,1)} %param.11, bf16[64,4096]{1,0:T(8,128)(2,1)S(1)} %collective-permute-done.24, bf16[64,4096]{1,0:T(8,128)(2,1)S(1)} %collective-permute-done.23, bf16[64,4096]{1,0:T(8,128)(2,1)S(1)} %collective-permute-done.14, bf16[64,4096]{1,0:T(8,128)(2,1)S(1)} %collective-permute-done.8), kind=kOutput, calls=%fused_computation.8 | convolution fusion | flops 3229614080 | bytes 16252928 | tf_op jit(solution)/shard_map/kernel5/dot_general | solution.py:15
  124.3 1.9 broadcast_multiply_fusion.4
  127.3 1.9 collective-permute-done.15
  129.2 4.0 %collective-permute-done.40 = bf16[64,4096]{1,0:T(8,128)(2,1)S(1)} collective-permute-done((bf16[64,4096]{1,0:T(8,128)(2,1)S(1)}, bf16[64,4096]{1,0:T(8,128)(2,1)S(1)}, u32[]{:S(2)}, u32[]{:S(2)}) %collective-permute-start.40) | collective-permute-done | bytes 524320 | tf_op jit(solution)/shard_map/rs4a/ppermute | solution.py:92
  133.2 7.1 %collective-permute-done.47 = bf16[64,4096]{1,0:T(8,128)(2,1)S(1)} collective-permute-done((bf16[64,4096]{1,0:T(8,128)(2,1)S(1)}, bf16[64,4096]{1,0:T(8,128)(2,1)S(1)}, u32[]{:S(2)}, u32[]{:S(2)}) %collective-permute-start.47) | collective-permute-done | bytes 524320 | tf_op jit(solution)/shard_map/rs4b/ppermute | solution.py:92
  141.1 1.1 collective-permute-done.21
  142.2 1.5 collective-permute-start.41
  143.7 6.5 %fusion.10 = f32[256,1536]{1,0:T(8,128)S(1)} fusion(bf16[1,4096,1536]{2,1,0:T(8,128)(2,1)} %param.11, bf16[64,4096]{1,0:T(8,128)(2,1)S(1)} %collective-permute-done.21, bf16[64,4096]{1,0:T(8,128)(2,1)S(1)} %collective-permute-done.20, bf16[64,4096]{1,0:T(8,128)(2,1)S(1)} %collective-permute-done.15, bf16[64,4096]{1,0:T(8,128)(2,1)S(1)} %collective-permute-done.9), kind=kOutput, calls=%fused_computation.10 | convolution fusion | flops 3229614080 | bytes 16252928 | tf_op jit(solution)/shard_map/kernel6/dot_general | solution.py:15
  150.2 1.9 broadcast_multiply_fusion.5
  153.1 1.9 collective-permute-done.16
  155.0 1.2 collective-permute-done.41
  156.2 10.0 %collective-permute-done.48 = bf16[64,4096]{1,0:T(8,128)(2,1)S(1)} collective-permute-done((bf16[64,4096]{1,0:T(8,128)(2,1)S(1)}, bf16[64,4096]{1,0:T(8,128)(2,1)S(1)}, u32[]{:S(2)}, u32[]{:S(2)}) %collective-permute-start.48) | collective-permute-done | bytes 524320 | tf_op jit(solution)/shard_map/rs5b/ppermute | solution.py:92
  166.3 1.5 collective-permute-start.42
  168.4 6.5 %fusion.12 = f32[256,1536]{1,0:T(8,128)S(1)} fusion(bf16[1,4096,1536]{2,1,0:T(8,128)(2,1)} %param.11, bf16[64,4096]{1,0:T(8,128)(2,1)S(1)} %collective-permute-done.18, bf16[64,4096]{1,0:T(8,128)(2,1)S(1)} %collective-permute-done.17, bf16[64,4096]{1,0:T(8,128)(2,1)S(1)} %collective-permute-done.16, bf16[64,4096]{1,0:T(8,128)(2,1)S(1)} %collective-permute-done.10), kind=kOutput, calls=%fused_computation.12 | convolution fusion | flops 3229614080 | bytes 16252928 | tf_op jit(solution)/shard_map/kernel7/dot_general | solution.py:15
  174.9 1.9 broadcast_multiply_fusion.6
  177.3 2.1 %collective-permute-done.42 = bf16[64,4096]{1,0:T(8,128)(2,1)S(1)} collective-permute-done((bf16[64,4096]{1,0:T(8,128)(2,1)S(1)}, bf16[64,4096]{1,0:T(8,128)(2,1)S(1)}, u32[]{:S(2)}, u32[]{:S(2)}) %collective-permute-start.42) | collective-permute-done | bytes 524320 | tf_op jit(solution)/shard_map/rs6a/ppermute | solution.py:92
  179.4 1.5 collective-permute-done.49
  181.1 1.8 collective-permute-start.43
  183.4 9.8 %collective-permute-done.43 = bf16[64,4096]{1,0:T(8,128)(2,1)S(1)} collective-permute-done((bf16[64,4096]{1,0:T(8,128)(2,1)S(1)}, bf16[64,4096]{1,0:T(8,128)(2,1)S(1)}, u32[]{:S(2)}, u32[]{:S(2)}) %collective-permute-start.43) | collective-permute-done | bytes 524320 | tf_op jit(solution)/shard_map/rs7a/ppermute | solution.py:92
  193.2 1.7 collective-permute-done.50
  195.1 0.6 collective-permute-start.44
  195.8 1.4 collective-permute-start.51
  197.5 8.9 %collective-permute-done.44 = bf16[64,4096]{1,0:T(8,128)(2,1)S(1)} collective-permute-done((bf16[64,4096]{1,0:T(8,128)(2,1)S(1)}, bf16[64,4096]{1,0:T(8,128)(2,1)S(1)}, u32[]{:S(2)}, u32[]{:S(2)}) %collective-permute-start.44) | collective-permute-done | bytes 524320 | tf_op jit(solution)/shard_map/rs0a/ppermute | solution.py:92
  206.9 1.0 pad_maximum_fusion
  (104 shorter events, 13.9 us)
Async XLA Ops:
  1.3 17.2 %collective-permute-start.2 = (bf16[64,4096]{1,0:T(8,128)(2,1)S(1)}, bf16[64,4096]{1,0:T(8,128)(2,1)S(1)}, u32[]{:S(2)}, u32[]{:S(2)}) collective-permute-start(bf16[64,4096]{1,0:T(8,128)(2,1)S(1)} %get-tuple-element.30), channel_id=1, source_target_pairs={{0,4},{1,5},{2,0},{3,1},{4,8},{5,9},{6,2},{7,3},{8,12},{9,13},{10,... | collective-permute-start | bytes 1572872 | tf_op jit(solution)/shard_map/ag1a/ppermute | solution.py:92
  4.3 16.0 %collective-permute-start.3 = (bf16[64,4096]{1,0:T(8,128)(2,1)S(1)}, bf16[64,4096]{1,0:T(8,128)(2,1)}, u32[]{:S(2)}, u32[]{:S(2)}) collective-permute-start(bf16[64,4096]{1,0:T(8,128)(2,1)S(1)} %get-tuple-element.29), channel_id=1, source_target_pairs={{0,2},{1,3},{2,6},{3,7},{4,0},{5,1},{6,10},{7,11},{8,4},{9,5},{10,... | collective-permute-start | bytes 1572872 | tf_op jit(solution)/shard_map/ag1b/ppermute | solution.py:92
  4.4 21.7 %collective-permute-start = (bf16[64,4096]{1,0:T(8,128)(2,1)S(1)}, bf16[64,4096]{1,0:T(8,128)(2,1)}, u32[]{:S(2)}, u32[]{:S(2)}) collective-permute-start(bf16[64,4096]{1,0:T(8,128)(2,1)S(1)} %get-tuple-element.30), channel_id=1, source_target_pairs={{0,1},{1,0},{2,3},{3,2},{4,5},{5,4},{6,7},{7,6},{8,9},{9,8},{10,11... | collective-permute-start | bytes 1572872 | tf_op jit(solution)/shard_map/xs0a/ppermute | solution.py:92
  4.4 22.0 %collective-permute-start.1 = (bf16[64,4096]{1,0:T(8,128)(2,1)S(1)}, bf16[64,4096]{1,0:T(8,128)(2,1)}, u32[]{:S(2)}, u32[]{:S(2)}) collective-permute-start(bf16[64,4096]{1,0:T(8,128)(2,1)S(1)} %get-tuple-element.29), channel_id=1, source_target_pairs={{0,1},{1,0},{2,3},{3,2},{4,5},{5,4},{6,7},{7,6},{8,9},{9,8},{10,11... | collective-permute-start | bytes 1572872 | tf_op jit(solution)/shard_map/xs0b/ppermute | solution.py:92
  6.3 14.4 %all-to-all-start = ((f32[16,1,128]{2,1,0:T(1,128)}), f32[16,1,128]{2,1,0:T(1,128)S(1)}, u32[]{:S(2)}, u32[]{:S(2)}) async-start(f32[16,1,128]{2,1,0:T(1,128)} %bitcast.7), calls=%async_computation | async-start | bytes 16384 | tf_op jit(solution)/shard_map/meta/all_to_all | solution.py:25
  18.4 2.2 %copy-start.2 = (bf16[64,4096]{1,0:T(8,128)(2,1)}, bf16[64,4096]{1,0:T(8,128)(2,1)S(1)}, u32[]{:S(2)}) copy-start(bf16[64,4096]{1,0:T(8,128)(2,1)S(1)} %collective-permute-done.2.refs_0_) | copy-start | bytes 1572868
  18.4 17.3 %collective-permute-start.5 = (bf16[64,4096]{1,0:T(8,128)(2,1)S(1)}, bf16[64,4096]{1,0:T(8,128)(2,1)S(1)}, u32[]{:S(2)}, u32[]{:S(2)}) collective-permute-start(bf16[64,4096]{1,0:T(8,128)(2,1)S(1)} %collective-permute-done.2.refs_0_), channel_id=1, source_target_pairs={{0,4},{1,5},{2,0},{3,1},{4,8},{5,9},{6,2},{7,3},{8,12},{9,13},{10,... | collective-permute-start | bytes 1572872 | tf_op jit(solution)/shard_map/ag2a/ppermute | solution.py:92
  20.4 15.9 %collective-permute-start.35 = (bf16[64,4096]{1,0:T(8,128)(2,1)S(1)}, bf16[64,4096]{1,0:T(8,128)(2,1)}, u32[]{:S(2)}, u32[]{:S(2)}) collective-permute-start(bf16[64,4096]{1,0:T(8,128)(2,1)S(1)} %collective-permute-done.2.refs_0_), channel_id=1, source_target_pairs={{0,1},{1,0},{2,3},{3,2},{4,5},{5,4},{6,7},{7,6},{8,9},{9,8},{10,11... | collective-permute-start | bytes 1572872 | tf_op jit(solution)/shard_map/xs1a/ppermute | solution.py:92
  20.4 15.6 %collective-permute-start.11 = (bf16[64,4096]{1,0:T(8,128)(2,1)}, bf16[64,4096]{1,0:T(8,128)(2,1)}, u32[]{:S(2)}, u32[]{:S(2)}) collective-permute-start(bf16[64,4096]{1,0:T(8,128)(2,1)} %collective-permute-done.3.refs_1_), channel_id=1, source_target_pairs={{0,2},{1,3},{2,6},{3,7},{4,0},{5,1},{6,10},{7,11},{8,4},{9,5},{10,... | collective-permute-start | bytes 1572872 | tf_op jit(solution)/shard_map/ag2b/ppermute | solution.py:92
  20.6 0.6 copy-start.1
  21.2 5.2 %copy-start = (bf16[128,4096]{1,0:T(8,128)(2,1)S(1)}, bf16[128,4096]{1,0:T(8,128)(2,1)}, u32[]{:S(2)}) copy-start(bf16[128,4096]{1,0:T(8,128)(2,1)} %param.8) | copy-start | bytes 3145732
  23.9 9.4 %slice-start = ((s8[6291456]{0:T(1024)(128)(4,1)}), s8[4194304]{0:T(1024)(128)(4,1)S(1)}, s32[]{:S(2)}) async-start(s8[6291456]{0:T(1024)(128)(4,1)} %bitcast.94), calls=%async_computation.1 | async-start | bytes 8388608
  26.1 7.2 %slice-start.1 = ((s8[6291456]{0:T(1024)(128)(4,1)}), s8[2097152]{0:T(1024)(128)(4,1)S(1)}, s32[]{:S(2)}) async-start(s8[6291456]{0:T(1024)(128)(4,1)} %bitcast.94), calls=%async_computation.2 | async-start | bytes 4194304
  26.1 10.1 %collective-permute-start.36 = (bf16[64,4096]{1,0:T(8,128)(2,1)}, bf16[64,4096]{1,0:T(8,128)(2,1)S(1)}, u32[]{:S(2)}, u32[]{:S(2)}) collective-permute-start(bf16[64,4096]{1,0:T(8,128)(2,1)} %collective-permute-done.3.refs_1_), channel_id=1, source_target_pairs={{0,1},{1,0},{2,3},{3,2},{4,5},{5,4},{6,7},{7,6},{8,9},{9,8},{10,11... | collective-permute-start | bytes 1572872 | tf_op jit(solution)/shard_map/xs1b/ppermute | solution.py:92
  33.3 2.9 %copy-start.3 = (bf16[64,4096]{1,0:T(8,128)(2,1)S(1)}, bf16[64,4096]{1,0:T(8,128)(2,1)}, u32[]{:S(2)}) copy-start(bf16[64,4096]{1,0:T(8,128)(2,1)} %copy-done.2) | copy-start | bytes 1572868
  35.3 161.9 %collective-permute-start.4 = (bf16[128,4096]{1,0:T(8,128)(2,1)S(1)}, bf16[128,4096]{1,0:T(8,128)(2,1)S(1)}, u32[]{:S(2)}, u32[]{:S(2)}) collective-permute-start(bf16[128,4096]{1,0:T(8,128)(2,1)S(1)} %slice.454), channel_id=1, source_target_pairs={{0,1},{1,0},{2,3},{3,2},{4,5},{5,4},{6,7},{7,6},{8,9},{9,8},{10,11... | collective-permute-start | bytes 3145736 | tf_op jit(solution)/shard_map/ps0/ppermute | solution.py:92
  35.7 11.4 %collective-permute-start.32 = (bf16[64,4096]{1,0:T(8,128)(2,1)S(1)}, bf16[64,4096]{1,0:T(8,128)(2,1)S(1)}, u32[]{:S(2)}, u32[]{:S(2)}) collective-permute-start(bf16[64,4096]{1,0:T(8,128)(2,1)S(1)} %collective-permute-done.5), channel_id=1, source_target_pairs={{0,1},{1,0},{2,3},{3,2},{4,5},{5,4},{6,7},{7,6},{8,9},{9,8},{10,11... | collective-permute-start | bytes 1572872 | tf_op jit(solution)/shard_map/xs2a/ppermute | solution.py:92
  35.9 11.5 %collective-permute-start.33 = (bf16[64,4096]{1,0:T(8,128)(2,1)}, bf16[64,4096]{1,0:T(8,128)(2,1)S(1)}, u32[]{:S(2)}, u32[]{:S(2)}) collective-permute-start(bf16[64,4096]{1,0:T(8,128)(2,1)} %collective-permute-done.11), channel_id=1, source_target_pairs={{0,1},{1,0},{2,3},{3,2},{4,5},{5,4},{6,7},{7,6},{8,9},{9,8},{10,11... | collective-permute-start | bytes 1572872 | tf_op jit(solution)/shard_map/xs2b/ppermute | solution.py:92
  45.1 17.6 %collective-permute-start.37 = (bf16[128,4096]{1,0:T(8,128)(2,1)S(1)}, bf16[128,4096]{1,0:T(8,128)(2,1)S(1)}, u32[]{:S(2)}, u32[]{:S(2)}) collective-permute-start(bf16[128,4096]{1,0:T(8,128)(2,1)S(1)} %slice.447), channel_id=1, source_target_pairs={{0,1},{1,0},{2,3},{3,2},{4,5},{5,4},{6,7},{7,6},{8,9},{9,8},{10,11... | collective-permute-start | bytes 3145736 | tf_op jit(solution)/shard_map/ps1/ppermute | solution.py:92
  45.4 14.1 %collective-permute-start.6 = (bf16[64,4096]{1,0:T(8,128)(2,1)S(1)}, bf16[64,4096]{1,0:T(8,128)(2,1)S(1)}, u32[]{:S(2)}, u32[]{:S(2)}) collective-permute-start(bf16[64,4096]{1,0:T(8,128)(2,1)S(1)} %collective-permute-done.5), channel_id=1, source_target_pairs={{0,4},{1,5},{2,0},{3,1},{4,8},{5,9},{6,2},{7,3},{8,12},{9,13},{10,... | collective-permute-start | bytes 1572872 | tf_op jit(solution)/shard_map/ag3a/ppermute | solution.py:92
  47.1 14.1 %collective-permute-start.12 = (bf16[64,4096]{1,0:T(8,128)(2,1)}, bf16[64,4096]{1,0:T(8,128)(2,1)S(1)}, u32[]{:S(2)}, u32[]{:S(2)}) collective-permute-start(bf16[64,4096]{1,0:T(8,128)(2,1)} %collective-permute-done.11), channel_id=1, source_target_pairs={{0,2},{1,3},{2,6},{3,7},{4,0},{5,1},{6,10},{7,11},{8,4},{9,5},{10,... | collective-permute-start | bytes 1572872 | tf_op jit(solution)/shard_map/ag3b/ppermute | solution.py:92
  56.1 18.5 %collective-permute-start.34 = (bf16[128,4096]{1,0:T(8,128)(2,1)S(1)}, bf16[128,4096]{1,0:T(8,128)(2,1)S(1)}, u32[]{:S(2)}, u32[]{:S(2)}) collective-permute-start(bf16[128,4096]{1,0:T(8,128)(2,1)S(1)} %slice.448), channel_id=1, source_target_pairs={{0,1},{1,0},{2,3},{3,2},{4,5},{5,4},{6,7},{7,6},{8,9},{9,8},{10,11... | collective-permute-start | bytes 3145736 | tf_op jit(solution)/shard_map/ps2/ppermute | solution.py:92
  59.5 3.5 %collective-permute-start.29 = (bf16[64,4096]{1,0:T(8,128)(2,1)S(1)}, bf16[64,4096]{1,0:T(8,128)(2,1)S(1)}, u32[]{:S(2)}, u32[]{:S(2)}) collective-permute-start(bf16[64,4096]{1,0:T(8,128)(2,1)S(1)} %collective-permute-done.6), channel_id=1, source_target_pairs={{0,1},{1,0},{2,3},{3,2},{4,5},{5,4},{6,7},{7,6},{8,9},{9,8},{10,11... | collective-permute-start | bytes 1572872 | tf_op jit(solution)/shard_map/xs3a/ppermute | solution.py:92
  61.2 14.9 %collective-permute-start.7 = (bf16[64,4096]{1,0:T(8,128)(2,1)S(1)}, bf16[64,4096]{1,0:T(8,128)(2,1)S(1)}, u32[]{:S(2)}, u32[]{:S(2)}) collective-permute-start(bf16[64,4096]{1,0:T(8,128)(2,1)S(1)} %collective-permute-done.6), channel_id=1, source_target_pairs={{0,4},{1,5},{2,0},{3,1},{4,8},{5,9},{6,2},{7,3},{8,12},{9,13},{10,... | collective-permute-start | bytes 1572872 | tf_op jit(solution)/shard_map/ag4a/ppermute | solution.py:92
  62.7 1.9 collective-permute-start.30
  63.0 14.6 %collective-permute-start.13 = (bf16[64,4096]{1,0:T(8,128)(2,1)S(1)}, bf16[64,4096]{1,0:T(8,128)(2,1)S(1)}, u32[]{:S(2)}, u32[]{:S(2)}) collective-permute-start(bf16[64,4096]{1,0:T(8,128)(2,1)S(1)} %collective-permute-done.12), channel_id=1, source_target_pairs={{0,2},{1,3},{2,6},{3,7},{4,0},{5,1},{6,10},{7,11},{8,4},{9,5},{10,... | collective-permute-start | bytes 1572872 | tf_op jit(solution)/shard_map/ag4b/ppermute | solution.py:92
  64.6 20.9 %collective-permute-start.38 = (bf16[64,4096]{1,0:T(8,128)(2,1)S(1)}, bf16[64,4096]{1,0:T(8,128)(2,1)S(1)}, u32[]{:S(2)}, u32[]{:S(2)}) collective-permute-start(bf16[64,4096]{1,0:T(8,128)(2,1)S(1)} %get-tuple-element.27), channel_id=1, source_target_pairs={{0,4},{1,5},{2,0},{3,1},{4,8},{5,9},{6,2},{7,3},{8,12},{9,13},{10,... | collective-permute-start | bytes 1572872 | tf_op jit(solution)/shard_map/rs2a/ppermute | solution.py:92
  74.6 14.0 %collective-permute-start.45 = (bf16[64,4096]{1,0:T(8,128)(2,1)S(1)}, bf16[64,4096]{1,0:T(8,128)(2,1)S(1)}, u32[]{:S(2)}, u32[]{:S(2)}) collective-permute-start(bf16[64,4096]{1,0:T(8,128)(2,1)S(1)} %get-tuple-element.28), channel_id=1, source_target_pairs={{0,2},{1,3},{2,6},{3,7},{4,0},{5,1},{6,10},{7,11},{8,4},{9,5},{10,... | collective-permute-start | bytes 1572872 | tf_op jit(solution)/shard_map/rs2b/ppermute | solution.py:92
  76.0 24.5 %collective-permute-start.31 = (bf16[128,4096]{1,0:T(8,128)(2,1)S(1)}, bf16[128,4096]{1,0:T(8,128)(2,1)S(1)}, u32[]{:S(2)}, u32[]{:S(2)}) collective-permute-start(bf16[128,4096]{1,0:T(8,128)(2,1)S(1)} %slice.449), channel_id=1, source_target_pairs={{0,1},{1,0},{2,3},{3,2},{4,5},{5,4},{6,7},{7,6},{8,9},{9,8},{10,11... | collective-permute-start | bytes 3145736 | tf_op jit(solution)/shard_map/ps3/ppermute | solution.py:92
  77.6 11.2 %collective-permute-start.26 = (bf16[64,4096]{1,0:T(8,128)(2,1)S(1)}, bf16[64,4096]{1,0:T(8,128)(2,1)S(1)}, u32[]{:S(2)}, u32[]{:S(2)}) collective-permute-start(bf16[64,4096]{1,0:T(8,128)(2,1)S(1)} %collective-permute-done.7), channel_id=1, source_target_pairs={{0,1},{1,0},{2,3},{3,2},{4,5},{5,4},{6,7},{7,6},{8,9},{9,8},{10,11... | collective-permute-start | bytes 1572872 | tf_op jit(solution)/shard_map/xs4a/ppermute | solution.py:92
  85.4 15.9 %collective-permute-start.8 = (bf16[64,4096]{1,0:T(8,128)(2,1)S(1)}, bf16[64,4096]{1,0:T(8,128)(2,1)S(1)}, u32[]{:S(2)}, u32[]{:S(2)}) collective-permute-start(bf16[64,4096]{1,0:T(8,128)(2,1)S(1)} %collective-permute-done.7), channel_id=1, source_target_pairs={{0,4},{1,5},{2,0},{3,1},{4,8},{5,9},{6,2},{7,3},{8,12},{9,13},{10,... | collective-permute-start | bytes 1572872 | tf_op jit(solution)/shard_map/ag5a/ppermute | solution.py:92
  88.6 1.9 collective-permute-start.27
  88.8 14.5 %collective-permute-start.14 = (bf16[64,4096]{1,0:T(8,128)(2,1)S(1)}, bf16[64,4096]{1,0:T(8,128)(2,1)S(1)}, u32[]{:S(2)}, u32[]{:S(2)}) collective-permute-start(bf16[64,4096]{1,0:T(8,128)(2,1)S(1)} %collective-permute-done.13), channel_id=1, source_target_pairs={{0,2},{1,3},{2,6},{3,7},{4,0},{5,1},{6,10},{7,11},{8,4},{9,5},{10,... | collective-permute-start | bytes 1572872 | tf_op jit(solution)/shard_map/ag5b/ppermute | solution.py:92
  90.5 19.1 %collective-permute-start.39 = (bf16[64,4096]{1,0:T(8,128)(2,1)S(1)}, bf16[64,4096]{1,0:T(8,128)(2,1)S(1)}, u32[]{:S(2)}, u32[]{:S(2)}) collective-permute-start(bf16[64,4096]{1,0:T(8,128)(2,1)S(1)} %get-tuple-element.25), channel_id=1, source_target_pairs={{0,4},{1,5},{2,0},{3,1},{4,8},{5,9},{6,2},{7,3},{8,12},{9,13},{10,... | collective-permute-start | bytes 1572872 | tf_op jit(solution)/shard_map/rs3a/ppermute | solution.py:92
  100.5 13.9 %collective-permute-start.46 = (bf16[64,4096]{1,0:T(8,128)(2,1)S(1)}, bf16[64,4096]{1,0:T(8,128)(2,1)S(1)}, u32[]{:S(2)}, u32[]{:S(2)}) collective-permute-start(bf16[64,4096]{1,0:T(8,128)(2,1)S(1)} %get-tuple-element.26), channel_id=1, source_target_pairs={{0,2},{1,3},{2,6},{3,7},{4,0},{5,1},{6,10},{7,11},{8,4},{9,5},{10,... | collective-permute-start | bytes 1572872 | tf_op jit(solution)/shard_map/rs3b/ppermute | solution.py:92
  101.4 25.0 %collective-permute-start.28 = (bf16[128,4096]{1,0:T(8,128)(2,1)S(1)}, bf16[128,4096]{1,0:T(8,128)(2,1)S(1)}, u32[]{:S(2)}, u32[]{:S(2)}) collective-permute-start(bf16[128,4096]{1,0:T(8,128)(2,1)S(1)} %slice.450), channel_id=1, source_target_pairs={{0,1},{1,0},{2,3},{3,2},{4,5},{5,4},{6,7},{7,6},{8,9},{9,8},{10,11... | collective-permute-start | bytes 3145736 | tf_op jit(solution)/shard_map/ps4/ppermute | solution.py:92
  103.3 11.3 %collective-permute-start.23 = (bf16[64,4096]{1,0:T(8,128)(2,1)S(1)}, bf16[64,4096]{1,0:T(8,128)(2,1)S(1)}, u32[]{:S(2)}, u32[]{:S(2)}) collective-permute-start(bf16[64,4096]{1,0:T(8,128)(2,1)S(1)} %collective-permute-done.8), channel_id=1, source_target_pairs={{0,1},{1,0},{2,3},{3,2},{4,5},{5,4},{6,7},{7,6},{8,9},{9,8},{10,11... | collective-permute-start | bytes 1572872 | tf_op jit(solution)/shard_map/xs5a/ppermute | solution.py:92
  109.6 17.6 %collective-permute-start.9 = (bf16[64,4096]{1,0:T(8,128)(2,1)S(1)}, bf16[64,4096]{1,0:T(8,128)(2,1)S(1)}, u32[]{:S(2)}, u32[]{:S(2)}) collective-permute-start(bf16[64,4096]{1,0:T(8,128)(2,1)S(1)} %collective-permute-done.8), channel_id=1, source_target_pairs={{0,4},{1,5},{2,0},{3,1},{4,8},{5,9},{6,2},{7,3},{8,12},{9,13},{10,... | collective-permute-start | bytes 1572872 | tf_op jit(solution)/shard_map/ag6a/ppermute | solution.py:92
  114.5 1.9 collective-permute-start.24
  114.7 14.5 %collective-permute-start.15 = (bf16[64,4096]{1,0:T(8,128)(2,1)S(1)}, bf16[64,4096]{1,0:T(8,128)(2,1)S(1)}, u32[]{:S(2)}, u32[]{:S(2)}) collective-permute-start(bf16[64,4096]{1,0:T(8,128)(2,1)S(1)} %collective-permute-done.14), channel_id=1, source_target_pairs={{0,2},{1,3},{2,6},{3,7},{4,0},{5,1},{6,10},{7,11},{8,4},{9,5},{10,... | collective-permute-start | bytes 1572872 | tf_op jit(solution)/shard_map/ag6b/ppermute | solution.py:92
  116.4 16.8 %collective-permute-start.40 = (bf16[64,4096]{1,0:T(8,128)(2,1)S(1)}, bf16[64,4096]{1,0:T(8,128)(2,1)S(1)}, u32[]{:S(2)}, u32[]{:S(2)}) collective-permute-start(bf16[64,4096]{1,0:T(8,128)(2,1)S(1)} %get-tuple-element.23), channel_id=1, source_target_pairs={{0,4},{1,5},{2,0},{3,1},{4,8},{5,9},{6,2},{7,3},{8,12},{9,13},{10,... | collective-permute-start | bytes 1572872 | tf_op jit(solution)/shard_map/rs4a/ppermute | solution.py:92
  126.4 13.9 %collective-permute-start.47 = (bf16[64,4096]{1,0:T(8,128)(2,1)S(1)}, bf16[64,4096]{1,0:T(8,128)(2,1)S(1)}, u32[]{:S(2)}, u32[]{:S(2)}) collective-permute-start(bf16[64,4096]{1,0:T(8,128)(2,1)S(1)} %get-tuple-element.24), channel_id=1, source_target_pairs={{0,2},{1,3},{2,6},{3,7},{4,0},{5,1},{6,10},{7,11},{8,4},{9,5},{10,... | collective-permute-start | bytes 1572872 | tf_op jit(solution)/shard_map/rs4b/ppermute | solution.py:92
  127.2 25.0 %collective-permute-start.25 = (bf16[128,4096]{1,0:T(8,128)(2,1)S(1)}, bf16[128,4096]{1,0:T(8,128)(2,1)S(1)}, u32[]{:S(2)}, u32[]{:S(2)}) collective-permute-start(bf16[128,4096]{1,0:T(8,128)(2,1)S(1)} %slice.451), channel_id=1, source_target_pairs={{0,1},{1,0},{2,3},{3,2},{4,5},{5,4},{6,7},{7,6},{8,9},{9,8},{10,11... | collective-permute-start | bytes 3145736 | tf_op jit(solution)/shard_map/ps5/ppermute | solution.py:92
  129.2 11.3 %collective-permute-start.20 = (bf16[64,4096]{1,0:T(8,128)(2,1)S(1)}, bf16[64,4096]{1,0:T(8,128)(2,1)S(1)}, u32[]{:S(2)}, u32[]{:S(2)}) collective-permute-start(bf16[64,4096]{1,0:T(8,128)(2,1)S(1)} %collective-permute-done.9), channel_id=1, source_target_pairs={{0,1},{1,0},{2,3},{3,2},{4,5},{5,4},{6,7},{7,6},{8,9},{9,8},{10,11... | collective-permute-start | bytes 1572872 | tf_op jit(solution)/shard_map/xs6a/ppermute | solution.py:92
  133.2 19.9 %collective-permute-start.10 = (bf16[64,4096]{1,0:T(8,128)(2,1)S(1)}, bf16[64,4096]{1,0:T(8,128)(2,1)S(1)}, u32[]{:S(2)}, u32[]{:S(2)}) collective-permute-start(bf16[64,4096]{1,0:T(8,128)(2,1)S(1)} %collective-permute-done.9), channel_id=1, source_target_pairs={{0,4},{1,5},{2,0},{3,1},{4,8},{5,9},{6,2},{7,3},{8,12},{9,13},{10,... | collective-permute-start | bytes 1572872 | tf_op jit(solution)/shard_map/ag7a/ppermute | solution.py:92
  140.3 1.9 collective-permute-start.21
  140.5 14.5 %collective-permute-start.16 = (bf16[64,4096]{1,0:T(8,128)(2,1)S(1)}, bf16[64,4096]{1,0:T(8,128)(2,1)S(1)}, u32[]{:S(2)}, u32[]{:S(2)}) collective-permute-start(bf16[64,4096]{1,0:T(8,128)(2,1)S(1)} %collective-permute-done.15), channel_id=1, source_target_pairs={{0,2},{1,3},{2,6},{3,7},{4,0},{5,1},{6,10},{7,11},{8,4},{9,5},{10,... | collective-permute-start | bytes 1572872 | tf_op jit(solution)/shard_map/ag7b/ppermute | solution.py:92
  142.2 14.0 %collective-permute-start.41 = (bf16[64,4096]{1,0:T(8,128)(2,1)S(1)}, bf16[64,4096]{1,0:T(8,128)(2,1)S(1)}, u32[]{:S(2)}, u32[]{:S(2)}) collective-permute-start(bf16[64,4096]{1,0:T(8,128)(2,1)S(1)} %get-tuple-element.21), channel_id=1, source_target_pairs={{0,4},{1,5},{2,0},{3,1},{4,8},{5,9},{6,2},{7,3},{8,12},{9,13},{10,... | collective-permute-start | bytes 1572872 | tf_op jit(solution)/shard_map/rs5a/ppermute | solution.py:92
  152.2 13.9 %collective-permute-start.48 = (bf16[64,4096]{1,0:T(8,128)(2,1)S(1)}, bf16[64,4096]{1,0:T(8,128)(2,1)S(1)}, u32[]{:S(2)}, u32[]{:S(2)}) collective-permute-start(bf16[64,4096]{1,0:T(8,128)(2,1)S(1)} %get-tuple-element.22), channel_id=1, source_target_pairs={{0,2},{1,3},{2,6},{3,7},{4,0},{5,1},{6,10},{7,11},{8,4},{9,5},{10,... | collective-permute-start | bytes 1572872 | tf_op jit(solution)/shard_map/rs5b/ppermute | solution.py:92
  153.0 24.0 %collective-permute-start.22 = (bf16[128,4096]{1,0:T(8,128)(2,1)S(1)}, bf16[128,4096]{1,0:T(8,128)(2,1)S(1)}, u32[]{:S(2)}, u32[]{:S(2)}) collective-permute-start(bf16[128,4096]{1,0:T(8,128)(2,1)S(1)} %slice.452), channel_id=1, source_target_pairs={{0,1},{1,0},{2,3},{3,2},{4,5},{5,4},{6,7},{7,6},{8,9},{9,8},{10,11... | collective-permute-start | bytes 3145736 | tf_op jit(solution)/shard_map/ps6/ppermute | solution.py:92
  155.0 12.8 %collective-permute-start.17 = (bf16[64,4096]{1,0:T(8,128)(2,1)S(1)}, bf16[64,4096]{1,0:T(8,128)(2,1)S(1)}, u32[]{:S(2)}, u32[]{:S(2)}) collective-permute-start(bf16[64,4096]{1,0:T(8,128)(2,1)S(1)} %collective-permute-done.10), channel_id=1, source_target_pairs={{0,1},{1,0},{2,3},{3,2},{4,5},{5,4},{6,7},{7,6},{8,9},{9,8},{10,11... | collective-permute-start | bytes 1572872 | tf_op jit(solution)/shard_map/xs7a/ppermute | solution.py:92
  156.2 12.3 %collective-permute-start.18 = (bf16[64,4096]{1,0:T(8,128)(2,1)S(1)}, bf16[64,4096]{1,0:T(8,128)(2,1)S(1)}, u32[]{:S(2)}, u32[]{:S(2)}) collective-permute-start(bf16[64,4096]{1,0:T(8,128)(2,1)S(1)} %collective-permute-done.16), channel_id=1, source_target_pairs={{0,1},{1,0},{2,3},{3,2},{4,5},{5,4},{6,7},{7,6},{8,9},{9,8},{10,11... | collective-permute-start | bytes 1572872 | tf_op jit(solution)/shard_map/xs7b/ppermute | solution.py:92
  166.3 13.1 %collective-permute-start.42 = (bf16[64,4096]{1,0:T(8,128)(2,1)S(1)}, bf16[64,4096]{1,0:T(8,128)(2,1)S(1)}, u32[]{:S(2)}, u32[]{:S(2)}) collective-permute-start(bf16[64,4096]{1,0:T(8,128)(2,1)S(1)} %get-tuple-element.19), channel_id=1, source_target_pairs={{0,4},{1,5},{2,0},{3,1},{4,8},{5,9},{6,2},{7,3},{8,12},{9,13},{10,... | collective-permute-start | bytes 1572872 | tf_op jit(solution)/shard_map/rs6a/ppermute | solution.py:92
  167.9 13.0 %collective-permute-start.49 = (bf16[64,4096]{1,0:T(8,128)(2,1)S(1)}, bf16[64,4096]{1,0:T(8,128)(2,1)S(1)}, u32[]{:S(2)}, u32[]{:S(2)}) collective-permute-start(bf16[64,4096]{1,0:T(8,128)(2,1)S(1)} %get-tuple-element.20), channel_id=1, source_target_pairs={{0,2},{1,3},{2,6},{3,7},{4,0},{5,1},{6,10},{7,11},{8,4},{9,5},{10,... | collective-permute-start | bytes 1572872 | tf_op jit(solution)/shard_map/rs6b/ppermute | solution.py:92
  177.0 6.2 %collective-permute-start.19 = (bf16[128,4096]{1,0:T(8,128)(2,1)S(1)}, bf16[128,4096]{1,0:T(8,128)(2,1)S(1)}, u32[]{:S(2)}, u32[]{:S(2)}) collective-permute-start(bf16[128,4096]{1,0:T(8,128)(2,1)S(1)} %slice.453), channel_id=1, source_target_pairs={{0,1},{1,0},{2,3},{3,2},{4,5},{5,4},{6,7},{7,6},{8,9},{9,8},{10,11... | collective-permute-start | bytes 3145736 | tf_op jit(solution)/shard_map/ps7/ppermute | solution.py:92
  181.1 12.1 %collective-permute-start.43 = (bf16[64,4096]{1,0:T(8,128)(2,1)S(1)}, bf16[64,4096]{1,0:T(8,128)(2,1)S(1)}, u32[]{:S(2)}, u32[]{:S(2)}) collective-permute-start(bf16[64,4096]{1,0:T(8,128)(2,1)S(1)} %get-tuple-element.17), channel_id=1, source_target_pairs={{0,4},{1,5},{2,0},{3,1},{4,8},{5,9},{6,2},{7,3},{8,12},{9,13},{10,... | collective-permute-start | bytes 1572872 | tf_op jit(solution)/shard_map/rs7a/ppermute | solution.py:92
  182.9 12.1 %collective-permute-start.50 = (bf16[64,4096]{1,0:T(8,128)(2,1)S(1)}, bf16[64,4096]{1,0:T(8,128)(2,1)S(1)}, u32[]{:S(2)}, u32[]{:S(2)}) collective-permute-start(bf16[64,4096]{1,0:T(8,128)(2,1)S(1)} %get-tuple-element.18), channel_id=1, source_target_pairs={{0,2},{1,3},{2,6},{3,7},{4,0},{5,1},{6,10},{7,11},{8,4},{9,5},{10,... | collective-permute-start | bytes 1572872 | tf_op jit(solution)/shard_map/rs7b/ppermute | solution.py:92
  195.1 11.2 %collective-permute-start.44 = (bf16[64,4096]{1,0:T(8,128)(2,1)S(1)}, bf16[64,4096]{1,0:T(8,128)(2,1)S(1)}, u32[]{:S(2)}, u32[]{:S(2)}) collective-permute-start(bf16[64,4096]{1,0:T(8,128)(2,1)S(1)} %get-tuple-element.15), channel_id=1, source_target_pairs={{0,4},{1,5},{2,0},{3,1},{4,8},{5,9},{6,2},{7,3},{8,12},{9,13},{10,... | collective-permute-start | bytes 1572872 | tf_op jit(solution)/shard_map/rs0a/ppermute | solution.py:92
  195.8 10.9 %collective-permute-start.51 = (bf16[64,4096]{1,0:T(8,128)(2,1)S(1)}, bf16[64,4096]{1,0:T(8,128)(2,1)S(1)}, u32[]{:S(2)}, u32[]{:S(2)}) collective-permute-start(bf16[64,4096]{1,0:T(8,128)(2,1)S(1)} %get-tuple-element.16), channel_id=1, source_target_pairs={{0,2},{1,3},{2,6},{3,7},{4,0},{5,1},{6,10},{7,11},{8,4},{9,5},{10,... | collective-permute-start | bytes 1572872 | tf_op jit(solution)/shard_map/rs0b/ppermute | solution.py:92

commit v3 on v2

--- a/solution.py
+++ b/solution.py
@@ -25,7 +25,8 @@
     return lax.all_to_all(outgoing[:, None], AXIS, split_axis=0, concat_axis=0, tiled=True)[:, 0]
 
 
-def table_kernel(limit, where, gate_ref, *refs):
+def table_kernel(mine, placement, capacity, owners, gate_ref, *refs):
+    limit = capacity[placement[mine[0]]]
     gate = gate_ref[...]
     devices, rows = gate.shape
     hit = jnp.where(gate > 0, 1.0, 0.0).astype(jnp.bfloat16)
@@ -38,7 +39,7 @@
     earlier = jnp.where(earlier, 1.0, 0.0).astype(jnp.bfloat16)
     before = jnp.dot(earlier, hit, preferred_element_type=jnp.float32)
     rank = within + jnp.sum(before, axis=1, keepdims=True)
-    table = jnp.where(rank < limit[0].astype(jnp.float32), gate, 0.0).T
+    table = jnp.where(rank < limit.astype(jnp.float32), gate, 0.0).T
     out = refs[-1]
     steps = out.shape[1]
     half = rows // 2
@@ -49,24 +50,23 @@
         piece = table[part : part + half]
         made = jnp.zeros((half, steps), jnp.float32)
         for step in range(steps):
-            picked = jnp.sum(jnp.where(column == where[step, index], piece, 0.0), axis=1, keepdims=True)
+            picked = jnp.sum(jnp.where(column == owners[(mine[0] * steps + step) * 4 + index], piece, 0.0), axis=1, keepdims=True)
             made = jnp.where(turn == step, picked, made)
         out[index * half : (index + 1) * half, :] = made
 
 
-def weight_table(gate, where, placement, capacity, gates):
-    expert = lax.dynamic_index_in_dim(placement, lax.axis_index(AXIS), 0, False)
-    limit = lax.dynamic_index_in_dim(capacity, expert, 0, True)
+def weight_table(gate, owners, placement, capacity, gates):
     smem = pl.BlockSpec(memory_space=pltpu.SMEM)
     hbm = pl.BlockSpec(memory_space=pl.ANY)
     vmem = pl.BlockSpec(memory_space=pltpu.VMEM)
+    mine = lax.axis_index(AXIS).astype(jnp.int32).reshape(1)
     return pl.pallas_call(
         table_kernel,
-        out_shape=jax.ShapeDtypeStruct((2 * gate.shape[1], where.shape[0]), jnp.float32),
-        in_specs=[smem, smem, vmem] + [hbm] * len(gates),
+        out_shape=jax.ShapeDtypeStruct((2 * gate.shape[1], owners.shape[1]), jnp.float32),
+        in_specs=[smem] * 4 + [vmem] + [hbm] * len(gates),
         out_specs=vmem,
         cost_estimate=COST,
-    )(limit, where, gate, *gates)
+    )(mine, placement, capacity, jnp.asarray(owners.reshape(-1)), gate, *gates)
 
 
 def ring_form(tokens, expert_ids, gate_weights, weights_in, weights_out, placement, capacity):
@@ -96,7 +96,6 @@
         for step in range(chips):
             for index, (way, core) in enumerate([(-1, 0), (1, 0), (-1, 1), (1, 1)]):
                 owners[d, step, index] = 2 * chip_at((spot_of[d // 2] + way * step) % chips) + (d + core) % 2
-    where = lax.dynamic_index_in_dim(jnp.asarray(owners), lax.axis_index(AXIS), 0, False)
     first_weights, second_weights = weights_in[0], weights_out[0]
 
     aheads, behinds = [tokens[:half]], [tokens[half:]]
@@ -105,14 +104,23 @@
         behinds.append(send(behinds[-1], back, f"ag{step}b"))
     with jax.named_scope("meta"):
         gate = incoming_gates(expert_ids, gate_weights, placement)
-        scales = weight_table(gate, where, placement, capacity, (aheads[1], behinds[1]))
+        scales = weight_table(gate, owners, placement, capacity, (aheads[1], behinds[1]))
+    joined = min(3, chips - 1)
     sums_a = sums_b = None
     for turn in range(1, chips + 1):
         step = turn % chips
         pieces = [aheads[step], behinds[step]]
-        pieces += [send(pieces[0], swap, f"xs{step}a"), send(pieces[1], swap, f"xs{step}b")]
+        if step:
+            pieces += [send(pieces[0], swap, f"xs{step}a"), send(pieces[1], swap, f"xs{step}b")]
         with jax.named_scope(f"kernel{step}"):
-            outs = expert_block(jnp.concatenate(pieces, axis=0), first_weights, second_weights)
+            if step == joined:
+                pieces += [tokens, send(tokens, swap, "xs0")]
+            if step:
+                outs = expert_block(jnp.concatenate(pieces, axis=0), first_weights, second_weights)
+            else:
+                outs = own_outs
+            if step == joined:
+                outs, own_outs = outs[: 2 * rows], outs[2 * rows :]
             outs = outs.astype(jnp.float32) * scales[:, step : step + 1]
             kept, other = outs[:rows], outs[rows:].astype(jnp.bfloat16)
         from_other = send(other, swap, f"ps{step}")

time: 208 us -> 205 us (0.986)
  matrix products: 67.9 us -> 64 us
  local copies, waits for them, and re-layouts: 8.93 us -> 5.68 us
  starting transfers between devices: 36.6 us -> 39 us
  waiting for transfers between devices: 83.8 us -> 86 us
    dot_general x8 -> x7, matrix products: 52.7 us -> 45.8 us  [expert_block(): jnp.dot(inputs, first_weights, preferred_element_type=jnp.float32)]
    dot_general x8 -> x7, matrix products: 15.2 us -> 18.1 us  [expert_block(): jnp.dot(hidden, second_weights, preferred_element_type=jnp.float32)]
    dynamic_slice x2 -> x0, local copies, waits for them, and re-layouts: 2.47 us -> none  [the longest x1 1.24 us: weight_table(): expert = lax.dynamic_index_in_dim(placement, lax.axis_index(AXIS), 0, False)]
    ppermute x52 -> x51, starting transfers between devices: 30.3 us -> 32.6 us  [send(): return lax.ppermute(value, AXIS, where)]
    ppermute x52 -> x51, waiting for transfers between devices: 83.8 us -> 84.8 us  [send(): return lax.ppermute(value, AXIS, where)]
  transfers between devices with their start and end apart: 53 -> 52, of which waited for: 25 -> 27; matrix products, arithmetic and copies ran while one was open for 38% -> 36% of each run, Pallas kernels for 1% -> 1%
where the time goes in v3:
time: 205 us; the launch traced here: 204 us
  waiting for transfers between devices  86 us (42%)
  matrix products  64 us (31%)
  starting transfers between devices  39 us (19%)
  other arithmetic  7 us (3%)
  local copies, waits for them, and re-layouts  5.68 us (3%)
    ppermute x51, waiting for transfers between devices, send(): return lax.ppermute(value, AXIS, where)  84.8 us
    dot_general x7, matrix products, expert_block(): jnp.dot(inputs, first_weights, preferred_element_type=jnp.float32)  45.8 us
    ppermute x51, starting transfers between devices, send(): return lax.ppermute(value, AXIS, where)  32.6 us
    dot_general x7, matrix products, expert_block(): jnp.dot(hidden, second_weights, preferred_element_type=jnp.float32)  18.1 us
    all_to_all x1, starting transfers between devices, incoming_gates(): lax.all_to_all(outgoing[:, None], AXIS, split_axis=0, concat_axis=0, tile...  6.38 us
  transfers between devices with their start and end apart: 52, of which 27 were waited for; matrix products, arithmetic and copies ran while one was open for 36% of the time, Pallas kernels for 1%

profile of v3, /device:TPU:0, one launch (start us, length us, event | category | flops | bytes accessed | tf_op | source)
XLA Modules:
  0.0 204.3 jit_solution(9311186485589283929)
XLA Ops:
  0.0 1.3 fusion.183
  1.3 3.1 %collective-permute-start = (bf16[64,4096]{1,0:T(8,128)(2,1)S(1)}, bf16[64,4096]{1,0:T(8,128)(2,1)S(1)}, u32[]{:S(2)}, u32[]{:S(2)}) collective-permute-start(bf16[64,4096]{1,0:T(8,128)(2,1)S(1)} %get-tuple-element.32), channel_id=1, source_target_pairs={{0,4},{1,5},{2,0},{3,1},{4,8},{5,9},{6,2},{7,3},{8,12},{9,13},{10,... | collective-permute-start | bytes 1572872 | tf_op jit(solution)/shard_map/ag1a/ppermute | solution.py:92
  4.4 1.4 select_reduce_fusion
  5.8 6.4 %all-to-all-start = ((f32[16,1,128]{2,1,0:T(1,128)}), f32[16,1,128]{2,1,0:T(1,128)S(1)}, u32[]{:S(2)}, u32[]{:S(2)}) async-start(f32[16,1,128]{2,1,0:T(1,128)} %bitcast.6), calls=%async_computation | async-start | bytes 16384 | tf_op jit(solution)/shard_map/meta/all_to_all | solution.py:25
  12.5 3.7 %collective-permute-done.refs_0_ = bf16[64,4096]{1,0:T(8,128)(2,1)S(1)} collective-permute-done((bf16[64,4096]{1,0:T(8,128)(2,1)S(1)}, bf16[64,4096]{1,0:T(8,128)(2,1)S(1)}, u32[]{:S(2)}, u32[]{:S(2)}) %collective-permute-start) | collective-permute-done | bytes 524320 | tf_op jit(solution)/shard_map/ag1a/ppermute | solution.py:92
  16.2 1.9 collective-permute-start.1
  18.6 1.2 all-to-all-done
  19.8 0.6 copy-done.1
  20.4 2.0 meta.1
  22.4 2.4 %slice_reduce_fusion = (f32[256]{0:T(256)S(1)}, f32[256]{0:T(256)S(1)}, f32[256]{0:T(256)S(1)}, f32[256]{0:T(256)S(1)}, f32[256]{0:T(256)S(1)}, /*index=5*/f32[256]{0:T(256)S(1)}, f32[256]{0:T(256)S(1)}, f32[256]{0:T(256)S(1)}) fusion(f32[256,8]{1,0:T(8,128)} %meta.1), kind=kLoop, calls=%fused_computation.158 | loop fusion | bytes 16384 | tf_op jit(solution)/shard_map/kernel1/slice | solution.py:124
  24.8 4.6 %collective-permute-done.1 = bf16[64,4096]{1,0:T(8,128)(2,1)S(1)} collective-permute-done((bf16[64,4096]{1,0:T(8,128)(2,1)S(1)}, bf16[64,4096]{1,0:T(8,128)(2,1)S(1)}, u32[]{:S(2)}, u32[]{:S(2)}) %collective-permute-start.1) | collective-permute-done | bytes 524320 | tf_op jit(solution)/shard_map/ag2a/ppermute | solution.py:92
  29.5 3.2 %collective-permute-done.4 = bf16[64,4096]{1,0:T(8,128)(2,1)S(1)} collective-permute-done((bf16[64,4096]{1,0:T(8,128)(2,1)}, bf16[64,4096]{1,0:T(8,128)(2,1)S(1)}, u32[]{:S(2)}, u32[]{:S(2)}) %collective-permute-start.4) | collective-permute-done | bytes 524320 | tf_op jit(solution)/shard_map/ag2b/ppermute | solution.py:92
  32.7 7.0 %fusion = f32[256,1536]{1,0:T(8,128)S(1)} fusion(bf16[1,4096,1536]{2,1,0:T(8,128)(2,1)} %param.11, bf16[64,4096]{1,0:T(8,128)(2,1)} %collective-permute-done.35, bf16[64,4096]{1,0:T(8,128)(2,1)S(1)} %collective-permute-done.34, bf16[64,4096]{1,0:T(8,128)(2,1)} %collective-permute-done.3.refs_1_, bf16[64,4096]{1,0:T(8,128)(2,1)} %copy-done.2), kind=kOutput, calls=%fused_computation | convolution fusion | flops 3229614080 | bytes 16252928 | tf_op jit(solution)/shard_map/kernel1/dot_general | solution.py:15
  39.8 1.9 broadcast_multiply_fusion
  42.4 1.6 collective-permute-start.2
  44.4 3.4 %fusion.2 = f32[256,1536]{1,0:T(8,128)S(1)} fusion(bf16[1,4096,1536]{2,1,0:T(8,128)(2,1)S(1)} %bitcast.80, bf16[64,4096]{1,0:T(8,128)(2,1)S(1)} %collective-permute-done.32, bf16[64,4096]{1,0:T(8,128)(2,1)S(1)} %collective-permute-done.31, bf16[64,4096]{1,0:T(8,128)(2,1)S(1)} %collective-permute-done.4, bf16[64,4096]{1,0:T(8,128)(2,1)S(1)} %collective-permute-done.1), kind=kOutput, calls=%fused_computation.2 | convolution fusion | flops 3229614080 | bytes 16252928 | tf_op jit(solution)/shard_map/kernel2/dot_general | solution.py:15
  47.8 4.7 %broadcast_multiply_fusion.1 = f32[256,4096]{1,0:T(8,128)S(1)} fusion(f32[256]{0:T(256)S(1)} %get-tuple-element.6, bf16[1,768,4096]{2,1,0:T(8,128)(2,1)} %param.12, f32[256,1536]{1,0:T(8,128)S(1)} %fusion.2), kind=kOutput, calls=%fused_computation.103 | convolution fusion | flops 1614938112 | bytes 12059648 | tf_op jit(solution)/shard_map/kernel2/dot_general | solution.py:19
  52.7 3.5 %collective-permute-done.2 = bf16[64,4096]{1,0:T(8,128)(2,1)S(1)} collective-permute-done((bf16[64,4096]{1,0:T(8,128)(2,1)S(1)}, bf16[64,4096]{1,0:T(8,128)(2,1)S(1)}, u32[]{:S(2)}, u32[]{:S(2)}) %collective-permute-start.2) | collective-permute-done | bytes 524320 | tf_op jit(solution)/shard_map/ag3a/ppermute | solution.py:92
  56.3 1.4 collective-permute-done.5
  57.8 1.6 collective-permute-start.10
  60.3 1.6 collective-permute-start.37
  62.0 0.7 collective-permute-start.44
  62.8 9.4 %fusion.12 = f32[512,1536]{1,0:T(8,128)S(1)} fusion(bf16[512,4096]{1,0:T(8,128)(2,1)S(1)} %constant_dynamic-update-slice_fusion, bf16[1,4096,1536]{2,1,0:T(8,128)(2,1)} %param.11), kind=kOutput, calls=%fused_computation.12 | convolution fusion | flops 6442450944 | bytes 19922944 | tf_op jit(solution)/shard_map/kernel3/dot_general | solution.py:15
  72.2 3.8 %fusion.28 = bf16[512,4096]{1,0:T(8,128)(2,1)S(1)} fusion(bf16[1,768,4096]{2,1,0:T(8,128)(2,1)S(1)} %bitcast.84, f32[512,1536]{1,0:T(8,128)S(1)} %fusion.12), kind=kOutput, calls=%fused_computation.28 | convolution fusion | flops 3225681920 | bytes 13631488 | tf_op jit(solution)/shard_map/kernel3/dot_general | solution.py:19
  76.0 1.2 convert_multiply_fusion
  78.4 5.0 %collective-permute-done.37 = bf16[64,4096]{1,0:T(8,128)(2,1)S(1)} collective-permute-done((bf16[64,4096]{1,0:T(8,128)(2,1)S(1)}, bf16[64,4096]{1,0:T(8,128)(2,1)S(1)}, u32[]{:S(2)}, u32[]{:S(2)}) %collective-permute-start.37) | collective-permute-done | bytes 524320 | tf_op jit(solution)/shard_map/rs2a/ppermute | solution.py:92
  83.4 1.5 collective-permute-start.11
  85.8 1.3 collective-permute-done.28
  87.1 1.5 collective-permute-start.38
  88.6 6.7 %fusion.4 = f32[256,1536]{1,0:T(8,128)S(1)} fusion(bf16[1,4096,1536]{2,1,0:T(8,128)(2,1)} %param.11, bf16[64,4096]{1,0:T(8,128)(2,1)S(1)} %collective-permute-done.28, bf16[64,4096]{1,0:T(8,128)(2,1)S(1)} %collective-permute-done.27, bf16[64,4096]{1,0:T(8,128)(2,1)} %collective-permute-done.14, bf16[64,4096]{1,0:T(8,128)(2,1)} %collective-permute-done.10), kind=kOutput, calls=%fused_computation.4 | convolution fusion | flops 3229614080 | bytes 16252928 | tf_op jit(solution)/shard_map/kernel4/dot_general | solution.py:15
  95.4 1.9 broadcast_multiply_fusion.2
  98.4 1.4 collective-permute-done.15
  99.9 8.5 %collective-permute-done.38 = bf16[64,4096]{1,0:T(8,128)(2,1)S(1)} collective-permute-done((bf16[64,4096]{1,0:T(8,128)(2,1)S(1)}, bf16[64,4096]{1,0:T(8,128)(2,1)S(1)}, u32[]{:S(2)}, u32[]{:S(2)}) %collective-permute-start.38) | collective-permute-done | bytes 524320 | tf_op jit(solution)/shard_map/rs3a/ppermute | solution.py:92
  108.4 1.5 collective-permute-start.12
  109.9 1.3 collective-permute-done.45
  112.0 1.1 collective-permute-done.25
  113.1 1.4 collective-permute-start.39
  114.5 6.4 %fusion.6 = f32[256,1536]{1,0:T(8,128)S(1)} fusion(bf16[1,4096,1536]{2,1,0:T(8,128)(2,1)} %param.11, bf16[64,4096]{1,0:T(8,128)(2,1)S(1)} %collective-permute-done.25, bf16[64,4096]{1,0:T(8,128)(2,1)S(1)} %collective-permute-done.24, bf16[64,4096]{1,0:T(8,128)(2,1)S(1)} %collective-permute-done.15, bf16[64,4096]{1,0:T(8,128)(2,1)S(1)} %collective-permute-done.11), kind=kOutput, calls=%fused_computation.6 | convolution fusion | flops 3229614080 | bytes 16252928 | tf_op jit(solution)/shard_map/kernel5/dot_general | solution.py:15
  121.0 1.9 broadcast_multiply_fusion.3
  123.1 0.7 collective-permute-start.46
  124.0 2.0 collective-permute-done.16
  126.1 6.2 %collective-permute-done.39 = bf16[64,4096]{1,0:T(8,128)(2,1)S(1)} collective-permute-done((bf16[64,4096]{1,0:T(8,128)(2,1)S(1)}, bf16[64,4096]{1,0:T(8,128)(2,1)S(1)}, u32[]{:S(2)}, u32[]{:S(2)}) %collective-permute-start.39) | collective-permute-done | bytes 524320 | tf_op jit(solution)/shard_map/rs4a/ppermute | solution.py:92
  132.3 1.5 collective-permute-start.13
  133.8 3.3 %collective-permute-done.46 = bf16[64,4096]{1,0:T(8,128)(2,1)S(1)} collective-permute-done((bf16[64,4096]{1,0:T(8,128)(2,1)S(1)}, bf16[64,4096]{1,0:T(8,128)(2,1)S(1)}, u32[]{:S(2)}, u32[]{:S(2)}) %collective-permute-start.46) | collective-permute-done | bytes 524320 | tf_op jit(solution)/shard_map/rs4b/ppermute | solution.py:92
  137.9 1.1 collective-permute-done.22
  139.0 1.4 collective-permute-start.40
  140.4 6.4 %fusion.8 = f32[256,1536]{1,0:T(8,128)S(1)} fusion(bf16[1,4096,1536]{2,1,0:T(8,128)(2,1)} %param.11, bf16[64,4096]{1,0:T(8,128)(2,1)S(1)} %collective-permute-done.22, bf16[64,4096]{1,0:T(8,128)(2,1)S(1)} %collective-permute-done.21, bf16[64,4096]{1,0:T(8,128)(2,1)S(1)} %collective-permute-done.16, bf16[64,4096]{1,0:T(8,128)(2,1)S(1)} %collective-permute-done.12), kind=kOutput, calls=%fused_computation.8 | convolution fusion | flops 3229614080 | bytes 16252928 | tf_op jit(solution)/shard_map/kernel6/dot_general | solution.py:15
  146.9 1.9 broadcast_multiply_fusion.4
  148.9 0.7 collective-permute-start.47
  149.9 2.0 collective-permute-done.17
  151.9 3.3 %collective-permute-done.40 = bf16[64,4096]{1,0:T(8,128)(2,1)S(1)} collective-permute-done((bf16[64,4096]{1,0:T(8,128)(2,1)S(1)}, bf16[64,4096]{1,0:T(8,128)(2,1)S(1)}, u32[]{:S(2)}, u32[]{:S(2)}) %collective-permute-start.40) | collective-permute-done | bytes 524320 | tf_op jit(solution)/shard_map/rs5a/ppermute | solution.py:92
  155.3 7.7 %collective-permute-done.47 = bf16[64,4096]{1,0:T(8,128)(2,1)S(1)} collective-permute-done((bf16[64,4096]{1,0:T(8,128)(2,1)S(1)}, bf16[64,4096]{1,0:T(8,128)(2,1)S(1)}, u32[]{:S(2)}, u32[]{:S(2)}) %collective-permute-start.47) | collective-permute-done | bytes 524320 | tf_op jit(solution)/shard_map/rs5b/ppermute | solution.py:92
  163.2 1.5 collective-permute-start.41
  164.7 0.6 collective-permute-start.48
  165.3 6.4 %fusion.10 = f32[256,1536]{1,0:T(8,128)S(1)} fusion(bf16[1,4096,1536]{2,1,0:T(8,128)(2,1)} %param.11, bf16[64,4096]{1,0:T(8,128)(2,1)S(1)} %collective-permute-done.19, bf16[64,4096]{1,0:T(8,128)(2,1)S(1)} %collective-permute-done.18, bf16[64,4096]{1,0:T(8,128)(2,1)S(1)} %collective-permute-done.17, bf16[64,4096]{1,0:T(8,128)(2,1)S(1)} %collective-permute-done.13), kind=kOutput, calls=%fused_computation.10 | convolution fusion | flops 3229614080 | bytes 16252928 | tf_op jit(solution)/shard_map/kernel7/dot_general | solution.py:15
  171.7 1.9 broadcast_multiply_fusion.5
  174.1 2.2 %collective-permute-done.41 = bf16[64,4096]{1,0:T(8,128)(2,1)S(1)} collective-permute-done((bf16[64,4096]{1,0:T(8,128)(2,1)S(1)}, bf16[64,4096]{1,0:T(8,128)(2,1)S(1)}, u32[]{:S(2)}, u32[]{:S(2)}) %collective-permute-start.41) | collective-permute-done | bytes 524320 | tf_op jit(solution)/shard_map/rs6a/ppermute | solution.py:92
  176.4 1.6 collective-permute-done.48
  178.6 1.7 collective-permute-start.49
  180.5 10.1 %collective-permute-done.42 = bf16[64,4096]{1,0:T(8,128)(2,1)S(1)} collective-permute-done((bf16[64,4096]{1,0:T(8,128)(2,1)S(1)}, bf16[64,4096]{1,0:T(8,128)(2,1)S(1)}, u32[]{:S(2)}, u32[]{:S(2)}) %collective-permute-start.42) | collective-permute-done | bytes 524320 | tf_op jit(solution)/shard_map/rs7a/ppermute | solution.py:92
  191.2 1.0 collective-permute-start.43
  192.2 1.1 collective-permute-start.50
  193.5 9.1 %collective-permute-done.43 = bf16[64,4096]{1,0:T(8,128)(2,1)S(1)} collective-permute-done((bf16[64,4096]{1,0:T(8,128)(2,1)S(1)}, bf16[64,4096]{1,0:T(8,128)(2,1)S(1)}, u32[]{:S(2)}, u32[]{:S(2)}) %collective-permute-start.43) | collective-permute-done | bytes 524320 | tf_op jit(solution)/shard_map/rs0a/ppermute | solution.py:92
  203.3 1.0 pad_maximum_fusion
  (113 shorter events, 12.0 us)
Async XLA Ops:
  1.3 15.0 %collective-permute-start = (bf16[64,4096]{1,0:T(8,128)(2,1)S(1)}, bf16[64,4096]{1,0:T(8,128)(2,1)S(1)}, u32[]{:S(2)}, u32[]{:S(2)}) collective-permute-start(bf16[64,4096]{1,0:T(8,128)(2,1)S(1)} %get-tuple-element.32), channel_id=1, source_target_pairs={{0,4},{1,5},{2,0},{3,1},{4,8},{5,9},{6,2},{7,3},{8,12},{9,13},{10,... | collective-permute-start | bytes 1572872 | tf_op jit(solution)/shard_map/ag1a/ppermute | solution.py:92
  4.3 13.7 %collective-permute-start.3 = (bf16[64,4096]{1,0:T(8,128)(2,1)S(1)}, bf16[64,4096]{1,0:T(8,128)(2,1)}, u32[]{:S(2)}, u32[]{:S(2)}) collective-permute-start(bf16[64,4096]{1,0:T(8,128)(2,1)S(1)} %get-tuple-element.31), channel_id=1, source_target_pairs={{0,2},{1,3},{2,6},{3,7},{4,0},{5,1},{6,10},{7,11},{8,4},{9,5},{10,... | collective-permute-start | bytes 1572872 | tf_op jit(solution)/shard_map/ag1b/ppermute | solution.py:92
  5.8 14.0 %all-to-all-start = ((f32[16,1,128]{2,1,0:T(1,128)}), f32[16,1,128]{2,1,0:T(1,128)S(1)}, u32[]{:S(2)}, u32[]{:S(2)}) async-start(f32[16,1,128]{2,1,0:T(1,128)} %bitcast.6), calls=%async_computation | async-start | bytes 16384 | tf_op jit(solution)/shard_map/meta/all_to_all | solution.py:25
  12.1 49.9 %collective-permute-start.8 = (bf16[128,4096]{1,0:T(8,128)(2,1)}, bf16[128,4096]{1,0:T(8,128)(2,1)S(1)}, u32[]{:S(2)}, u32[]{:S(2)}) collective-permute-start(bf16[128,4096]{1,0:T(8,128)(2,1)} %param.8), channel_id=1, source_target_pairs={{0,1},{1,0},{2,3},{3,2},{4,5},{5,4},{6,7},{7,6},{8,9},{9,8},{10,11... | collective-permute-start | bytes 3145736 | tf_op jit(solution)/shard_map/kernel3/xs0/ppermute | solution.py:92
  16.2 3.6 %copy-start.2 = (bf16[64,4096]{1,0:T(8,128)(2,1)}, bf16[64,4096]{1,0:T(8,128)(2,1)S(1)}, u32[]{:S(2)}) copy-start(bf16[64,4096]{1,0:T(8,128)(2,1)S(1)} %collective-permute-done.refs_0_) | copy-start | bytes 1572868
  16.2 13.2 %collective-permute-start.1 = (bf16[64,4096]{1,0:T(8,128)(2,1)S(1)}, bf16[64,4096]{1,0:T(8,128)(2,1)S(1)}, u32[]{:S(2)}, u32[]{:S(2)}) collective-permute-start(bf16[64,4096]{1,0:T(8,128)(2,1)S(1)} %collective-permute-done.refs_0_), channel_id=1, source_target_pairs={{0,4},{1,5},{2,0},{3,1},{4,8},{5,9},{6,2},{7,3},{8,12},{9,13},{10,... | collective-permute-start | bytes 1572872 | tf_op jit(solution)/shard_map/ag2a/ppermute | solution.py:92
  18.1 14.6 %collective-permute-start.34 = (bf16[64,4096]{1,0:T(8,128)(2,1)S(1)}, bf16[64,4096]{1,0:T(8,128)(2,1)S(1)}, u32[]{:S(2)}, u32[]{:S(2)}) collective-permute-start(bf16[64,4096]{1,0:T(8,128)(2,1)S(1)} %collective-permute-done.refs_0_), channel_id=1, source_target_pairs={{0,1},{1,0},{2,3},{3,2},{4,5},{5,4},{6,7},{7,6},{8,9},{9,8},{10,11... | collective-permute-start | bytes 1572872 | tf_op jit(solution)/shard_map/xs1a/ppermute | solution.py:92
  18.1 14.5 %collective-permute-start.4 = (bf16[64,4096]{1,0:T(8,128)(2,1)}, bf16[64,4096]{1,0:T(8,128)(2,1)S(1)}, u32[]{:S(2)}, u32[]{:S(2)}) collective-permute-start(bf16[64,4096]{1,0:T(8,128)(2,1)} %collective-permute-done.3.refs_1_), channel_id=1, source_target_pairs={{0,2},{1,3},{2,6},{3,7},{4,0},{5,1},{6,10},{7,11},{8,4},{9,5},{10,... | collective-permute-start | bytes 1572872 | tf_op jit(solution)/shard_map/ag2b/ppermute | solution.py:92
  18.3 14.4 %collective-permute-start.35 = (bf16[64,4096]{1,0:T(8,128)(2,1)}, bf16[64,4096]{1,0:T(8,128)(2,1)}, u32[]{:S(2)}, u32[]{:S(2)}) collective-permute-start(bf16[64,4096]{1,0:T(8,128)(2,1)} %collective-permute-done.3.refs_1_), channel_id=1, source_target_pairs={{0,1},{1,0},{2,3},{3,2},{4,5},{5,4},{6,7},{7,6},{8,9},{9,8},{10,11... | collective-permute-start | bytes 1572872 | tf_op jit(solution)/shard_map/xs1b/ppermute | solution.py:92
  19.8 0.6 copy-start.1
  22.4 17.3 %slice-start.3 = ((s8[6291456]{0:T(1024)(128)(4,1)}), s8[4194304]{0:T(1024)(128)(4,1)S(1)}, s32[]{:S(2)}) async-start(s8[6291456]{0:T(1024)(128)(4,1)} %bitcast.81), calls=%async_computation.4 | async-start | bytes 8388608
  24.8 14.9 %slice-start.4 = ((s8[6291456]{0:T(1024)(128)(4,1)}), s8[2097152]{0:T(1024)(128)(4,1)S(1)}, s32[]{:S(2)}) async-start(s8[6291456]{0:T(1024)(128)(4,1)} %bitcast.81), calls=%async_computation.5 | async-start | bytes 4194304
  29.5 14.6 %collective-permute-start.31 = (bf16[64,4096]{1,0:T(8,128)(2,1)S(1)}, bf16[64,4096]{1,0:T(8,128)(2,1)S(1)}, u32[]{:S(2)}, u32[]{:S(2)}) collective-permute-start(bf16[64,4096]{1,0:T(8,128)(2,1)S(1)} %collective-permute-done.1), channel_id=1, source_target_pairs={{0,1},{1,0},{2,3},{3,2},{4,5},{5,4},{6,7},{7,6},{8,9},{9,8},{10,11... | collective-permute-start | bytes 1572872 | tf_op jit(solution)/shard_map/xs2a/ppermute | solution.py:92
  32.6 11.8 %collective-permute-start.32 = (bf16[64,4096]{1,0:T(8,128)(2,1)S(1)}, bf16[64,4096]{1,0:T(8,128)(2,1)S(1)}, u32[]{:S(2)}, u32[]{:S(2)}) collective-permute-start(bf16[64,4096]{1,0:T(8,128)(2,1)S(1)} %collective-permute-done.4), channel_id=1, source_target_pairs={{0,1},{1,0},{2,3},{3,2},{4,5},{5,4},{6,7},{7,6},{8,9},{9,8},{10,11... | collective-permute-start | bytes 1572872 | tf_op jit(solution)/shard_map/xs2b/ppermute | solution.py:92
  32.6 11.8 %slice-start = ((s8[12582912]{0:T(1024)(128)(4,1)}), s8[4194304]{0:T(1024)(128)(4,1)S(1)}, s32[]{:S(2)}) async-start(s8[12582912]{0:T(1024)(128)(4,1)} %bitcast.79), calls=%async_computation.1 | async-start | bytes 8388608
  32.7 11.8 %slice-start.1 = ((s8[12582912]{0:T(1024)(128)(4,1)}), s8[4194304]{0:T(1024)(128)(4,1)S(1)}, s32[]{:S(2)}) async-start(s8[12582912]{0:T(1024)(128)(4,1)} %bitcast.79), calls=%async_computation.2 | async-start | bytes 8388608
  39.7 4.7 %slice-start.2 = ((s8[12582912]{0:T(1024)(128)(4,1)}), s8[4194304]{0:T(1024)(128)(4,1)S(1)}, s32[]{:S(2)}) async-start(s8[12582912]{0:T(1024)(128)(4,1)} %bitcast.79), calls=%async_computation.3 | async-start | bytes 8388608
  41.8 15.9 %collective-permute-start.36 = (bf16[128,4096]{1,0:T(8,128)(2,1)S(1)}, bf16[128,4096]{1,0:T(8,128)(2,1)S(1)}, u32[]{:S(2)}, u32[]{:S(2)}) collective-permute-start(bf16[128,4096]{1,0:T(8,128)(2,1)S(1)} %slice.434), channel_id=1, source_target_pairs={{0,1},{1,0},{2,3},{3,2},{4,5},{5,4},{6,7},{7,6},{8,9},{9,8},{10,11... | collective-permute-start | bytes 3145736 | tf_op jit(solution)/shard_map/ps1/ppermute | solution.py:92
  42.4 13.9 %collective-permute-start.2 = (bf16[64,4096]{1,0:T(8,128)(2,1)S(1)}, bf16[64,4096]{1,0:T(8,128)(2,1)S(1)}, u32[]{:S(2)}, u32[]{:S(2)}) collective-permute-start(bf16[64,4096]{1,0:T(8,128)(2,1)S(1)} %collective-permute-done.1), channel_id=1, source_target_pairs={{0,4},{1,5},{2,0},{3,1},{4,8},{5,9},{6,2},{7,3},{8,12},{9,13},{10,... | collective-permute-start | bytes 1572872 | tf_op jit(solution)/shard_map/ag3a/ppermute | solution.py:92
  44.0 13.6 %collective-permute-start.5 = (bf16[64,4096]{1,0:T(8,128)(2,1)S(1)}, bf16[64,4096]{1,0:T(8,128)(2,1)S(1)}, u32[]{:S(2)}, u32[]{:S(2)}) collective-permute-start(bf16[64,4096]{1,0:T(8,128)(2,1)S(1)} %collective-permute-done.4), channel_id=1, source_target_pairs={{0,2},{1,3},{2,6},{3,7},{4,0},{5,1},{6,10},{7,11},{8,4},{9,5},{10,... | collective-permute-start | bytes 1572872 | tf_op jit(solution)/shard_map/ag3b/ppermute | solution.py:92
  52.6 24.8 %collective-permute-start.33 = (bf16[128,4096]{1,0:T(8,128)(2,1)S(1)}, bf16[128,4096]{1,0:T(8,128)(2,1)S(1)}, u32[]{:S(2)}, u32[]{:S(2)}) collective-permute-start(bf16[128,4096]{1,0:T(8,128)(2,1)S(1)} %slice.435), channel_id=1, source_target_pairs={{0,1},{1,0},{2,3},{3,2},{4,5},{5,4},{6,7},{7,6},{8,9},{9,8},{10,11... | collective-permute-start | bytes 3145736 | tf_op jit(solution)/shard_map/ps2/ppermute | solution.py:92
  56.3 3.4 %collective-permute-start.6 = (bf16[64,4096]{1,0:T(8,128)(2,1)S(1)}, bf16[64,4096]{1,0:T(8,128)(2,1)S(1)}, u32[]{:S(2)}, u32[]{:S(2)}) collective-permute-start(bf16[64,4096]{1,0:T(8,128)(2,1)S(1)} %collective-permute-done.2), channel_id=1, source_target_pairs={{0,1},{1,0},{2,3},{3,2},{4,5},{5,4},{6,7},{7,6},{8,9},{9,8},{10,11... | collective-permute-start | bytes 1572872 | tf_op jit(solution)/shard_map/xs3a/ppermute | solution.py:92
  57.6 2.6 %collective-permute-start.7 = (bf16[64,4096]{1,0:T(8,128)(2,1)S(1)}, bf16[64,4096]{1,0:T(8,128)(2,1)S(1)}, u32[]{:S(2)}, u32[]{:S(2)}) collective-permute-start(bf16[64,4096]{1,0:T(8,128)(2,1)S(1)} %collective-permute-done.5), channel_id=1, source_target_pairs={{0,1},{1,0},{2,3},{3,2},{4,5},{5,4},{6,7},{7,6},{8,9},{9,8},{10,11... | collective-permute-start | bytes 1572872 | tf_op jit(solution)/shard_map/xs3b/ppermute | solution.py:92
  57.7 4.2 %copy-start = (bf16[128,4096]{1,0:T(8,128)(2,1)S(1)}, bf16[128,4096]{1,0:T(8,128)(2,1)}, u32[]{:S(2)}) copy-start(bf16[128,4096]{1,0:T(8,128)(2,1)} %param.8) | copy-start | bytes 3145732
  57.8 20.0 %collective-permute-start.10 = (bf16[64,4096]{1,0:T(8,128)(2,1)S(1)}, bf16[64,4096]{1,0:T(8,128)(2,1)}, u32[]{:S(2)}, u32[]{:S(2)}) collective-permute-start(bf16[64,4096]{1,0:T(8,128)(2,1)S(1)} %collective-permute-done.2), channel_id=1, source_target_pairs={{0,4},{1,5},{2,0},{3,1},{4,8},{5,9},{6,2},{7,3},{8,12},{9,13},{10,... | collective-permute-start | bytes 1572872 | tf_op jit(solution)/shard_map/ag4a/ppermute | solution.py:92
  59.7 18.7 %collective-permute-start.14 = (bf16[64,4096]{1,0:T(8,128)(2,1)S(1)}, bf16[64,4096]{1,0:T(8,128)(2,1)}, u32[]{:S(2)}, u32[]{:S(2)}) collective-permute-start(bf16[64,4096]{1,0:T(8,128)(2,1)S(1)} %collective-permute-done.5), channel_id=1, source_target_pairs={{0,2},{1,3},{2,6},{3,7},{4,0},{5,1},{6,10},{7,11},{8,4},{9,5},{10,... | collective-permute-start | bytes 1572872 | tf_op jit(solution)/shard_map/ag4b/ppermute | solution.py:92
  60.3 23.1 %collective-permute-start.37 = (bf16[64,4096]{1,0:T(8,128)(2,1)S(1)}, bf16[64,4096]{1,0:T(8,128)(2,1)S(1)}, u32[]{:S(2)}, u32[]{:S(2)}) collective-permute-start(bf16[64,4096]{1,0:T(8,128)(2,1)S(1)} %get-tuple-element.29), channel_id=1, source_target_pairs={{0,4},{1,5},{2,0},{3,1},{4,8},{5,9},{6,2},{7,3},{8,12},{9,13},{10,... | collective-permute-start | bytes 1572872 | tf_op jit(solution)/shard_map/rs2a/ppermute | solution.py:92
  61.9 10.3 %slice-start.5 = ((s8[6291456]{0:T(1024)(128)(4,1)}), s8[2097152]{0:T(1024)(128)(4,1)S(1)}, s32[]{:S(2)}) async-start(s8[6291456]{0:T(1024)(128)(4,1)} %bitcast.83), calls=%async_computation.6 | async-start | bytes 4194304
  62.0 23.0 %collective-permute-start.44 = (bf16[64,4096]{1,0:T(8,128)(2,1)S(1)}, bf16[64,4096]{1,0:T(8,128)(2,1)S(1)}, u32[]{:S(2)}, u32[]{:S(2)}) collective-permute-start(bf16[64,4096]{1,0:T(8,128)(2,1)S(1)} %get-tuple-element.30), channel_id=1, source_target_pairs={{0,2},{1,3},{2,6},{3,7},{4,0},{5,1},{6,10},{7,11},{8,4},{9,5},{10,... | collective-permute-start | bytes 1572872 | tf_op jit(solution)/shard_map/rs2b/ppermute | solution.py:92
  62.8 9.4 %slice-start.6 = ((s8[6291456]{0:T(1024)(128)(4,1)}), s8[4194304]{0:T(1024)(128)(4,1)S(1)}, s32[]{:S(2)}) async-start(s8[6291456]{0:T(1024)(128)(4,1)} %bitcast.83), calls=%async_computation.7 | async-start | bytes 8388608
  77.5 20.0 %collective-permute-start.30 = (bf16[128,4096]{1,0:T(8,128)(2,1)S(1)}, bf16[128,4096]{1,0:T(8,128)(2,1)S(1)}, u32[]{:S(2)}, u32[]{:S(2)}) collective-permute-start(bf16[128,4096]{1,0:T(8,128)(2,1)S(1)} %slice.436), channel_id=1, source_target_pairs={{0,1},{1,0},{2,3},{3,2},{4,5},{5,4},{6,7},{7,6},{8,9},{9,8},{10,11... | collective-permute-start | bytes 3145736 | tf_op jit(solution)/shard_map/ps3/ppermute | solution.py:92
  77.8 115.5 %collective-permute-start.9 = (bf16[128,4096]{1,0:T(8,128)(2,1)S(1)}, bf16[128,4096]{1,0:T(8,128)(2,1)S(1)}, u32[]{:S(2)}, u32[]{:S(2)}) collective-permute-start(bf16[128,4096]{1,0:T(8,128)(2,1)S(1)} %slice.441), channel_id=1, source_target_pairs={{0,1},{1,0},{2,3},{3,2},{4,5},{5,4},{6,7},{7,6},{8,9},{9,8},{10,11... | collective-permute-start | bytes 3145736 | tf_op jit(solution)/shard_map/ps0/ppermute | solution.py:92
  78.3 6.9 %collective-permute-start.27 = (bf16[64,4096]{1,0:T(8,128)(2,1)}, bf16[64,4096]{1,0:T(8,128)(2,1)S(1)}, u32[]{:S(2)}, u32[]{:S(2)}) collective-permute-start(bf16[64,4096]{1,0:T(8,128)(2,1)} %collective-permute-done.10), channel_id=1, source_target_pairs={{0,1},{1,0},{2,3},{3,2},{4,5},{5,4},{6,7},{7,6},{8,9},{9,8},{10,11... | collective-permute-start | bytes 1572872 | tf_op jit(solution)/shard_map/xs4a/ppermute | solution.py:92
  83.4 15.0 %collective-permute-start.11 = (bf16[64,4096]{1,0:T(8,128)(2,1)}, bf16[64,4096]{1,0:T(8,128)(2,1)S(1)}, u32[]{:S(2)}, u32[]{:S(2)}) collective-permute-start(bf16[64,4096]{1,0:T(8,128)(2,1)} %collective-permute-done.10), channel_id=1, source_target_pairs={{0,4},{1,5},{2,0},{3,1},{4,8},{5,9},{6,2},{7,3},{8,12},{9,13},{10,... | collective-permute-start | bytes 1572872 | tf_op jit(solution)/shard_map/ag5a/ppermute | solution.py:92
  85.0 2.1 %collective-permute-start.28 = (bf16[64,4096]{1,0:T(8,128)(2,1)}, bf16[64,4096]{1,0:T(8,128)(2,1)S(1)}, u32[]{:S(2)}, u32[]{:S(2)}) collective-permute-start(bf16[64,4096]{1,0:T(8,128)(2,1)} %collective-permute-done.14), channel_id=1, source_target_pairs={{0,1},{1,0},{2,3},{3,2},{4,5},{5,4},{6,7},{7,6},{8,9},{9,8},{10,11... | collective-permute-start | bytes 1572872 | tf_op jit(solution)/shard_map/xs4b/ppermute | solution.py:92
  85.3 14.6 %collective-permute-start.15 = (bf16[64,4096]{1,0:T(8,128)(2,1)}, bf16[64,4096]{1,0:T(8,128)(2,1)S(1)}, u32[]{:S(2)}, u32[]{:S(2)}) collective-permute-start(bf16[64,4096]{1,0:T(8,128)(2,1)} %collective-permute-done.14), channel_id=1, source_target_pairs={{0,2},{1,3},{2,6},{3,7},{4,0},{5,1},{6,10},{7,11},{8,4},{9,5},{10,... | collective-permute-start | bytes 1572872 | tf_op jit(solution)/shard_map/ag5b/ppermute | solution.py:92
  87.1 21.2 %collective-permute-start.38 = (bf16[64,4096]{1,0:T(8,128)(2,1)S(1)}, bf16[64,4096]{1,0:T(8,128)(2,1)S(1)}, u32[]{:S(2)}, u32[]{:S(2)}) collective-permute-start(bf16[64,4096]{1,0:T(8,128)(2,1)S(1)} %get-tuple-element.27), channel_id=1, source_target_pairs={{0,4},{1,5},{2,0},{3,1},{4,8},{5,9},{6,2},{7,3},{8,12},{9,13},{10,... | collective-permute-start | bytes 1572872 | tf_op jit(solution)/shard_map/rs3a/ppermute | solution.py:92
  97.5 13.7 %collective-permute-start.45 = (bf16[64,4096]{1,0:T(8,128)(2,1)S(1)}, bf16[64,4096]{1,0:T(8,128)(2,1)S(1)}, u32[]{:S(2)}, u32[]{:S(2)}) collective-permute-start(bf16[64,4096]{1,0:T(8,128)(2,1)S(1)} %get-tuple-element.28), channel_id=1, source_target_pairs={{0,2},{1,3},{2,6},{3,7},{4,0},{5,1},{6,10},{7,11},{8,4},{9,5},{10,... | collective-permute-start | bytes 1572872 | tf_op jit(solution)/shard_map/rs3b/ppermute | solution.py:92
  98.4 24.6 %collective-permute-start.29 = (bf16[128,4096]{1,0:T(8,128)(2,1)S(1)}, bf16[128,4096]{1,0:T(8,128)(2,1)S(1)}, u32[]{:S(2)}, u32[]{:S(2)}) collective-permute-start(bf16[128,4096]{1,0:T(8,128)(2,1)S(1)} %slice.437), channel_id=1, source_target_pairs={{0,1},{1,0},{2,3},{3,2},{4,5},{5,4},{6,7},{7,6},{8,9},{9,8},{10,11... | collective-permute-start | bytes 3145736 | tf_op jit(solution)/shard_map/ps4/ppermute | solution.py:92
  99.9 11.6 %collective-permute-start.24 = (bf16[64,4096]{1,0:T(8,128)(2,1)S(1)}, bf16[64,4096]{1,0:T(8,128)(2,1)S(1)}, u32[]{:S(2)}, u32[]{:S(2)}) collective-permute-start(bf16[64,4096]{1,0:T(8,128)(2,1)S(1)} %collective-permute-done.11), channel_id=1, source_target_pairs={{0,1},{1,0},{2,3},{3,2},{4,5},{5,4},{6,7},{7,6},{8,9},{9,8},{10,11... | collective-permute-start | bytes 1572872 | tf_op jit(solution)/shard_map/xs5a/ppermute | solution.py:92
  108.4 15.6 %collective-permute-start.12 = (bf16[64,4096]{1,0:T(8,128)(2,1)S(1)}, bf16[64,4096]{1,0:T(8,128)(2,1)S(1)}, u32[]{:S(2)}, u32[]{:S(2)}) collective-permute-start(bf16[64,4096]{1,0:T(8,128)(2,1)S(1)} %collective-permute-done.11), channel_id=1, source_target_pairs={{0,4},{1,5},{2,0},{3,1},{4,8},{5,9},{6,2},{7,3},{8,12},{9,13},{10,... | collective-permute-start | bytes 1572872 | tf_op jit(solution)/shard_map/ag6a/ppermute | solution.py:92
  111.2 1.9 collective-permute-start.25
  111.5 14.6 %collective-permute-start.16 = (bf16[64,4096]{1,0:T(8,128)(2,1)S(1)}, bf16[64,4096]{1,0:T(8,128)(2,1)S(1)}, u32[]{:S(2)}, u32[]{:S(2)}) collective-permute-start(bf16[64,4096]{1,0:T(8,128)(2,1)S(1)} %collective-permute-done.15), channel_id=1, source_target_pairs={{0,2},{1,3},{2,6},{3,7},{4,0},{5,1},{6,10},{7,11},{8,4},{9,5},{10,... | collective-permute-start | bytes 1572872 | tf_op jit(solution)/shard_map/ag6b/ppermute | solution.py:92
  113.1 19.2 %collective-permute-start.39 = (bf16[64,4096]{1,0:T(8,128)(2,1)S(1)}, bf16[64,4096]{1,0:T(8,128)(2,1)S(1)}, u32[]{:S(2)}, u32[]{:S(2)}) collective-permute-start(bf16[64,4096]{1,0:T(8,128)(2,1)S(1)} %get-tuple-element.25), channel_id=1, source_target_pairs={{0,4},{1,5},{2,0},{3,1},{4,8},{5,9},{6,2},{7,3},{8,12},{9,13},{10,... | collective-permute-start | bytes 1572872 | tf_op jit(solution)/shard_map/rs4a/ppermute | solution.py:92
  123.1 14.0 %collective-permute-start.46 = (bf16[64,4096]{1,0:T(8,128)(2,1)S(1)}, bf16[64,4096]{1,0:T(8,128)(2,1)S(1)}, u32[]{:S(2)}, u32[]{:S(2)}) collective-permute-start(bf16[64,4096]{1,0:T(8,128)(2,1)S(1)} %get-tuple-element.26), channel_id=1, source_target_pairs={{0,2},{1,3},{2,6},{3,7},{4,0},{5,1},{6,10},{7,11},{8,4},{9,5},{10,... | collective-permute-start | bytes 1572872 | tf_op jit(solution)/shard_map/rs4b/ppermute | solution.py:92
  123.9 25.0 %collective-permute-start.26 = (bf16[128,4096]{1,0:T(8,128)(2,1)S(1)}, bf16[128,4096]{1,0:T(8,128)(2,1)S(1)}, u32[]{:S(2)}, u32[]{:S(2)}) collective-permute-start(bf16[128,4096]{1,0:T(8,128)(2,1)S(1)} %slice.438), channel_id=1, source_target_pairs={{0,1},{1,0},{2,3},{3,2},{4,5},{5,4},{6,7},{7,6},{8,9},{9,8},{10,11... | collective-permute-start | bytes 3145736 | tf_op jit(solution)/shard_map/ps5/ppermute | solution.py:92
  126.1 11.3 %collective-permute-start.21 = (bf16[64,4096]{1,0:T(8,128)(2,1)S(1)}, bf16[64,4096]{1,0:T(8,128)(2,1)S(1)}, u32[]{:S(2)}, u32[]{:S(2)}) collective-permute-start(bf16[64,4096]{1,0:T(8,128)(2,1)S(1)} %collective-permute-done.12), channel_id=1, source_target_pairs={{0,1},{1,0},{2,3},{3,2},{4,5},{5,4},{6,7},{7,6},{8,9},{9,8},{10,11... | collective-permute-start | bytes 1572872 | tf_op jit(solution)/shard_map/xs6a/ppermute | solution.py:92
  132.3 17.5 %collective-permute-start.13 = (bf16[64,4096]{1,0:T(8,128)(2,1)S(1)}, bf16[64,4096]{1,0:T(8,128)(2,1)S(1)}, u32[]{:S(2)}, u32[]{:S(2)}) collective-permute-start(bf16[64,4096]{1,0:T(8,128)(2,1)S(1)} %collective-permute-done.12), channel_id=1, source_target_pairs={{0,4},{1,5},{2,0},{3,1},{4,8},{5,9},{6,2},{7,3},{8,12},{9,13},{10,... | collective-permute-start | bytes 1572872 | tf_op jit(solution)/shard_map/ag7a/ppermute | solution.py:92
  137.1 1.9 collective-permute-start.22
  137.3 14.6 %collective-permute-start.17 = (bf16[64,4096]{1,0:T(8,128)(2,1)S(1)}, bf16[64,4096]{1,0:T(8,128)(2,1)S(1)}, u32[]{:S(2)}, u32[]{:S(2)}) collective-permute-start(bf16[64,4096]{1,0:T(8,128)(2,1)S(1)} %collective-permute-done.16), channel_id=1, source_target_pairs={{0,2},{1,3},{2,6},{3,7},{4,0},{5,1},{6,10},{7,11},{8,4},{9,5},{10,... | collective-permute-start | bytes 1572872 | tf_op jit(solution)/shard_map/ag7b/ppermute | solution.py:92
  139.0 16.3 %collective-permute-start.40 = (bf16[64,4096]{1,0:T(8,128)(2,1)S(1)}, bf16[64,4096]{1,0:T(8,128)(2,1)S(1)}, u32[]{:S(2)}, u32[]{:S(2)}) collective-permute-start(bf16[64,4096]{1,0:T(8,128)(2,1)S(1)} %get-tuple-element.23), channel_id=1, source_target_pairs={{0,4},{1,5},{2,0},{3,1},{4,8},{5,9},{6,2},{7,3},{8,12},{9,13},{10,... | collective-permute-start | bytes 1572872 | tf_op jit(solution)/shard_map/rs5a/ppermute | solution.py:92
  148.9 14.0 %collective-permute-start.47 = (bf16[64,4096]{1,0:T(8,128)(2,1)S(1)}, bf16[64,4096]{1,0:T(8,128)(2,1)S(1)}, u32[]{:S(2)}, u32[]{:S(2)}) collective-permute-start(bf16[64,4096]{1,0:T(8,128)(2,1)S(1)} %get-tuple-element.24), channel_id=1, source_target_pairs={{0,2},{1,3},{2,6},{3,7},{4,0},{5,1},{6,10},{7,11},{8,4},{9,5},{10,... | collective-permute-start | bytes 1572872 | tf_op jit(solution)/shard_map/rs5b/ppermute | solution.py:92
  149.8 24.1 %collective-permute-start.23 = (bf16[128,4096]{1,0:T(8,128)(2,1)S(1)}, bf16[128,4096]{1,0:T(8,128)(2,1)S(1)}, u32[]{:S(2)}, u32[]{:S(2)}) collective-permute-start(bf16[128,4096]{1,0:T(8,128)(2,1)S(1)} %slice.439), channel_id=1, source_target_pairs={{0,1},{1,0},{2,3},{3,2},{4,5},{5,4},{6,7},{7,6},{8,9},{9,8},{10,11... | collective-permute-start | bytes 3145736 | tf_op jit(solution)/shard_map/ps6/ppermute | solution.py:92
  151.9 12.7 %collective-permute-start.18 = (bf16[64,4096]{1,0:T(8,128)(2,1)S(1)}, bf16[64,4096]{1,0:T(8,128)(2,1)S(1)}, u32[]{:S(2)}, u32[]{:S(2)}) collective-permute-start(bf16[64,4096]{1,0:T(8,128)(2,1)S(1)} %collective-permute-done.13), channel_id=1, source_target_pairs={{0,1},{1,0},{2,3},{3,2},{4,5},{5,4},{6,7},{7,6},{8,9},{9,8},{10,11... | collective-permute-start | bytes 1572872 | tf_op jit(solution)/shard_map/xs7a/ppermute | solution.py:92
  155.3 10.0 %collective-permute-start.19 = (bf16[64,4096]{1,0:T(8,128)(2,1)S(1)}, bf16[64,4096]{1,0:T(8,128)(2,1)S(1)}, u32[]{:S(2)}, u32[]{:S(2)}) collective-permute-start(bf16[64,4096]{1,0:T(8,128)(2,1)S(1)} %collective-permute-done.17), channel_id=1, source_target_pairs={{0,1},{1,0},{2,3},{3,2},{4,5},{5,4},{6,7},{7,6},{8,9},{9,8},{10,11... | collective-permute-start | bytes 1572872 | tf_op jit(solution)/shard_map/xs7b/ppermute | solution.py:92
  163.2 13.1 %collective-permute-start.41 = (bf16[64,4096]{1,0:T(8,128)(2,1)S(1)}, bf16[64,4096]{1,0:T(8,128)(2,1)S(1)}, u32[]{:S(2)}, u32[]{:S(2)}) collective-permute-start(bf16[64,4096]{1,0:T(8,128)(2,1)S(1)} %get-tuple-element.21), channel_id=1, source_target_pairs={{0,4},{1,5},{2,0},{3,1},{4,8},{5,9},{6,2},{7,3},{8,12},{9,13},{10,... | collective-permute-start | bytes 1572872 | tf_op jit(solution)/shard_map/rs6a/ppermute | solution.py:92
  164.7 13.3 %collective-permute-start.48 = (bf16[64,4096]{1,0:T(8,128)(2,1)S(1)}, bf16[64,4096]{1,0:T(8,128)(2,1)S(1)}, u32[]{:S(2)}, u32[]{:S(2)}) collective-permute-start(bf16[64,4096]{1,0:T(8,128)(2,1)S(1)} %get-tuple-element.22), channel_id=1, source_target_pairs={{0,2},{1,3},{2,6},{3,7},{4,0},{5,1},{6,10},{7,11},{8,4},{9,5},{10,... | collective-permute-start | bytes 1572872 | tf_op jit(solution)/shard_map/rs6b/ppermute | solution.py:92
  173.8 6.4 %collective-permute-start.20 = (bf16[128,4096]{1,0:T(8,128)(2,1)S(1)}, bf16[128,4096]{1,0:T(8,128)(2,1)S(1)}, u32[]{:S(2)}, u32[]{:S(2)}) collective-permute-start(bf16[128,4096]{1,0:T(8,128)(2,1)S(1)} %slice.440), channel_id=1, source_target_pairs={{0,1},{1,0},{2,3},{3,2},{4,5},{5,4},{6,7},{7,6},{8,9},{9,8},{10,11... | collective-permute-start | bytes 3145736 | tf_op jit(solution)/shard_map/ps7/ppermute | solution.py:92
  178.2 12.4 %collective-permute-start.42 = (bf16[64,4096]{1,0:T(8,128)(2,1)S(1)}, bf16[64,4096]{1,0:T(8,128)(2,1)S(1)}, u32[]{:S(2)}, u32[]{:S(2)}) collective-permute-start(bf16[64,4096]{1,0:T(8,128)(2,1)S(1)} %get-tuple-element.19), channel_id=1, source_target_pairs={{0,4},{1,5},{2,0},{3,1},{4,8},{5,9},{6,2},{7,3},{8,12},{9,13},{10,... | collective-permute-start | bytes 1572872 | tf_op jit(solution)/shard_map/rs7a/ppermute | solution.py:92
  178.6 12.3 %collective-permute-start.49 = (bf16[64,4096]{1,0:T(8,128)(2,1)S(1)}, bf16[64,4096]{1,0:T(8,128)(2,1)S(1)}, u32[]{:S(2)}, u32[]{:S(2)}) collective-permute-start(bf16[64,4096]{1,0:T(8,128)(2,1)S(1)} %get-tuple-element.20), channel_id=1, source_target_pairs={{0,2},{1,3},{2,6},{3,7},{4,0},{5,1},{6,10},{7,11},{8,4},{9,5},{10,... | collective-permute-start | bytes 1572872 | tf_op jit(solution)/shard_map/rs7b/ppermute | solution.py:92
  191.2 11.4 %collective-permute-start.43 = (bf16[64,4096]{1,0:T(8,128)(2,1)S(1)}, bf16[64,4096]{1,0:T(8,128)(2,1)S(1)}, u32[]{:S(2)}, u32[]{:S(2)}) collective-permute-start(bf16[64,4096]{1,0:T(8,128)(2,1)S(1)} %get-tuple-element.17), channel_id=1, source_target_pairs={{0,4},{1,5},{2,0},{3,1},{4,8},{5,9},{6,2},{7,3},{8,12},{9,13},{10,... | collective-permute-start | bytes 1572872 | tf_op jit(solution)/shard_map/rs0a/ppermute | solution.py:92
  192.2 10.9 %collective-permute-start.50 = (bf16[64,4096]{1,0:T(8,128)(2,1)S(1)}, bf16[64,4096]{1,0:T(8,128)(2,1)S(1)}, u32[]{:S(2)}, u32[]{:S(2)}) collective-permute-start(bf16[64,4096]{1,0:T(8,128)(2,1)S(1)} %get-tuple-element.18), channel_id=1, source_target_pairs={{0,2},{1,3},{2,6},{3,7},{4,0},{5,1},{6,10},{7,11},{8,4},{9,5},{10,... | collective-permute-start | bytes 1572872 | tf_op jit(solution)/shard_map/rs0b/ppermute | solution.py:92

commit v4 on v3

--- a/solution.py
+++ b/solution.py
@@ -129,11 +129,13 @@
             part_a, part_b = part[:half], part[half:]
         if turn != 1:
             sums_a, sums_b = send(sums_a, forth, f"rs{step}a"), send(sums_b, back, f"rs{step}b")
+            if step == 0:
+                got = jnp.concatenate([sums_a, sums_b], axis=0)
+                return (part + got.astype(jnp.float32)).astype(jnp.bfloat16)
             with jax.named_scope(f"add{step}"):
                 part_a, part_b = part_a + sums_a.astype(jnp.float32), part_b + sums_b.astype(jnp.float32)
         with jax.named_scope(f"add{step}"):
             sums_a, sums_b = part_a.astype(jnp.bfloat16), part_b.astype(jnp.bfloat16)
-    return jnp.concatenate([sums_a, sums_b], axis=0)
 
 
 def prefix(part):

time: 205 us -> 205 us (level)
  no operation moved by 1% of the time
where the time goes in v4:
time: 205 us; the launch traced here: 204 us
  waiting for transfers between devices  86.3 us (42%)
  matrix products  64 us (31%)
  starting transfers between devices  39 us (19%)
  other arithmetic  6.87 us (3%)
  local copies, waits for them, and re-layouts  5.6 us (3%)
    ppermute x51, waiting for transfers between devices, send(): return lax.ppermute(value, AXIS, where)  85.1 us
    dot_general x7, matrix products, expert_block(): jnp.dot(inputs, first_weights, preferred_element_type=jnp.float32)  45.8 us
    ppermute x51, starting transfers between devices, send(): return lax.ppermute(value, AXIS, where)  32.7 us
    dot_general x7, matrix products, expert_block(): jnp.dot(hidden, second_weights, preferred_element_type=jnp.float32)  18.1 us
    all_to_all x1, starting transfers between devices, incoming_gates(): lax.all_to_all(outgoing[:, None], AXIS, split_axis=0, concat_axis=0, tile...  6.38 us
  transfers between devices with their start and end apart: 52, of which 27 were waited for; matrix products, arithmetic and copies ran while one was open for 36% of the time, Pallas kernels for 1%

profile of v4, /device:TPU:0, one launch (start us, length us, event | category | flops | bytes accessed | tf_op | source)
XLA Modules:
  0.0 204.4 jit_solution(5512138162259286158)
XLA Ops:
  0.0 1.3 fusion.183
  1.3 3.1 %collective-permute-start = (bf16[64,4096]{1,0:T(8,128)(2,1)S(1)}, bf16[64,4096]{1,0:T(8,128)(2,1)S(1)}, u32[]{:S(2)}, u32[]{:S(2)}) collective-permute-start(bf16[64,4096]{1,0:T(8,128)(2,1)S(1)} %get-tuple-element.30), channel_id=1, source_target_pairs={{0,4},{1,5},{2,0},{3,1},{4,8},{5,9},{6,2},{7,3},{8,12},{9,13},{10,... | collective-permute-start | bytes 1572872 | tf_op jit(solution)/shard_map/ag1a/ppermute | solution.py:92
  4.4 1.4 select_reduce_fusion
  5.8 6.4 %all-to-all-start = ((f32[16,1,128]{2,1,0:T(1,128)}), f32[16,1,128]{2,1,0:T(1,128)S(1)}, u32[]{:S(2)}, u32[]{:S(2)}) async-start(f32[16,1,128]{2,1,0:T(1,128)} %bitcast.6), calls=%async_computation | async-start | bytes 16384 | tf_op jit(solution)/shard_map/meta/all_to_all | solution.py:25
  12.5 3.7 %collective-permute-done.refs_0_ = bf16[64,4096]{1,0:T(8,128)(2,1)S(1)} collective-permute-done((bf16[64,4096]{1,0:T(8,128)(2,1)S(1)}, bf16[64,4096]{1,0:T(8,128)(2,1)S(1)}, u32[]{:S(2)}, u32[]{:S(2)}) %collective-permute-start) | collective-permute-done | bytes 524320 | tf_op jit(solution)/shard_map/ag1a/ppermute | solution.py:92
  16.2 1.9 collective-permute-start.1
  18.6 1.2 all-to-all-done
  19.8 0.6 copy-done.1
  20.4 2.0 meta.1
  22.4 2.3 %slice_reduce_fusion = (f32[256]{0:T(256)S(1)}, f32[256]{0:T(256)S(1)}, f32[256]{0:T(256)S(1)}, f32[256]{0:T(256)S(1)}, f32[256]{0:T(256)S(1)}, /*index=5*/f32[256]{0:T(256)S(1)}, f32[256]{0:T(256)S(1)}, f32[256]{0:T(256)S(1)}) fusion(f32[256,8]{1,0:T(8,128)} %meta.1), kind=kLoop, calls=%fused_computation.155 | loop fusion | bytes 16384 | tf_op jit(solution)/shard_map/kernel1/slice | solution.py:124
  24.7 4.7 %collective-permute-done.1 = bf16[64,4096]{1,0:T(8,128)(2,1)S(1)} collective-permute-done((bf16[64,4096]{1,0:T(8,128)(2,1)S(1)}, bf16[64,4096]{1,0:T(8,128)(2,1)S(1)}, u32[]{:S(2)}, u32[]{:S(2)}) %collective-permute-start.1) | collective-permute-done | bytes 524320 | tf_op jit(solution)/shard_map/ag2a/ppermute | solution.py:92
  29.5 3.2 %collective-permute-done.4 = bf16[64,4096]{1,0:T(8,128)(2,1)S(1)} collective-permute-done((bf16[64,4096]{1,0:T(8,128)(2,1)}, bf16[64,4096]{1,0:T(8,128)(2,1)S(1)}, u32[]{:S(2)}, u32[]{:S(2)}) %collective-permute-start.4) | collective-permute-done | bytes 524320 | tf_op jit(solution)/shard_map/ag2b/ppermute | solution.py:92
  32.7 7.0 %fusion = f32[256,1536]{1,0:T(8,128)S(1)} fusion(bf16[1,4096,1536]{2,1,0:T(8,128)(2,1)} %param.11, bf16[64,4096]{1,0:T(8,128)(2,1)} %collective-permute-done.35, bf16[64,4096]{1,0:T(8,128)(2,1)S(1)} %collective-permute-done.34, bf16[64,4096]{1,0:T(8,128)(2,1)} %collective-permute-done.3.refs_1_, bf16[64,4096]{1,0:T(8,128)(2,1)} %copy-done.2), kind=kOutput, calls=%fused_computation | convolution fusion | flops 3229614080 | bytes 16252928 | tf_op jit(solution)/shard_map/kernel1/dot_general | solution.py:15
  39.8 1.9 broadcast_multiply_fusion
  42.4 1.6 collective-permute-start.2
  44.4 3.4 %fusion.2 = f32[256,1536]{1,0:T(8,128)S(1)} fusion(bf16[1,4096,1536]{2,1,0:T(8,128)(2,1)S(1)} %bitcast.80, bf16[64,4096]{1,0:T(8,128)(2,1)S(1)} %collective-permute-done.32, bf16[64,4096]{1,0:T(8,128)(2,1)S(1)} %collective-permute-done.31, bf16[64,4096]{1,0:T(8,128)(2,1)S(1)} %collective-permute-done.4, bf16[64,4096]{1,0:T(8,128)(2,1)S(1)} %collective-permute-done.1), kind=kOutput, calls=%fused_computation.2 | convolution fusion | flops 3229614080 | bytes 16252928 | tf_op jit(solution)/shard_map/kernel2/dot_general | solution.py:15
  47.8 4.7 %broadcast_multiply_fusion.1 = f32[256,4096]{1,0:T(8,128)S(1)} fusion(f32[256]{0:T(256)S(1)} %get-tuple-element.6, bf16[1,768,4096]{2,1,0:T(8,128)(2,1)} %param.12, f32[256,1536]{1,0:T(8,128)S(1)} %fusion.2), kind=kOutput, calls=%fused_computation.105 | convolution fusion | flops 1614938112 | bytes 12059648 | tf_op jit(solution)/shard_map/kernel2/dot_general | solution.py:19
  52.7 3.5 %collective-permute-done.2 = bf16[64,4096]{1,0:T(8,128)(2,1)S(1)} collective-permute-done((bf16[64,4096]{1,0:T(8,128)(2,1)S(1)}, bf16[64,4096]{1,0:T(8,128)(2,1)S(1)}, u32[]{:S(2)}, u32[]{:S(2)}) %collective-permute-start.2) | collective-permute-done | bytes 524320 | tf_op jit(solution)/shard_map/ag3a/ppermute | solution.py:92
  56.3 1.4 collective-permute-done.5
  57.8 1.6 collective-permute-start.10
  60.3 1.6 collective-permute-start.37
  62.0 0.7 collective-permute-start.44
  62.8 9.4 %fusion.12 = f32[512,1536]{1,0:T(8,128)S(1)} fusion(bf16[512,4096]{1,0:T(8,128)(2,1)S(1)} %constant_dynamic-update-slice_fusion, bf16[1,4096,1536]{2,1,0:T(8,128)(2,1)} %param.11), kind=kOutput, calls=%fused_computation.12 | convolution fusion | flops 6442450944 | bytes 19922944 | tf_op jit(solution)/shard_map/kernel3/dot_general | solution.py:15
  72.2 3.8 %fusion.28 = bf16[512,4096]{1,0:T(8,128)(2,1)S(1)} fusion(bf16[1,768,4096]{2,1,0:T(8,128)(2,1)S(1)} %bitcast.84, f32[512,1536]{1,0:T(8,128)S(1)} %fusion.12), kind=kOutput, calls=%fused_computation.28 | convolution fusion | flops 3225681920 | bytes 13631488 | tf_op jit(solution)/shard_map/kernel3/dot_general | solution.py:19
  76.0 1.2 convert_multiply_fusion
  78.4 5.0 %collective-permute-done.37 = bf16[64,4096]{1,0:T(8,128)(2,1)S(1)} collective-permute-done((bf16[64,4096]{1,0:T(8,128)(2,1)S(1)}, bf16[64,4096]{1,0:T(8,128)(2,1)S(1)}, u32[]{:S(2)}, u32[]{:S(2)}) %collective-permute-start.37) | collective-permute-done | bytes 524320 | tf_op jit(solution)/shard_map/rs2a/ppermute | solution.py:92
  83.4 1.5 collective-permute-start.11
  85.8 1.3 collective-permute-done.28
  87.1 1.5 collective-permute-start.38
  88.6 6.7 %fusion.4 = f32[256,1536]{1,0:T(8,128)S(1)} fusion(bf16[1,4096,1536]{2,1,0:T(8,128)(2,1)} %param.11, bf16[64,4096]{1,0:T(8,128)(2,1)S(1)} %collective-permute-done.28, bf16[64,4096]{1,0:T(8,128)(2,1)S(1)} %collective-permute-done.27, bf16[64,4096]{1,0:T(8,128)(2,1)} %collective-permute-done.14, bf16[64,4096]{1,0:T(8,128)(2,1)} %collective-permute-done.10), kind=kOutput, calls=%fused_computation.4 | convolution fusion | flops 3229614080 | bytes 16252928 | tf_op jit(solution)/shard_map/kernel4/dot_general | solution.py:15
  95.4 1.9 broadcast_multiply_fusion.2
  98.4 1.4 collective-permute-done.15
  99.9 8.5 %collective-permute-done.38 = bf16[64,4096]{1,0:T(8,128)(2,1)S(1)} collective-permute-done((bf16[64,4096]{1,0:T(8,128)(2,1)S(1)}, bf16[64,4096]{1,0:T(8,128)(2,1)S(1)}, u32[]{:S(2)}, u32[]{:S(2)}) %collective-permute-start.38) | collective-permute-done | bytes 524320 | tf_op jit(solution)/shard_map/rs3a/ppermute | solution.py:92
  108.4 1.5 collective-permute-start.12
  109.9 1.3 collective-permute-done.45
  112.0 1.1 collective-permute-done.25
  113.1 1.4 collective-permute-start.39
  114.5 6.4 %fusion.6 = f32[256,1536]{1,0:T(8,128)S(1)} fusion(bf16[1,4096,1536]{2,1,0:T(8,128)(2,1)} %param.11, bf16[64,4096]{1,0:T(8,128)(2,1)S(1)} %collective-permute-done.25, bf16[64,4096]{1,0:T(8,128)(2,1)S(1)} %collective-permute-done.24, bf16[64,4096]{1,0:T(8,128)(2,1)S(1)} %collective-permute-done.15, bf16[64,4096]{1,0:T(8,128)(2,1)S(1)} %collective-permute-done.11), kind=kOutput, calls=%fused_computation.6 | convolution fusion | flops 3229614080 | bytes 16252928 | tf_op jit(solution)/shard_map/kernel5/dot_general | solution.py:15
  121.0 1.9 broadcast_multiply_fusion.3
  123.1 0.7 collective-permute-start.46
  124.0 2.0 collective-permute-done.16
  126.1 6.2 %collective-permute-done.39 = bf16[64,4096]{1,0:T(8,128)(2,1)S(1)} collective-permute-done((bf16[64,4096]{1,0:T(8,128)(2,1)S(1)}, bf16[64,4096]{1,0:T(8,128)(2,1)S(1)}, u32[]{:S(2)}, u32[]{:S(2)}) %collective-permute-start.39) | collective-permute-done | bytes 524320 | tf_op jit(solution)/shard_map/rs4a/ppermute | solution.py:92
  132.3 1.5 collective-permute-start.13
  133.8 3.3 %collective-permute-done.46 = bf16[64,4096]{1,0:T(8,128)(2,1)S(1)} collective-permute-done((bf16[64,4096]{1,0:T(8,128)(2,1)S(1)}, bf16[64,4096]{1,0:T(8,128)(2,1)S(1)}, u32[]{:S(2)}, u32[]{:S(2)}) %collective-permute-start.46) | collective-permute-done | bytes 524320 | tf_op jit(solution)/shard_map/rs4b/ppermute | solution.py:92
  137.9 1.1 collective-permute-done.22
  139.0 1.4 collective-permute-start.40
  140.4 6.4 %fusion.8 = f32[256,1536]{1,0:T(8,128)S(1)} fusion(bf16[1,4096,1536]{2,1,0:T(8,128)(2,1)} %param.11, bf16[64,4096]{1,0:T(8,128)(2,1)S(1)} %collective-permute-done.22, bf16[64,4096]{1,0:T(8,128)(2,1)S(1)} %collective-permute-done.21, bf16[64,4096]{1,0:T(8,128)(2,1)S(1)} %collective-permute-done.16, bf16[64,4096]{1,0:T(8,128)(2,1)S(1)} %collective-permute-done.12), kind=kOutput, calls=%fused_computation.8 | convolution fusion | flops 3229614080 | bytes 16252928 | tf_op jit(solution)/shard_map/kernel6/dot_general | solution.py:15
  146.9 1.9 broadcast_multiply_fusion.4
  148.9 0.7 collective-permute-start.47
  149.9 2.0 collective-permute-done.17
  152.0 3.3 %collective-permute-done.40 = bf16[64,4096]{1,0:T(8,128)(2,1)S(1)} collective-permute-done((bf16[64,4096]{1,0:T(8,128)(2,1)S(1)}, bf16[64,4096]{1,0:T(8,128)(2,1)S(1)}, u32[]{:S(2)}, u32[]{:S(2)}) %collective-permute-start.40) | collective-permute-done | bytes 524320 | tf_op jit(solution)/shard_map/rs5a/ppermute | solution.py:92
  155.3 7.7 %collective-permute-done.47 = bf16[64,4096]{1,0:T(8,128)(2,1)S(1)} collective-permute-done((bf16[64,4096]{1,0:T(8,128)(2,1)S(1)}, bf16[64,4096]{1,0:T(8,128)(2,1)S(1)}, u32[]{:S(2)}, u32[]{:S(2)}) %collective-permute-start.47) | collective-permute-done | bytes 524320 | tf_op jit(solution)/shard_map/rs5b/ppermute | solution.py:92
  163.2 1.5 collective-permute-start.41
  164.7 0.6 collective-permute-start.48
  165.3 6.4 %fusion.10 = f32[256,1536]{1,0:T(8,128)S(1)} fusion(bf16[1,4096,1536]{2,1,0:T(8,128)(2,1)} %param.11, bf16[64,4096]{1,0:T(8,128)(2,1)S(1)} %collective-permute-done.19, bf16[64,4096]{1,0:T(8,128)(2,1)S(1)} %collective-permute-done.18, bf16[64,4096]{1,0:T(8,128)(2,1)S(1)} %collective-permute-done.17, bf16[64,4096]{1,0:T(8,128)(2,1)S(1)} %collective-permute-done.13), kind=kOutput, calls=%fused_computation.10 | convolution fusion | flops 3229614080 | bytes 16252928 | tf_op jit(solution)/shard_map/kernel7/dot_general | solution.py:15
  171.7 1.9 broadcast_multiply_fusion.5
  174.1 2.2 %collective-permute-done.41 = bf16[64,4096]{1,0:T(8,128)(2,1)S(1)} collective-permute-done((bf16[64,4096]{1,0:T(8,128)(2,1)S(1)}, bf16[64,4096]{1,0:T(8,128)(2,1)S(1)}, u32[]{:S(2)}, u32[]{:S(2)}) %collective-permute-start.41) | collective-permute-done | bytes 524320 | tf_op jit(solution)/shard_map/rs6a/ppermute | solution.py:92
  176.4 1.6 collective-permute-done.48
  178.6 1.7 collective-permute-start.49
  180.5 10.1 %collective-permute-done.42 = bf16[64,4096]{1,0:T(8,128)(2,1)S(1)} collective-permute-done((bf16[64,4096]{1,0:T(8,128)(2,1)S(1)}, bf16[64,4096]{1,0:T(8,128)(2,1)S(1)}, u32[]{:S(2)}, u32[]{:S(2)}) %collective-permute-start.42) | collective-permute-done | bytes 524320 | tf_op jit(solution)/shard_map/rs7a/ppermute | solution.py:92
  191.2 1.0 collective-permute-start.43
  192.2 1.1 collective-permute-start.50
  193.2 9.4 %collective-permute-done.43 = bf16[64,4096]{1,0:T(8,128)(2,1)S(1)} collective-permute-done((bf16[64,4096]{1,0:T(8,128)(2,1)S(1)}, bf16[64,4096]{1,0:T(8,128)(2,1)S(1)}, u32[]{:S(2)}, u32[]{:S(2)}) %collective-permute-start.43) | collective-permute-done | bytes 524320 | tf_op jit(solution)/shard_map/rs0a/ppermute | solution.py:92
  203.0 1.4 fusion.69
  (111 shorter events, 11.5 us)
Async XLA Ops:
  1.3 15.0 %collective-permute-start = (bf16[64,4096]{1,0:T(8,128)(2,1)S(1)}, bf16[64,4096]{1,0:T(8,128)(2,1)S(1)}, u32[]{:S(2)}, u32[]{:S(2)}) collective-permute-start(bf16[64,4096]{1,0:T(8,128)(2,1)S(1)} %get-tuple-element.30), channel_id=1, source_target_pairs={{0,4},{1,5},{2,0},{3,1},{4,8},{5,9},{6,2},{7,3},{8,12},{9,13},{10,... | collective-permute-start | bytes 1572872 | tf_op jit(solution)/shard_map/ag1a/ppermute | solution.py:92
  4.3 13.7 %collective-permute-start.3 = (bf16[64,4096]{1,0:T(8,128)(2,1)S(1)}, bf16[64,4096]{1,0:T(8,128)(2,1)}, u32[]{:S(2)}, u32[]{:S(2)}) collective-permute-start(bf16[64,4096]{1,0:T(8,128)(2,1)S(1)} %get-tuple-element.29), channel_id=1, source_target_pairs={{0,2},{1,3},{2,6},{3,7},{4,0},{5,1},{6,10},{7,11},{8,4},{9,5},{10,... | collective-permute-start | bytes 1572872 | tf_op jit(solution)/shard_map/ag1b/ppermute | solution.py:92
  5.8 14.0 %all-to-all-start = ((f32[16,1,128]{2,1,0:T(1,128)}), f32[16,1,128]{2,1,0:T(1,128)S(1)}, u32[]{:S(2)}, u32[]{:S(2)}) async-start(f32[16,1,128]{2,1,0:T(1,128)} %bitcast.6), calls=%async_computation | async-start | bytes 16384 | tf_op jit(solution)/shard_map/meta/all_to_all | solution.py:25
  12.1 49.9 %collective-permute-start.8 = (bf16[128,4096]{1,0:T(8,128)(2,1)}, bf16[128,4096]{1,0:T(8,128)(2,1)S(1)}, u32[]{:S(2)}, u32[]{:S(2)}) collective-permute-start(bf16[128,4096]{1,0:T(8,128)(2,1)} %param.8), channel_id=1, source_target_pairs={{0,1},{1,0},{2,3},{3,2},{4,5},{5,4},{6,7},{7,6},{8,9},{9,8},{10,11... | collective-permute-start | bytes 3145736 | tf_op jit(solution)/shard_map/kernel3/xs0/ppermute | solution.py:92
  16.2 3.6 %copy-start.2 = (bf16[64,4096]{1,0:T(8,128)(2,1)}, bf16[64,4096]{1,0:T(8,128)(2,1)S(1)}, u32[]{:S(2)}) copy-start(bf16[64,4096]{1,0:T(8,128)(2,1)S(1)} %collective-permute-done.refs_0_) | copy-start | bytes 1572868
  16.2 13.2 %collective-permute-start.1 = (bf16[64,4096]{1,0:T(8,128)(2,1)S(1)}, bf16[64,4096]{1,0:T(8,128)(2,1)S(1)}, u32[]{:S(2)}, u32[]{:S(2)}) collective-permute-start(bf16[64,4096]{1,0:T(8,128)(2,1)S(1)} %collective-permute-done.refs_0_), channel_id=1, source_target_pairs={{0,4},{1,5},{2,0},{3,1},{4,8},{5,9},{6,2},{7,3},{8,12},{9,13},{10,... | collective-permute-start | bytes 1572872 | tf_op jit(solution)/shard_map/ag2a/ppermute | solution.py:92
  18.1 14.6 %collective-permute-start.34 = (bf16[64,4096]{1,0:T(8,128)(2,1)S(1)}, bf16[64,4096]{1,0:T(8,128)(2,1)S(1)}, u32[]{:S(2)}, u32[]{:S(2)}) collective-permute-start(bf16[64,4096]{1,0:T(8,128)(2,1)S(1)} %collective-permute-done.refs_0_), channel_id=1, source_target_pairs={{0,1},{1,0},{2,3},{3,2},{4,5},{5,4},{6,7},{7,6},{8,9},{9,8},{10,11... | collective-permute-start | bytes 1572872 | tf_op jit(solution)/shard_map/xs1a/ppermute | solution.py:92
  18.1 14.5 %collective-permute-start.4 = (bf16[64,4096]{1,0:T(8,128)(2,1)}, bf16[64,4096]{1,0:T(8,128)(2,1)S(1)}, u32[]{:S(2)}, u32[]{:S(2)}) collective-permute-start(bf16[64,4096]{1,0:T(8,128)(2,1)} %collective-permute-done.3.refs_1_), channel_id=1, source_target_pairs={{0,2},{1,3},{2,6},{3,7},{4,0},{5,1},{6,10},{7,11},{8,4},{9,5},{10,... | collective-permute-start | bytes 1572872 | tf_op jit(solution)/shard_map/ag2b/ppermute | solution.py:92
  18.3 14.4 %collective-permute-start.35 = (bf16[64,4096]{1,0:T(8,128)(2,1)}, bf16[64,4096]{1,0:T(8,128)(2,1)}, u32[]{:S(2)}, u32[]{:S(2)}) collective-permute-start(bf16[64,4096]{1,0:T(8,128)(2,1)} %collective-permute-done.3.refs_1_), channel_id=1, source_target_pairs={{0,1},{1,0},{2,3},{3,2},{4,5},{5,4},{6,7},{7,6},{8,9},{9,8},{10,11... | collective-permute-start | bytes 1572872 | tf_op jit(solution)/shard_map/xs1b/ppermute | solution.py:92
  19.8 0.6 copy-start.1
  22.4 17.3 %slice-start.3 = ((s8[6291456]{0:T(1024)(128)(4,1)}), s8[4194304]{0:T(1024)(128)(4,1)S(1)}, s32[]{:S(2)}) async-start(s8[6291456]{0:T(1024)(128)(4,1)} %bitcast.81), calls=%async_computation.4 | async-start | bytes 8388608
  24.7 15.0 %slice-start.4 = ((s8[6291456]{0:T(1024)(128)(4,1)}), s8[2097152]{0:T(1024)(128)(4,1)S(1)}, s32[]{:S(2)}) async-start(s8[6291456]{0:T(1024)(128)(4,1)} %bitcast.81), calls=%async_computation.5 | async-start | bytes 4194304
  29.5 14.6 %collective-permute-start.31 = (bf16[64,4096]{1,0:T(8,128)(2,1)S(1)}, bf16[64,4096]{1,0:T(8,128)(2,1)S(1)}, u32[]{:S(2)}, u32[]{:S(2)}) collective-permute-start(bf16[64,4096]{1,0:T(8,128)(2,1)S(1)} %collective-permute-done.1), channel_id=1, source_target_pairs={{0,1},{1,0},{2,3},{3,2},{4,5},{5,4},{6,7},{7,6},{8,9},{9,8},{10,11... | collective-permute-start | bytes 1572872 | tf_op jit(solution)/shard_map/xs2a/ppermute | solution.py:92
  32.6 11.8 %collective-permute-start.32 = (bf16[64,4096]{1,0:T(8,128)(2,1)S(1)}, bf16[64,4096]{1,0:T(8,128)(2,1)S(1)}, u32[]{:S(2)}, u32[]{:S(2)}) collective-permute-start(bf16[64,4096]{1,0:T(8,128)(2,1)S(1)} %collective-permute-done.4), channel_id=1, source_target_pairs={{0,1},{1,0},{2,3},{3,2},{4,5},{5,4},{6,7},{7,6},{8,9},{9,8},{10,11... | collective-permute-start | bytes 1572872 | tf_op jit(solution)/shard_map/xs2b/ppermute | solution.py:92
  32.6 11.8 %slice-start = ((s8[12582912]{0:T(1024)(128)(4,1)}), s8[4194304]{0:T(1024)(128)(4,1)S(1)}, s32[]{:S(2)}) async-start(s8[12582912]{0:T(1024)(128)(4,1)} %bitcast.79), calls=%async_computation.1 | async-start | bytes 8388608
  32.7 11.8 %slice-start.1 = ((s8[12582912]{0:T(1024)(128)(4,1)}), s8[4194304]{0:T(1024)(128)(4,1)S(1)}, s32[]{:S(2)}) async-start(s8[12582912]{0:T(1024)(128)(4,1)} %bitcast.79), calls=%async_computation.2 | async-start | bytes 8388608
  39.7 4.7 %slice-start.2 = ((s8[12582912]{0:T(1024)(128)(4,1)}), s8[4194304]{0:T(1024)(128)(4,1)S(1)}, s32[]{:S(2)}) async-start(s8[12582912]{0:T(1024)(128)(4,1)} %bitcast.79), calls=%async_computation.3 | async-start | bytes 8388608
  41.8 15.9 %collective-permute-start.36 = (bf16[128,4096]{1,0:T(8,128)(2,1)S(1)}, bf16[128,4096]{1,0:T(8,128)(2,1)S(1)}, u32[]{:S(2)}, u32[]{:S(2)}) collective-permute-start(bf16[128,4096]{1,0:T(8,128)(2,1)S(1)} %slice.422), channel_id=1, source_target_pairs={{0,1},{1,0},{2,3},{3,2},{4,5},{5,4},{6,7},{7,6},{8,9},{9,8},{10,11... | collective-permute-start | bytes 3145736 | tf_op jit(solution)/shard_map/ps1/ppermute | solution.py:92
  42.4 13.9 %collective-permute-start.2 = (bf16[64,4096]{1,0:T(8,128)(2,1)S(1)}, bf16[64,4096]{1,0:T(8,128)(2,1)S(1)}, u32[]{:S(2)}, u32[]{:S(2)}) collective-permute-start(bf16[64,4096]{1,0:T(8,128)(2,1)S(1)} %collective-permute-done.1), channel_id=1, source_target_pairs={{0,4},{1,5},{2,0},{3,1},{4,8},{5,9},{6,2},{7,3},{8,12},{9,13},{10,... | collective-permute-start | bytes 1572872 | tf_op jit(solution)/shard_map/ag3a/ppermute | solution.py:92
  44.0 13.6 %collective-permute-start.5 = (bf16[64,4096]{1,0:T(8,128)(2,1)S(1)}, bf16[64,4096]{1,0:T(8,128)(2,1)S(1)}, u32[]{:S(2)}, u32[]{:S(2)}) collective-permute-start(bf16[64,4096]{1,0:T(8,128)(2,1)S(1)} %collective-permute-done.4), channel_id=1, source_target_pairs={{0,2},{1,3},{2,6},{3,7},{4,0},{5,1},{6,10},{7,11},{8,4},{9,5},{10,... | collective-permute-start | bytes 1572872 | tf_op jit(solution)/shard_map/ag3b/ppermute | solution.py:92
  52.6 24.8 %collective-permute-start.33 = (bf16[128,4096]{1,0:T(8,128)(2,1)S(1)}, bf16[128,4096]{1,0:T(8,128)(2,1)S(1)}, u32[]{:S(2)}, u32[]{:S(2)}) collective-permute-start(bf16[128,4096]{1,0:T(8,128)(2,1)S(1)} %slice.423), channel_id=1, source_target_pairs={{0,1},{1,0},{2,3},{3,2},{4,5},{5,4},{6,7},{7,6},{8,9},{9,8},{10,11... | collective-permute-start | bytes 3145736 | tf_op jit(solution)/shard_map/ps2/ppermute | solution.py:92
  56.3 3.4 %collective-permute-start.6 = (bf16[64,4096]{1,0:T(8,128)(2,1)S(1)}, bf16[64,4096]{1,0:T(8,128)(2,1)S(1)}, u32[]{:S(2)}, u32[]{:S(2)}) collective-permute-start(bf16[64,4096]{1,0:T(8,128)(2,1)S(1)} %collective-permute-done.2), channel_id=1, source_target_pairs={{0,1},{1,0},{2,3},{3,2},{4,5},{5,4},{6,7},{7,6},{8,9},{9,8},{10,11... | collective-permute-start | bytes 1572872 | tf_op jit(solution)/shard_map/xs3a/ppermute | solution.py:92
  57.6 2.6 %collective-permute-start.7 = (bf16[64,4096]{1,0:T(8,128)(2,1)S(1)}, bf16[64,4096]{1,0:T(8,128)(2,1)S(1)}, u32[]{:S(2)}, u32[]{:S(2)}) collective-permute-start(bf16[64,4096]{1,0:T(8,128)(2,1)S(1)} %collective-permute-done.5), channel_id=1, source_target_pairs={{0,1},{1,0},{2,3},{3,2},{4,5},{5,4},{6,7},{7,6},{8,9},{9,8},{10,11... | collective-permute-start | bytes 1572872 | tf_op jit(solution)/shard_map/xs3b/ppermute | solution.py:92
  57.7 4.2 %copy-start = (bf16[128,4096]{1,0:T(8,128)(2,1)S(1)}, bf16[128,4096]{1,0:T(8,128)(2,1)}, u32[]{:S(2)}) copy-start(bf16[128,4096]{1,0:T(8,128)(2,1)} %param.8) | copy-start | bytes 3145732
  57.8 20.0 %collective-permute-start.10 = (bf16[64,4096]{1,0:T(8,128)(2,1)S(1)}, bf16[64,4096]{1,0:T(8,128)(2,1)}, u32[]{:S(2)}, u32[]{:S(2)}) collective-permute-start(bf16[64,4096]{1,0:T(8,128)(2,1)S(1)} %collective-permute-done.2), channel_id=1, source_target_pairs={{0,4},{1,5},{2,0},{3,1},{4,8},{5,9},{6,2},{7,3},{8,12},{9,13},{10,... | collective-permute-start | bytes 1572872 | tf_op jit(solution)/shard_map/ag4a/ppermute | solution.py:92
  59.7 18.7 %collective-permute-start.14 = (bf16[64,4096]{1,0:T(8,128)(2,1)S(1)}, bf16[64,4096]{1,0:T(8,128)(2,1)}, u32[]{:S(2)}, u32[]{:S(2)}) collective-permute-start(bf16[64,4096]{1,0:T(8,128)(2,1)S(1)} %collective-permute-done.5), channel_id=1, source_target_pairs={{0,2},{1,3},{2,6},{3,7},{4,0},{5,1},{6,10},{7,11},{8,4},{9,5},{10,... | collective-permute-start | bytes 1572872 | tf_op jit(solution)/shard_map/ag4b/ppermute | solution.py:92
  60.3 23.1 %collective-permute-start.37 = (bf16[64,4096]{1,0:T(8,128)(2,1)S(1)}, bf16[64,4096]{1,0:T(8,128)(2,1)S(1)}, u32[]{:S(2)}, u32[]{:S(2)}) collective-permute-start(bf16[64,4096]{1,0:T(8,128)(2,1)S(1)} %get-tuple-element.27), channel_id=1, source_target_pairs={{0,4},{1,5},{2,0},{3,1},{4,8},{5,9},{6,2},{7,3},{8,12},{9,13},{10,... | collective-permute-start | bytes 1572872 | tf_op jit(solution)/shard_map/rs2a/ppermute | solution.py:92
  61.9 10.3 %slice-start.5 = ((s8[6291456]{0:T(1024)(128)(4,1)}), s8[2097152]{0:T(1024)(128)(4,1)S(1)}, s32[]{:S(2)}) async-start(s8[6291456]{0:T(1024)(128)(4,1)} %bitcast.83), calls=%async_computation.6 | async-start | bytes 4194304
  62.0 23.0 %collective-permute-start.44 = (bf16[64,4096]{1,0:T(8,128)(2,1)S(1)}, bf16[64,4096]{1,0:T(8,128)(2,1)S(1)}, u32[]{:S(2)}, u32[]{:S(2)}) collective-permute-start(bf16[64,4096]{1,0:T(8,128)(2,1)S(1)} %get-tuple-element.28), channel_id=1, source_target_pairs={{0,2},{1,3},{2,6},{3,7},{4,0},{5,1},{6,10},{7,11},{8,4},{9,5},{10,... | collective-permute-start | bytes 1572872 | tf_op jit(solution)/shard_map/rs2b/ppermute | solution.py:92
  62.8 9.4 %slice-start.6 = ((s8[6291456]{0:T(1024)(128)(4,1)}), s8[4194304]{0:T(1024)(128)(4,1)S(1)}, s32[]{:S(2)}) async-start(s8[6291456]{0:T(1024)(128)(4,1)} %bitcast.83), calls=%async_computation.7 | async-start | bytes 8388608
  77.5 20.0 %collective-permute-start.30 = (bf16[128,4096]{1,0:T(8,128)(2,1)S(1)}, bf16[128,4096]{1,0:T(8,128)(2,1)S(1)}, u32[]{:S(2)}, u32[]{:S(2)}) collective-permute-start(bf16[128,4096]{1,0:T(8,128)(2,1)S(1)} %slice.424), channel_id=1, source_target_pairs={{0,1},{1,0},{2,3},{3,2},{4,5},{5,4},{6,7},{7,6},{8,9},{9,8},{10,11... | collective-permute-start | bytes 3145736 | tf_op jit(solution)/shard_map/ps3/ppermute | solution.py:92
  77.8 115.5 %collective-permute-start.9 = (bf16[128,4096]{1,0:T(8,128)(2,1)S(1)}, bf16[128,4096]{1,0:T(8,128)(2,1)S(1)}, u32[]{:S(2)}, u32[]{:S(2)}) collective-permute-start(bf16[128,4096]{1,0:T(8,128)(2,1)S(1)} %slice.429), channel_id=1, source_target_pairs={{0,1},{1,0},{2,3},{3,2},{4,5},{5,4},{6,7},{7,6},{8,9},{9,8},{10,11... | collective-permute-start | bytes 3145736 | tf_op jit(solution)/shard_map/ps0/ppermute | solution.py:92
  78.3 6.9 %collective-permute-start.27 = (bf16[64,4096]{1,0:T(8,128)(2,1)}, bf16[64,4096]{1,0:T(8,128)(2,1)S(1)}, u32[]{:S(2)}, u32[]{:S(2)}) collective-permute-start(bf16[64,4096]{1,0:T(8,128)(2,1)} %collective-permute-done.10), channel_id=1, source_target_pairs={{0,1},{1,0},{2,3},{3,2},{4,5},{5,4},{6,7},{7,6},{8,9},{9,8},{10,11... | collective-permute-start | bytes 1572872 | tf_op jit(solution)/shard_map/xs4a/ppermute | solution.py:92
  83.4 15.0 %collective-permute-start.11 = (bf16[64,4096]{1,0:T(8,128)(2,1)}, bf16[64,4096]{1,0:T(8,128)(2,1)S(1)}, u32[]{:S(2)}, u32[]{:S(2)}) collective-permute-start(bf16[64,4096]{1,0:T(8,128)(2,1)} %collective-permute-done.10), channel_id=1, source_target_pairs={{0,4},{1,5},{2,0},{3,1},{4,8},{5,9},{6,2},{7,3},{8,12},{9,13},{10,... | collective-permute-start | bytes 1572872 | tf_op jit(solution)/shard_map/ag5a/ppermute | solution.py:92
  85.0 2.1 %collective-permute-start.28 = (bf16[64,4096]{1,0:T(8,128)(2,1)}, bf16[64,4096]{1,0:T(8,128)(2,1)S(1)}, u32[]{:S(2)}, u32[]{:S(2)}) collective-permute-start(bf16[64,4096]{1,0:T(8,128)(2,1)} %collective-permute-done.14), channel_id=1, source_target_pairs={{0,1},{1,0},{2,3},{3,2},{4,5},{5,4},{6,7},{7,6},{8,9},{9,8},{10,11... | collective-permute-start | bytes 1572872 | tf_op jit(solution)/shard_map/xs4b/ppermute | solution.py:92
  85.3 14.6 %collective-permute-start.15 = (bf16[64,4096]{1,0:T(8,128)(2,1)}, bf16[64,4096]{1,0:T(8,128)(2,1)S(1)}, u32[]{:S(2)}, u32[]{:S(2)}) collective-permute-start(bf16[64,4096]{1,0:T(8,128)(2,1)} %collective-permute-done.14), channel_id=1, source_target_pairs={{0,2},{1,3},{2,6},{3,7},{4,0},{5,1},{6,10},{7,11},{8,4},{9,5},{10,... | collective-permute-start | bytes 1572872 | tf_op jit(solution)/shard_map/ag5b/ppermute | solution.py:92
  87.1 21.2 %collective-permute-start.38 = (bf16[64,4096]{1,0:T(8,128)(2,1)S(1)}, bf16[64,4096]{1,0:T(8,128)(2,1)S(1)}, u32[]{:S(2)}, u32[]{:S(2)}) collective-permute-start(bf16[64,4096]{1,0:T(8,128)(2,1)S(1)} %get-tuple-element.25), channel_id=1, source_target_pairs={{0,4},{1,5},{2,0},{3,1},{4,8},{5,9},{6,2},{7,3},{8,12},{9,13},{10,... | collective-permute-start | bytes 1572872 | tf_op jit(solution)/shard_map/rs3a/ppermute | solution.py:92
  97.5 13.7 %collective-permute-start.45 = (bf16[64,4096]{1,0:T(8,128)(2,1)S(1)}, bf16[64,4096]{1,0:T(8,128)(2,1)S(1)}, u32[]{:S(2)}, u32[]{:S(2)}) collective-permute-start(bf16[64,4096]{1,0:T(8,128)(2,1)S(1)} %get-tuple-element.26), channel_id=1, source_target_pairs={{0,2},{1,3},{2,6},{3,7},{4,0},{5,1},{6,10},{7,11},{8,4},{9,5},{10,... | collective-permute-start | bytes 1572872 | tf_op jit(solution)/shard_map/rs3b/ppermute | solution.py:92
  98.4 24.6 %collective-permute-start.29 = (bf16[128,4096]{1,0:T(8,128)(2,1)S(1)}, bf16[128,4096]{1,0:T(8,128)(2,1)S(1)}, u32[]{:S(2)}, u32[]{:S(2)}) collective-permute-start(bf16[128,4096]{1,0:T(8,128)(2,1)S(1)} %slice.425), channel_id=1, source_target_pairs={{0,1},{1,0},{2,3},{3,2},{4,5},{5,4},{6,7},{7,6},{8,9},{9,8},{10,11... | collective-permute-start | bytes 3145736 | tf_op jit(solution)/shard_map/ps4/ppermute | solution.py:92
  99.9 11.6 %collective-permute-start.24 = (bf16[64,4096]{1,0:T(8,128)(2,1)S(1)}, bf16[64,4096]{1,0:T(8,128)(2,1)S(1)}, u32[]{:S(2)}, u32[]{:S(2)}) collective-permute-start(bf16[64,4096]{1,0:T(8,128)(2,1)S(1)} %collective-permute-done.11), channel_id=1, source_target_pairs={{0,1},{1,0},{2,3},{3,2},{4,5},{5,4},{6,7},{7,6},{8,9},{9,8},{10,11... | collective-permute-start | bytes 1572872 | tf_op jit(solution)/shard_map/xs5a/ppermute | solution.py:92
  108.4 15.6 %collective-permute-start.12 = (bf16[64,4096]{1,0:T(8,128)(2,1)S(1)}, bf16[64,4096]{1,0:T(8,128)(2,1)S(1)}, u32[]{:S(2)}, u32[]{:S(2)}) collective-permute-start(bf16[64,4096]{1,0:T(8,128)(2,1)S(1)} %collective-permute-done.11), channel_id=1, source_target_pairs={{0,4},{1,5},{2,0},{3,1},{4,8},{5,9},{6,2},{7,3},{8,12},{9,13},{10,... | collective-permute-start | bytes 1572872 | tf_op jit(solution)/shard_map/ag6a/ppermute | solution.py:92
  111.2 1.9 collective-permute-start.25
  111.5 14.6 %collective-permute-start.16 = (bf16[64,4096]{1,0:T(8,128)(2,1)S(1)}, bf16[64,4096]{1,0:T(8,128)(2,1)S(1)}, u32[]{:S(2)}, u32[]{:S(2)}) collective-permute-start(bf16[64,4096]{1,0:T(8,128)(2,1)S(1)} %collective-permute-done.15), channel_id=1, source_target_pairs={{0,2},{1,3},{2,6},{3,7},{4,0},{5,1},{6,10},{7,11},{8,4},{9,5},{10,... | collective-permute-start | bytes 1572872 | tf_op jit(solution)/shard_map/ag6b/ppermute | solution.py:92
  113.1 19.2 %collective-permute-start.39 = (bf16[64,4096]{1,0:T(8,128)(2,1)S(1)}, bf16[64,4096]{1,0:T(8,128)(2,1)S(1)}, u32[]{:S(2)}, u32[]{:S(2)}) collective-permute-start(bf16[64,4096]{1,0:T(8,128)(2,1)S(1)} %get-tuple-element.23), channel_id=1, source_target_pairs={{0,4},{1,5},{2,0},{3,1},{4,8},{5,9},{6,2},{7,3},{8,12},{9,13},{10,... | collective-permute-start | bytes 1572872 | tf_op jit(solution)/shard_map/rs4a/ppermute | solution.py:92
  123.1 14.0 %collective-permute-start.46 = (bf16[64,4096]{1,0:T(8,128)(2,1)S(1)}, bf16[64,4096]{1,0:T(8,128)(2,1)S(1)}, u32[]{:S(2)}, u32[]{:S(2)}) collective-permute-start(bf16[64,4096]{1,0:T(8,128)(2,1)S(1)} %get-tuple-element.24), channel_id=1, source_target_pairs={{0,2},{1,3},{2,6},{3,7},{4,0},{5,1},{6,10},{7,11},{8,4},{9,5},{10,... | collective-permute-start | bytes 1572872 | tf_op jit(solution)/shard_map/rs4b/ppermute | solution.py:92
  123.9 25.0 %collective-permute-start.26 = (bf16[128,4096]{1,0:T(8,128)(2,1)S(1)}, bf16[128,4096]{1,0:T(8,128)(2,1)S(1)}, u32[]{:S(2)}, u32[]{:S(2)}) collective-permute-start(bf16[128,4096]{1,0:T(8,128)(2,1)S(1)} %slice.426), channel_id=1, source_target_pairs={{0,1},{1,0},{2,3},{3,2},{4,5},{5,4},{6,7},{7,6},{8,9},{9,8},{10,11... | collective-permute-start | bytes 3145736 | tf_op jit(solution)/shard_map/ps5/ppermute | solution.py:92
  126.1 11.3 %collective-permute-start.21 = (bf16[64,4096]{1,0:T(8,128)(2,1)S(1)}, bf16[64,4096]{1,0:T(8,128)(2,1)S(1)}, u32[]{:S(2)}, u32[]{:S(2)}) collective-permute-start(bf16[64,4096]{1,0:T(8,128)(2,1)S(1)} %collective-permute-done.12), channel_id=1, source_target_pairs={{0,1},{1,0},{2,3},{3,2},{4,5},{5,4},{6,7},{7,6},{8,9},{9,8},{10,11... | collective-permute-start | bytes 1572872 | tf_op jit(solution)/shard_map/xs6a/ppermute | solution.py:92
  132.3 17.6 %collective-permute-start.13 = (bf16[64,4096]{1,0:T(8,128)(2,1)S(1)}, bf16[64,4096]{1,0:T(8,128)(2,1)S(1)}, u32[]{:S(2)}, u32[]{:S(2)}) collective-permute-start(bf16[64,4096]{1,0:T(8,128)(2,1)S(1)} %collective-permute-done.12), channel_id=1, source_target_pairs={{0,4},{1,5},{2,0},{3,1},{4,8},{5,9},{6,2},{7,3},{8,12},{9,13},{10,... | collective-permute-start | bytes 1572872 | tf_op jit(solution)/shard_map/ag7a/ppermute | solution.py:92
  137.1 1.9 collective-permute-start.22
  137.3 14.6 %collective-permute-start.17 = (bf16[64,4096]{1,0:T(8,128)(2,1)S(1)}, bf16[64,4096]{1,0:T(8,128)(2,1)S(1)}, u32[]{:S(2)}, u32[]{:S(2)}) collective-permute-start(bf16[64,4096]{1,0:T(8,128)(2,1)S(1)} %collective-permute-done.16), channel_id=1, source_target_pairs={{0,2},{1,3},{2,6},{3,7},{4,0},{5,1},{6,10},{7,11},{8,4},{9,5},{10,... | collective-permute-start | bytes 1572872 | tf_op jit(solution)/shard_map/ag7b/ppermute | solution.py:92
  139.0 16.3 %collective-permute-start.40 = (bf16[64,4096]{1,0:T(8,128)(2,1)S(1)}, bf16[64,4096]{1,0:T(8,128)(2,1)S(1)}, u32[]{:S(2)}, u32[]{:S(2)}) collective-permute-start(bf16[64,4096]{1,0:T(8,128)(2,1)S(1)} %get-tuple-element.21), channel_id=1, source_target_pairs={{0,4},{1,5},{2,0},{3,1},{4,8},{5,9},{6,2},{7,3},{8,12},{9,13},{10,... | collective-permute-start | bytes 1572872 | tf_op jit(solution)/shard_map/rs5a/ppermute | solution.py:92
  148.9 14.0 %collective-permute-start.47 = (bf16[64,4096]{1,0:T(8,128)(2,1)S(1)}, bf16[64,4096]{1,0:T(8,128)(2,1)S(1)}, u32[]{:S(2)}, u32[]{:S(2)}) collective-permute-start(bf16[64,4096]{1,0:T(8,128)(2,1)S(1)} %get-tuple-element.22), channel_id=1, source_target_pairs={{0,2},{1,3},{2,6},{3,7},{4,0},{5,1},{6,10},{7,11},{8,4},{9,5},{10,... | collective-permute-start | bytes 1572872 | tf_op jit(solution)/shard_map/rs5b/ppermute | solution.py:92
  149.8 24.1 %collective-permute-start.23 = (bf16[128,4096]{1,0:T(8,128)(2,1)S(1)}, bf16[128,4096]{1,0:T(8,128)(2,1)S(1)}, u32[]{:S(2)}, u32[]{:S(2)}) collective-permute-start(bf16[128,4096]{1,0:T(8,128)(2,1)S(1)} %slice.427), channel_id=1, source_target_pairs={{0,1},{1,0},{2,3},{3,2},{4,5},{5,4},{6,7},{7,6},{8,9},{9,8},{10,11... | collective-permute-start | bytes 3145736 | tf_op jit(solution)/shard_map/ps6/ppermute | solution.py:92
  151.9 12.7 %collective-permute-start.18 = (bf16[64,4096]{1,0:T(8,128)(2,1)S(1)}, bf16[64,4096]{1,0:T(8,128)(2,1)S(1)}, u32[]{:S(2)}, u32[]{:S(2)}) collective-permute-start(bf16[64,4096]{1,0:T(8,128)(2,1)S(1)} %collective-permute-done.13), channel_id=1, source_target_pairs={{0,1},{1,0},{2,3},{3,2},{4,5},{5,4},{6,7},{7,6},{8,9},{9,8},{10,11... | collective-permute-start | bytes 1572872 | tf_op jit(solution)/shard_map/xs7a/ppermute | solution.py:92
  155.3 10.0 %collective-permute-start.19 = (bf16[64,4096]{1,0:T(8,128)(2,1)S(1)}, bf16[64,4096]{1,0:T(8,128)(2,1)S(1)}, u32[]{:S(2)}, u32[]{:S(2)}) collective-permute-start(bf16[64,4096]{1,0:T(8,128)(2,1)S(1)} %collective-permute-done.17), channel_id=1, source_target_pairs={{0,1},{1,0},{2,3},{3,2},{4,5},{5,4},{6,7},{7,6},{8,9},{9,8},{10,11... | collective-permute-start | bytes 1572872 | tf_op jit(solution)/shard_map/xs7b/ppermute | solution.py:92
  163.2 13.2 %collective-permute-start.41 = (bf16[64,4096]{1,0:T(8,128)(2,1)S(1)}, bf16[64,4096]{1,0:T(8,128)(2,1)S(1)}, u32[]{:S(2)}, u32[]{:S(2)}) collective-permute-start(bf16[64,4096]{1,0:T(8,128)(2,1)S(1)} %get-tuple-element.19), channel_id=1, source_target_pairs={{0,4},{1,5},{2,0},{3,1},{4,8},{5,9},{6,2},{7,3},{8,12},{9,13},{10,... | collective-permute-start | bytes 1572872 | tf_op jit(solution)/shard_map/rs6a/ppermute | solution.py:92
  164.7 13.3 %collective-permute-start.48 = (bf16[64,4096]{1,0:T(8,128)(2,1)S(1)}, bf16[64,4096]{1,0:T(8,128)(2,1)S(1)}, u32[]{:S(2)}, u32[]{:S(2)}) collective-permute-start(bf16[64,4096]{1,0:T(8,128)(2,1)S(1)} %get-tuple-element.20), channel_id=1, source_target_pairs={{0,2},{1,3},{2,6},{3,7},{4,0},{5,1},{6,10},{7,11},{8,4},{9,5},{10,... | collective-permute-start | bytes 1572872 | tf_op jit(solution)/shard_map/rs6b/ppermute | solution.py:92
  173.8 6.4 %collective-permute-start.20 = (bf16[128,4096]{1,0:T(8,128)(2,1)S(1)}, bf16[128,4096]{1,0:T(8,128)(2,1)S(1)}, u32[]{:S(2)}, u32[]{:S(2)}) collective-permute-start(bf16[128,4096]{1,0:T(8,128)(2,1)S(1)} %slice.428), channel_id=1, source_target_pairs={{0,1},{1,0},{2,3},{3,2},{4,5},{5,4},{6,7},{7,6},{8,9},{9,8},{10,11... | collective-permute-start | bytes 3145736 | tf_op jit(solution)/shard_map/ps7/ppermute | solution.py:92
  178.2 12.4 %collective-permute-start.42 = (bf16[64,4096]{1,0:T(8,128)(2,1)S(1)}, bf16[64,4096]{1,0:T(8,128)(2,1)S(1)}, u32[]{:S(2)}, u32[]{:S(2)}) collective-permute-start(bf16[64,4096]{1,0:T(8,128)(2,1)S(1)} %get-tuple-element.17), channel_id=1, source_target_pairs={{0,4},{1,5},{2,0},{3,1},{4,8},{5,9},{6,2},{7,3},{8,12},{9,13},{10,... | collective-permute-start | bytes 1572872 | tf_op jit(solution)/shard_map/rs7a/ppermute | solution.py:92
  178.6 12.3 %collective-permute-start.49 = (bf16[64,4096]{1,0:T(8,128)(2,1)S(1)}, bf16[64,4096]{1,0:T(8,128)(2,1)S(1)}, u32[]{:S(2)}, u32[]{:S(2)}) collective-permute-start(bf16[64,4096]{1,0:T(8,128)(2,1)S(1)} %get-tuple-element.18), channel_id=1, source_target_pairs={{0,2},{1,3},{2,6},{3,7},{4,0},{5,1},{6,10},{7,11},{8,4},{9,5},{10,... | collective-permute-start | bytes 1572872 | tf_op jit(solution)/shard_map/rs7b/ppermute | solution.py:92
  191.2 11.4 %collective-permute-start.43 = (bf16[64,4096]{1,0:T(8,128)(2,1)S(1)}, bf16[64,4096]{1,0:T(8,128)(2,1)S(1)}, u32[]{:S(2)}, u32[]{:S(2)}) collective-permute-start(bf16[64,4096]{1,0:T(8,128)(2,1)S(1)} %get-tuple-element.15), channel_id=1, source_target_pairs={{0,4},{1,5},{2,0},{3,1},{4,8},{5,9},{6,2},{7,3},{8,12},{9,13},{10,... | collective-permute-start | bytes 1572872 | tf_op jit(solution)/shard_map/rs0a/ppermute | solution.py:92
  192.2 10.9 %collective-permute-start.50 = (bf16[64,4096]{1,0:T(8,128)(2,1)S(1)}, bf16[64,4096]{1,0:T(8,128)(2,1)S(1)}, u32[]{:S(2)}, u32[]{:S(2)}) collective-permute-start(bf16[64,4096]{1,0:T(8,128)(2,1)S(1)} %get-tuple-element.16), channel_id=1, source_target_pairs={{0,2},{1,3},{2,6},{3,7},{4,0},{5,1},{6,10},{7,11},{8,4},{9,5},{10,... | collective-permute-start | bytes 1572872 | tf_op jit(solution)/shard_map/rs0b/ppermute | solution.py:92
